TPU v7x, 128 devices: a whole 4x4x4 slice. The times are simulated.
128 devices in a mesh: group: 16 (over y_hi, x, core), mp: 8 (over z, y_lo).
Axes of the slice: x: 4, y: 4 (y_hi: 2, y_lo: 2; y = y_hi * 2 + y_lo), z: 4, core: 2. Of those that a mesh axis runs over, the one named last changes fastest.
Arguments:
- hidden_in: bfloat16 [8192, 1024], P('group'), may hold values from -8 to 8
- request_ids: int32 [8192], P('group'), may hold values from 63 to 8191, as said below
- w_qkv: float32 [1024, 3072], P(('group', 'mp')), may hold values from -1 to 1
- w_out: float32 [1024, 1024], P(('group', 'mp')), may hold values from -0.1875 to 0.1875
- w_up: float32 [1024, 4096], P(('group', 'mp')), may hold values from -0.1875 to 0.1875
- w_down: float32 [1024, 4096], P(('group', 'mp')), may hold values from -0.09375 to 0.09375
- ln1_gain: float32 [1024], replicated, may hold values from 0.25 to 1.75
- ln1_shift: float32 [1024], replicated, may hold values from -3 to 3
- ln2_gain: float32 [1024], replicated, may hold values from 0.25 to 1.75
- ln2_shift: float32 [1024], replicated, may hold values from -3 to 3
Outputs:
- hidden_out: bfloat16 [8192, 1024], P(('group', 'mp'))
- keys_cache: bfloat16 [8192, 1024], P('group', 'mp')
- values_cache: bfloat16 [8192, 1024], P('group', 'mp')
Inputs may be any that keep to these rules, and one draw needn't show every extreme that they name: `request_ids`: each slot holds the index of the last slot of its request. In groups 2i and 2i+1 (of 512 slots each) one request of exactly 512 slots ends the first group and begins the second, at least 64 of its slots in each; every other request lies within one aligned block of 64 slots, one or two requests a block, and some blocks hold one request of exactly 64 slots.
All inputs are finite; a program needn't handle non-finite values.
Results may differ from a plain program's by a relative error of at most 0.011.
Values may be sent and summed in bfloat16 or wider, within the bound.
No kernel may reach another device: no remote copies, remote signals or barrier semaphores. Data moves between devices by JAX's collectives and lax.ppermute only.
A program may use at most 64 MiB of HBM per device.

v0:
```python
import jax
import jax.numpy as jnp
from jax import lax
from jax.sharding import PartitionSpec as P

HD = 64
SHORT = 64


def swapped(value, axis, distance):
    return lax.ppermute(value, axis, [(i, i ^ 1 << distance) for i in range(lax.axis_size(axis))])


def layer_norm(values_in, norm_gain, norm_shift):
    center = values_in - jnp.mean(values_in, axis=-1, keepdims=True)
    spread = jnp.mean(center * center, axis=-1, keepdims=True)
    return center * lax.rsqrt(spread + 1e-05) * norm_gain + norm_shift


def body(
    hidden_in, request_ids, w_qkv, w_out, w_up, w_down, ln1_gain, ln1_shift, ln2_gain, ln2_shift
):
    groups = lax.axis_size("group")
    shards = lax.axis_size("mp")
    model_width = hidden_in.shape[1]
    local_width = model_width // shards
    local_hidden = w_up.shape[1] // shards
    tok_rows = hidden_in.shape[0]
    part_rows = w_qkv.shape[0]
    pieces = (
        w_qkv.astype(jnp.bfloat16).reshape(part_rows, 3, shards, local_width),
        w_out.astype(jnp.bfloat16).reshape(part_rows, 1, shards, local_width),
        w_up.astype(jnp.bfloat16).reshape(part_rows, 1, shards, local_hidden),
        w_down.astype(jnp.bfloat16).reshape(part_rows, 1, shards, local_hidden),
    )
    gathered = (
        lax.all_gather(pieces[0], "group", axis=0, tiled=True),
        lax.all_gather(pieces[1], "group", axis=0, tiled=True),
        lax.all_gather(pieces[2], "group", axis=0, tiled=True),
        lax.all_gather(pieces[3], "group", axis=0, tiled=True),
    )
    exchanged = (
        lax.all_to_all(gathered[0], "mp", split_axis=2, concat_axis=0, tiled=True),
        lax.all_to_all(gathered[1], "mp", split_axis=2, concat_axis=0, tiled=True),
        lax.all_to_all(gathered[2], "mp", split_axis=2, concat_axis=0, tiled=True),
        lax.all_to_all(gathered[3], "mp", split_axis=2, concat_axis=0, tiled=True),
    )
    served = tuple(
        (
            jnp.transpose(
                weight_piece.reshape(shards, groups, part_rows, -1), (1, 0, 2, 3)
            ).reshape(model_width, -1)
            for weight_piece in exchanged
        )
    )
    qkv_local, out_local, up_local, down_local = served
    projected = jnp.dot(hidden_in, qkv_local, preferred_element_type=jnp.float32)
    queries = projected[:, :local_width].astype(jnp.bfloat16)
    key_rows = projected[:, local_width : 2 * local_width].astype(jnp.bfloat16)
    value_rows = projected[:, 2 * local_width :].astype(jnp.bfloat16)
    partner_keys, partner_values = swapped((key_rows, value_rows), "group", 0)
    group_index = lax.axis_index("group")
    parity = group_index % 2
    long_id = jnp.where(parity == 0, request_ids[-1], request_ids[0])
    own_long = request_ids == long_id
    local_heads = local_width // HD
    score_scale = HD ** (-0.5)
    block_total = tok_rows // SHORT
    short_q = queries.reshape(block_total, SHORT, local_heads, HD)
    short_k = key_rows.reshape(block_total, SHORT, local_heads, HD)
    short_v = value_rows.reshape(block_total, SHORT, local_heads, HD)
    short_ids = request_ids.reshape(block_total, SHORT)
    short_scores = (
        jnp.einsum("bqhd,bkhd->bhqk", short_q, short_k, preferred_element_type=jnp.float32)
        * score_scale
    )
    short_mask = short_ids[:, :, None] == short_ids[:, None, :]
    short_scores = jnp.where(short_mask[:, None], short_scores, -1e30)
    short_peak = jnp.max(short_scores, axis=-1, keepdims=True)
    short_weights = jnp.exp(short_scores - short_peak).astype(jnp.bfloat16)
    short_totals = jnp.sum(short_weights.astype(jnp.float32), axis=-1)
    short_mixed = jnp.einsum(
        "bhqk,bkhd->bqhd", short_weights, short_v, preferred_element_type=jnp.float32
    )
    short_out = (
        (short_mixed / jnp.transpose(short_totals, (0, 2, 1))[:, :, :, None])
        .astype(jnp.bfloat16)
        .reshape(tok_rows, local_width)
    )
    first_keys = jnp.where(parity == 0, key_rows, partner_keys)
    second_keys = jnp.where(parity == 0, partner_keys, key_rows)
    first_values = jnp.where(parity == 0, value_rows, partner_values)
    second_values = jnp.where(parity == 0, partner_values, value_rows)
    pair_base = (group_index - parity) * tok_rows
    span_start = long_id - tok_rows + 1 - pair_base
    long_keys = lax.dynamic_slice_in_dim(
        jnp.concatenate([first_keys, second_keys], 0), span_start, tok_rows, 0
    ).reshape(tok_rows, local_heads, HD)
    long_values = lax.dynamic_slice_in_dim(
        jnp.concatenate([first_values, second_values], 0), span_start, tok_rows, 0
    ).reshape(tok_rows, local_heads, HD)
    query_rows = min(512, tok_rows)
    query_blocks = tok_rows // query_rows

    def long_attend(block_queries):
        heads_view = block_queries.reshape(query_rows, local_heads, HD)
        scores = (
            jnp.einsum("qhd,khd->hqk", heads_view, long_keys, preferred_element_type=jnp.float32)
            * score_scale
        )
        row_peak = jnp.max(scores, axis=-1, keepdims=True)
        weights = jnp.exp(scores - row_peak).astype(jnp.bfloat16)
        totals = jnp.sum(weights.astype(jnp.float32), axis=-1)
        mixed_heads = jnp.einsum(
            "hqk,khd->qhd", weights, long_values, preferred_element_type=jnp.float32
        )
        return (
            (mixed_heads / jnp.transpose(totals)[:, :, None])
            .astype(jnp.bfloat16)
            .reshape(query_rows, local_width)
        )

    def skipped(block_queries):
        return jnp.zeros((query_rows, local_width), jnp.bfloat16)

    def long_block(query_block):
        block_queries, block_long = query_block
        return lax.cond(jnp.any(block_long), long_attend, skipped, block_queries)

    long_out = lax.map(
        long_block,
        (
            queries.reshape(query_blocks, query_rows, local_width),
            own_long.reshape(query_blocks, query_rows),
        ),
    ).reshape(tok_rows, local_width)
    attended = jnp.where(own_long[:, None], long_out, short_out)
    share_rows = tok_rows // shards
    row_start = lax.axis_index("mp") * share_rows

    def combine(term_fn, residual, norm_gain, norm_shift):
        summed = lax.psum(term_fn(0, tok_rows), "mp")
        whole_rows = layer_norm(
            residual.astype(jnp.float32) + summed, norm_gain, norm_shift
        ).astype(jnp.bfloat16)
        normed = lax.dynamic_slice_in_dim(whole_rows, row_start, share_rows, 0)
        return (normed, whole_rows)

    def attn_term(row_begin, row_count):
        return lax.dot_general(
            attended, out_local, (((1,), (1,)), ((), ())), preferred_element_type=jnp.float32
        )

    attn_share, attn_normed = combine(attn_term, hidden_in, ln1_gain, ln1_shift)
    activated = jax.nn.gelu(
        jnp.dot(attn_normed, up_local, preferred_element_type=jnp.float32), approximate=False
    ).astype(jnp.bfloat16)

    def feed_term(row_begin, row_count):
        return lax.dot_general(
            activated, down_local, (((1,), (1,)), ((), ())), preferred_element_type=jnp.float32
        )

    final_share, unused = combine(feed_term, attn_normed, ln2_gain, ln2_shift)
    return (final_share, key_rows, value_rows)


def solution(mesh):
    in_specs = (
        P("group", None),
        P("group"),
        P(("group", "mp"), None),
        P(("group", "mp"), None),
        P(("group", "mp"), None),
        P(("group", "mp"), None),
        P(),
        P(),
        P(),
        P(),
    )
    out_specs = (P(("group", "mp"), None), P("group", "mp"), P("group", "mp"))
    return jax.shard_map(body, mesh=mesh, in_specs=in_specs, out_specs=out_specs, check_vma=False)
```

profile of v0, /device:TPU:1, one launch (start us, length us, event | category | flops | bytes accessed | tf_op | source)
XLA Modules:
  0.0 345.1 jit_solution(3405241490203082044)
XLA Ops:
  8.0 1.5 convert_element_type.73
  9.6 0.8 convert_bitcast_fusion.1
  10.4 27.8 %all_gather.13 = bf16[128,1,8,128]{3,0,1,2:T(8,128)(2,1)} all-gather(bf16[8,1,8,128]{3,0,1,2:T(8,128)(2,1)S(1)} %convert_bitcast_fusion.1), channel_id=1, replica_groups=mesh['group'=16,'mp'=8] {'group'}, dimensions={0}, use_global_device_ids=true | all-gather | bytes 278528 | tf_op jit(solution)/shard_map/all_gather | solution.py:38
  38.1 5.1 %all-to-all-start.1 = ((bf16[128,1,8,128]{3,0,1,2:T(8,128)(2,1)}), bf16[128,1,8,128]{3,0,1,2:T(8,128)(2,1)S(1)}, u32[]{:S(2)}, u32[]{:S(2)}) async-start(bf16[128,1,8,128]{3,0,1,2:T(8,128)(2,1)} %all_gather.13), calls=%async_computation.1 | async-start | bytes 524288 | tf_op jit(solution)/shard_map/all_to_all | solution.py:44
  43.3 0.9 convert_bitcast_fusion
  44.2 22.1 %all_gather.12 = bf16[128,3,8,128]{3,2,1,0:T(8,128)(2,1)S(1)} all-gather(bf16[8,3,8,128]{3,2,1,0:T(8,128)(2,1)S(1)} %bitcast.100), channel_id=1, replica_groups=mesh['group'=16,'mp'=8] {'group'}, dimensions={0}, use_global_device_ids=true | all-gather | bytes 835584 | tf_op jit(solution)/shard_map/all_gather | solution.py:37
  66.3 1.1 copy.76
  67.4 5.8 %all-to-all-start = ((bf16[128,3,8,128]{3,0,1,2:T(8,128)(2,1)}), bf16[128,3,8,128]{3,0,1,2:T(8,128)(2,1)S(1)}, u32[]{:S(2)}, u32[]{:S(2)}) async-start(bf16[128,3,8,128]{3,0,1,2:T(8,128)(2,1)} %copy.76), calls=%async_computation | async-start | bytes 1572864 | tf_op jit(solution)/shard_map/all_to_all | solution.py:43
  73.2 0.6 convert_element_type.75
  75.9 0.6 fusion.96
  77.4 8.3 %all-to-all-done = bf16[128,3,8,128]{3,0,1,2:T(8,128)(2,1)S(1)} async-done(((bf16[128,3,8,128]{3,0,1,2:T(8,128)(2,1)}), bf16[128,3,8,128]{3,0,1,2:T(8,128)(2,1)S(1)}, u32[]{:S(2)}, u32[]{:S(2)}) %all-to-all-start) | async-done | bytes 786464 | tf_op jit(solution)/shard_map/all_to_all | solution.py:43
  85.8 0.7 copy.77
  86.5 0.7 reshape.140
  87.7 0.7 convolution_convert_fusion
  88.5 1.4 collective-permute-start
  90.8 0.6 copy-done.12
  91.4 1.5 fusion.10
  93.5 2.0 conditional.1
  95.5 1.8 fusion.61
  97.3 3.6 %all-to-all-start.2 = ((bf16[128,1,8,512]{3,0,1,2:T(8,128)(2,1)}), bf16[128,1,8,512]{3,0,1,2:T(8,128)(2,1)S(1)}, u32[]{:S(2)}, u32[]{:S(2)}) async-start(bf16[128,1,8,512]{3,0,1,2:T(8,128)(2,1)} %all-gather.3.cloned.1.call-done), calls=%async_computation.2 | async-start | bytes 2097152 | tf_op jit(solution)/shard_map/all_to_all | solution.py:45
  100.9 30.2 %all-gather.5.cloned.1.call-done = bf16[128,1,8,512]{3,0,1,2:T(8,128)(2,1)} async-done(((bf16[8,1,8,512]{3,0,1,2:T(8,128)(2,1)}), bf16[128,1,8,512]{3,0,1,2:T(8,128)(2,1)}) %all-gather.5.cloned.1.call-update) | async-done | bytes 1048592 | tf_op jit(solution)/shard_map/all_gather | solution.py:40
  131.1 4.2 %all-to-all-start.3 = ((bf16[128,1,8,512]{3,0,1,2:T(8,128)(2,1)}), bf16[128,1,8,512]{3,0,1,2:T(8,128)(2,1)S(1)}, u32[]{:S(2)}, u32[]{:S(2)}) async-start(bf16[128,1,8,512]{3,0,1,2:T(8,128)(2,1)} %all-gather.5.cloned.1.call-done), calls=%async_computation.3 | async-start | bytes 2097152 | tf_op jit(solution)/shard_map/all_to_all | solution.py:46
  135.5 1.1 copy.88
  136.6 26.0 %all-to-all-done.3 = bf16[128,1,8,512]{3,0,1,2:T(8,128)(2,1)S(1)} async-done(((bf16[128,1,8,512]{3,0,1,2:T(8,128)(2,1)}), bf16[128,1,8,512]{3,0,1,2:T(8,128)(2,1)S(1)}, u32[]{:S(2)}, u32[]{:S(2)}) %all-to-all-start.3) | async-done | bytes 1048608 | tf_op jit(solution)/shard_map/all_to_all | solution.py:46
  162.6 1.1 copy.89
  163.7 56.5 %all-reduce.3.cloned.1.call-done = f32[512,1024]{1,0:T(8,128)} async-done(((f32[512,1024]{1,0:T(8,128)}), f32[512,1024]{1,0:T(8,128)}) %all-reduce.3.cloned.1.call-update) | async-done | bytes 2097168 | tf_op jit(solution)/shard_map/psum | solution.py:142
  220.2 2.0 fusion.21
  223.5 0.7 copy-done.5
  224.2 5.9 %fusion.22 = f32[512,1024]{1,0:T(8,128)} fusion(bf16[1024,512]{1,0:T(8,128)(2,1)} %bitcast.91, bf16[512,1024]{1,0:T(8,128)(2,1)S(1)} %add_convert_fusion, bf16[1024,512]{1,0:T(8,128)(2,1)S(1)} %bitcast.90), kind=kOutput, calls=%fused_computation.44 | convolution fusion | flops 1090781184 | bytes 5242880 | tf_op jit(solution)/shard_map/dot_general | solution.py:160
  230.2 103.9 %all-reduce.5.cloned.1.call-done = f32[512,1024]{1,0:T(8,128)} async-done(((f32[512,1024]{1,0:T(8,128)}), f32[512,1024]{1,0:T(8,128)}) %all-reduce.5.cloned.1.call-update) | async-done | bytes 2097168 | tf_op jit(solution)/shard_map/psum | solution.py:142
  334.0 2.0 fusion.7
  337.0 0.8 fusion.56
  (70 shorter events, 7.4 us)
Async XLA Ops:
  8.0 89.3 %all-gather.3.cloned.1.call-start = ((), (), s32[]{:S(2)}) async-start(), calls=%async_computation.5 | async-start | bytes 1114112 | tf_op jit(solution)/shard_map/all_gather | solution.py:39
  38.1 29.3 %all-to-all-start.1 = ((bf16[128,1,8,128]{3,0,1,2:T(8,128)(2,1)}), bf16[128,1,8,128]{3,0,1,2:T(8,128)(2,1)S(1)}, u32[]{:S(2)}, u32[]{:S(2)}) async-start(bf16[128,1,8,128]{3,0,1,2:T(8,128)(2,1)} %all_gather.13), calls=%async_computation.1 | async-start | bytes 524288 | tf_op jit(solution)/shard_map/all_to_all | solution.py:44
  43.3 29.9 %copy-start.6 = (f32[8,4096]{1,0:T(8,128)S(1)}, f32[8,4096]{1,0:T(8,128)}, u32[]{:S(2)}) copy-start(f32[8,4096]{1,0:T(8,128)} %param.17) | copy-start | bytes 393220
  44.2 29.8 %copy-start.7 = (s32[512]{0:T(512)S(1)}, s32[512]{0:T(512)}, u32[]{:S(2)}) copy-start(s32[512]{0:T(512)} %param.13) | copy-start | bytes 6148
  67.4 18.4 %all-to-all-start = ((bf16[128,3,8,128]{3,0,1,2:T(8,128)(2,1)}), bf16[128,3,8,128]{3,0,1,2:T(8,128)(2,1)S(1)}, u32[]{:S(2)}, u32[]{:S(2)}) async-start(bf16[128,3,8,128]{3,0,1,2:T(8,128)(2,1)} %copy.76), calls=%async_computation | async-start | bytes 1572864 | tf_op jit(solution)/shard_map/all_to_all | solution.py:43
  73.2 57.9 %all-gather.5.cloned.1.call-start = ((), (), s32[]{:S(2)}) async-start(), calls=%async_computation.6 | async-start | bytes 1114112 | tf_op jit(solution)/shard_map/all_gather | solution.py:40
  73.9 146.3 %all-reduce.3.cloned.1.call-start = ((), (), s32[]{:S(2)}) async-start(), calls=%async_computation.4 | async-start | bytes 4194304 | tf_op jit(solution)/shard_map/psum | solution.py:142
  86.4 1.2 copy-start.1
  88.5 4.9 %copy-start.3 = (bf16[512,128]{1,0:T(8,128)(2,1)}, bf16[512,128]{1,0:T(8,128)(2,1)S(1)}, u32[]{:S(2)}) copy-start(bf16[512,128]{1,0:T(8,128)(2,1)S(1)} %get-tuple-element.157) | copy-start | bytes 393220
  88.5 4.9 %copy-start.4 = (bf16[512,128]{1,0:T(8,128)(2,1)}, bf16[512,128]{1,0:T(8,128)(2,1)S(1)}, u32[]{:S(2)}) copy-start(bf16[512,128]{1,0:T(8,128)(2,1)S(1)} %get-tuple-element.159) | copy-start | bytes 393220
  88.5 4.9 %collective-permute-start = (bf16[512,128]{1,0:T(8,128)(2,1)S(1)}, bf16[512,128]{1,0:T(8,128)(2,1)S(1)}, u32[]{:S(2)}, u32[]{:S(2)}) collective-permute-start(bf16[512,128]{1,0:T(8,128)(2,1)S(1)} %get-tuple-element.159), channel_id=1, source_target_pairs={{0,8},{8,0},{16,24},{24,16},{32,40},{40,32},{48,56},{56,48},{64,72... | collective-permute-start | bytes 393224 | tf_op jit(solution)/shard_map/ppermute | solution.py:11
  90.0 3.3 collective-permute-start.1
  90.6 0.8 copy-start.12
  97.3 33.8 %all-to-all-start.2 = ((bf16[128,1,8,512]{3,0,1,2:T(8,128)(2,1)}), bf16[128,1,8,512]{3,0,1,2:T(8,128)(2,1)S(1)}, u32[]{:S(2)}, u32[]{:S(2)}) async-start(bf16[128,1,8,512]{3,0,1,2:T(8,128)(2,1)} %all-gather.3.cloned.1.call-done), calls=%async_computation.2 | async-start | bytes 2097152 | tf_op jit(solution)/shard_map/all_to_all | solution.py:45
  131.1 31.5 %all-to-all-start.3 = ((bf16[128,1,8,512]{3,0,1,2:T(8,128)(2,1)}), bf16[128,1,8,512]{3,0,1,2:T(8,128)(2,1)S(1)}, u32[]{:S(2)}, u32[]{:S(2)}) async-start(bf16[128,1,8,512]{3,0,1,2:T(8,128)(2,1)} %all-gather.5.cloned.1.call-done), calls=%async_computation.3 | async-start | bytes 2097152 | tf_op jit(solution)/shard_map/all_to_all | solution.py:46
  135.2 198.8 %all-reduce.5.cloned.1.call-start = ((), (), s32[]{:S(2)}) async-start(), calls=%async_computation.7 | async-start | bytes 4194304 | tf_op jit(solution)/shard_map/psum | solution.py:142
  220.2 2.2 copy-start
  222.2 0.7 copy-start.8
  222.3 0.7 copy-start.9
  223.0 1.2 copy-start.5
  334.0 2.2 copy-start.2
  336.3 0.7 copy-start.10
  336.3 0.7 copy-start.11
Sparse Core Ops, SparseCore 0:
  11.1 50.7 all-gather.2
  76.8 54.1 all-gather.4
Sparse Core Ops, SparseCore 1:
  97.4 122.8 all-reduce.2
  230.3 103.7 all-reduce.4
where the time goes:
time: 346 us; the launch traced here: 345 us
  waiting for transfers between devices  225 us (65%)
  blocking collectives  49.9 us (14%)
  starting transfers between devices  20.4 us (6%)
  between operations  17.7 us (5%)
  other arithmetic  11.5 us (3%)
  matrix products  11.2 us (3%)
  local copies, waits for them, and re-layouts  9.31 us (3%)
    psum x2, waiting for transfers between devices, combine(): summed = lax.psum(term_fn(0, tok_rows), 'mp')  160 us
    all_gather x1, waiting for transfers between devices, body(): lax.all_gather(pieces[3], 'group', axis=0, tiled=True)  30.2 us
    all_gather x1, blocking collectives, body(): lax.all_gather(pieces[1], 'group', axis=0, tiled=True)  27.8 us
    all_to_all x1, waiting for transfers between devices, body(): lax.all_to_all(gathered[3], 'mp', split_axis=2, concat_axis=0, tiled=True)  26 us
    all_gather x1, blocking collectives, body(): lax.all_gather(pieces[0], 'group', axis=0, tiled=True)  22.1 us
    all_to_all x1, waiting for transfers between devices, body(): lax.all_to_all(gathered[0], 'mp', split_axis=2, concat_axis=0, tiled=True)  8.33 us
  transfers between devices with their start and end apart: 10, of which 5 were waited for; matrix products, arithmetic and copies ran while one was open for 5% of the time, Pallas kernels for 0%

commit v1 on v0

v1 whole, which is shorter than its diff:
```python
import jax
import jax.numpy as jnp
from jax import lax
from jax.experimental import pallas as pl
from jax.experimental.pallas import tpu as pltpu
from jax.sharding import Mesh
from jax.sharding import PartitionSpec as P

HD = 64
BF = jnp.bfloat16
F32 = jnp.float32
EPS = 1e-05
NT = (((1,), (1,)), ((), ()))
GROUP = ("yh", "xx", "cc")
PART = ("zz", "yl")
PARAMS = pltpu.CompilerParams(vmem_limit_bytes=56 * 1024 * 1024)
VM = pl.BlockSpec(memory_space=pltpu.VMEM)
SM = pl.BlockSpec(memory_space=pltpu.SMEM)


def low_lanes(shape):
    return lax.broadcasted_iota(jnp.int32, shape, len(shape) - 1) < HD


def turned(value):
    return pltpu.roll(value, HD, len(value.shape) - 1)


def pack_kernel(qkv_ref, out_ref, up_ref, down_ref, packed_ref):
    rows, width = out_ref.shape
    copies, targets = packed_ref.shape[:2]
    shards = targets // 2
    hidden = up_ref.shape[1] // shards
    half_w, half_h = width // 2, hidden // 2
    low = low_lanes((rows, 128))
    for core in range(2):
        outs = []
        for pair in range(shards // 2):
            one = out_ref[:, pair * 256 : pair * 256 + 128]
            two = out_ref[:, pair * 256 + 128 : pair * 256 + 256]
            if core == 0:
                outs.append(jnp.where(low, one, turned(two)))
            else:
                outs.append(jnp.where(low, turned(one), two))
        out_half = jnp.concatenate(outs, axis=1).astype(BF)
        for part in range(shards):
            q_tile = qkv_ref[:, part * 128 : part * 128 + 128]
            k_tile = qkv_ref[:, width + part * 128 : width + part * 128 + 128]
            v_tile = qkv_ref[:, 2 * width + part * 128 : 2 * width + part * 128 + 128]
            if core == 0:
                qk = jnp.where(low, q_tile, turned(k_tile))
                vz = jnp.where(low, v_tile, 0.0)
            else:
                qk = jnp.where(low, turned(q_tile), k_tile)
                vz = jnp.where(low, turned(v_tile), 0.0)
            start = part * hidden + core * half_h
            up_half = up_ref[:, start : start + half_h].astype(BF)
            down_half = down_ref[:, start : start + half_h].astype(BF)
            row = jnp.concatenate([out_half, up_half, down_half, qk.astype(BF), vz.astype(BF)], axis=1)
            for copy in range(copies):
                packed_ref[copy, core * shards + part] = row


def attend_kernel(core_ref, own_ref, other_ref, weight_ref, idc_ref, idr_ref, att_ref, kv_own_ref, kv_other_ref, q_scr, k_scr, v_scr):
    core = core_ref[0]
    rows = own_ref.shape[0]
    shards = att_ref.shape[1]
    weight = weight_ref[...]
    low = low_lanes((rows, 128))
    for side, (x_ref, kv_ref) in enumerate(((own_ref, kv_own_ref), (other_ref, kv_other_ref))):
        projected = jnp.dot(x_ref[...], weight, preferred_element_type=F32)
        projected = projected.astype(BF).astype(F32)
        qk = projected[:, :128]
        vv = projected[:, 128:]
        keys = turned(qk)
        span = slice(side * rows, (side + 1) * rows)
        q_scr[span] = jnp.where(low, qk * (HD ** (-0.5)), 0.0).astype(BF)
        k_scr[span] = keys.astype(BF)
        v_scr[span] = jnp.where(low, vv, 1.0).astype(BF)
        kv_ref[...] = jnp.where(low, keys, turned(vv)).astype(BF)
    all_keys = k_scr[...]
    all_values = v_scr[...]
    ids_row = idr_ref[...]
    step = 128
    low_step = low_lanes((step, 128))

    def chunk(start):
        scores = lax.dot_general(q_scr[start : start + step], all_keys, NT, preferred_element_type=F32)
        same = idc_ref[start : start + step, 0:1] == ids_row
        scores = jnp.where(same, scores, -1e30)
        peak = jnp.max(scores, axis=1, keepdims=True)
        weights = jnp.exp(scores - peak).astype(BF)
        mixed = jnp.dot(weights, all_values, preferred_element_type=F32)
        return mixed / mixed[:, HD : HD + 1]

    for side in range(2):
        place = core if side == 0 else 1 - core
        for begin in range(0, rows // 2, step):
            first = chunk(side * rows + begin)
            second = chunk(side * rows + rows // 2 + begin)
            packed = jnp.where(low_step, first, turned(second)).astype(BF)
            for part in range(shards):
                att_ref[place, part, begin : begin + step] = packed


def normed(values, gain, shift):
    center = values - jnp.mean(values, axis=-1, keepdims=True)
    spread = jnp.mean(center * center, axis=-1, keepdims=True)
    return center * lax.rsqrt(spread + EPS) * gain + shift


def gelu(value):
    return 0.5 * value * (1.0 + lax.erf(value * (2.0 ** (-0.5))))


def feed_kernel(place_ref, att_ref, mine_ref, theirs_ref, x_ref, gain_ref, shift_ref, part_ref, keep_ref, att_scr, norm_scr):
    core = place_ref[0]
    part = place_ref[1]
    shards = att_ref.shape[1]
    half_rows = att_ref.shape[2]
    rows, width = x_ref.shape
    half_w = width // 2
    half_h = (mine_ref.shape[1] - 256 - half_w) // 2
    low = low_lanes((half_rows, 128))
    for side in range(2):
        place = core if side == 0 else 1 - core
        for pair in range(shards // 2):
            one = att_ref[place, 2 * pair].astype(F32)
            two = att_ref[place, 2 * pair + 1].astype(F32)
            lanes = slice(pair * 128, pair * 128 + 128)
            att_scr[side, :half_rows, lanes] = jnp.where(low, one, turned(two)).astype(BF)
            att_scr[side, half_rows:, lanes] = jnp.where(low, turned(one), two).astype(BF)
    gain = gain_ref[...]
    shift = shift_ref[...]
    step = rows // 2
    share = rows // shards
    for begin in range(0, rows, step):
        span = slice(begin, begin + step)
        total = x_ref[span].astype(F32)
        for side, ref in enumerate((mine_ref, theirs_ref)):
            total += lax.dot_general(att_scr[side, span], ref[:, :half_w], NT, preferred_element_type=F32)
        norm = normed(total, gain, shift).astype(BF)
        norm_scr[span] = norm
        result = jnp.zeros((step, width), F32)
        for ref in (mine_ref, theirs_ref):
            up = jnp.dot(norm, ref[:, half_w : half_w + half_h], preferred_element_type=F32)
            active = gelu(up).astype(BF)
            result += lax.dot_general(active, ref[:, half_w + half_h : half_w + 2 * half_h], NT, preferred_element_type=F32)
        for row in range(0, step, share):
            part_ref[(begin + row) // share] = result[row : row + share].astype(BF)
    keep_ref[...] = norm_scr[pl.ds(pl.multiple_of(part * share, share), share)]


def final_kernel(sums_ref, keep_ref, gain_ref, shift_ref, out_ref):
    total = keep_ref[...].astype(F32)
    for shard in range(sums_ref.shape[0]):
        total += sums_ref[shard].astype(F32)
    out_ref[...] = normed(total, gain_ref[...], shift_ref[...]).astype(BF)


def cache_kernel(core_ref, own_ref, got_ref, keys_ref, values_ref):
    low = low_lanes(own_ref.shape)
    own = own_ref[...].astype(F32)
    got = got_ref[...].astype(F32)
    even = core_ref[0] == 0
    first = jnp.where(even, own, got)
    second = jnp.where(even, got, own)
    keys_ref[...] = jnp.where(low, first, turned(second)).astype(BF)
    values_ref[...] = jnp.where(low, turned(first), second).astype(BF)


def exchange(value, axes):
    return lax.all_to_all(value, axes, split_axis=0, concat_axis=0, tiled=True)


def swapped(value):
    return lax.ppermute(value, "cc", [(0, 1), (1, 0)])


def body(hidden_in, request_ids, w_qkv, w_out, w_up, w_down, ln1_gain, ln1_shift, ln2_gain, ln2_shift):
    groups = lax.axis_size("yh") * lax.axis_size("xx") * lax.axis_size("cc")
    shards = lax.axis_size("zz") * lax.axis_size("yl")
    rows, width = hidden_in.shape
    part_rows = w_qkv.shape[0]
    hidden = w_up.shape[1] // shards
    columns = width // 2 + hidden + 256
    core = lax.axis_index("cc")
    part = lax.axis_index("zz") * lax.axis_size("yl") + lax.axis_index("yl")
    core_arg = core.reshape(1).astype(jnp.int32)
    place_arg = jnp.stack([core, part]).astype(jnp.int32)

    packed = pl.pallas_call(
        pack_kernel,
        out_shape=jax.ShapeDtypeStruct((groups // 2, 2 * shards, part_rows, columns), BF),
        in_specs=[VM] * 4,
        out_specs=VM,
        compiler_params=PARAMS,
        name="pack",
    )(w_qkv, w_out, w_up, w_down)
    served = exchange(packed.reshape(groups * shards, part_rows, columns), GROUP + PART)
    served = served.reshape(width, columns)
    other_hidden = swapped(hidden_in)
    other_ids = swapped(request_ids)
    ids = jnp.concatenate([request_ids, other_ids])
    ids_col = jnp.broadcast_to(ids[:, None], (2 * rows, 128))
    ids_row = ids[None, :]
    last = columns // 256 - 1

    att, kv_own, kv_other = pl.pallas_call(
        attend_kernel,
        grid=(1,),
        out_shape=(
            jax.ShapeDtypeStruct((2, shards, rows // 2, 128), BF),
            jax.ShapeDtypeStruct((rows, 128), BF),
            jax.ShapeDtypeStruct((rows, 128), BF),
        ),
        in_specs=[SM, VM, VM, pl.BlockSpec((width, 256), lambda i: (0, last)), VM, VM],
        out_specs=(VM, VM, VM),
        scratch_shapes=[pltpu.VMEM((2 * rows, 128), BF)] * 3,
        compiler_params=PARAMS,
        name="attend",
    )(core_arg, hidden_in, other_hidden, served, ids_col, ids_row)
    served_other = swapped(served)
    kv_got = swapped(kv_other)
    att_all = exchange(att.reshape(2 * shards, rows // 2, 128), ("cc",) + PART)
    att_all = att_all.reshape(2, shards, rows // 2, 128)

    keys_out, values_out = pl.pallas_call(
        cache_kernel,
        out_shape=(jax.ShapeDtypeStruct((rows, 128), BF),) * 2,
        in_specs=[SM, VM, VM],
        out_specs=(VM, VM),
        compiler_params=PARAMS,
        name="cache",
    )(core_arg, kv_own, kv_got)

    share = rows // shards
    sums, keep = pl.pallas_call(
        feed_kernel,
        out_shape=(
            jax.ShapeDtypeStruct((shards, share, width), BF),
            jax.ShapeDtypeStruct((share, width), BF),
        ),
        in_specs=[SM] + [VM] * 6,
        out_specs=(VM, VM),
        scratch_shapes=[pltpu.VMEM((2, rows, width // 2), BF), pltpu.VMEM((rows, width), BF)],
        compiler_params=PARAMS,
        name="feed",
    )(place_arg, att_all, served, served_other, hidden_in, ln1_gain[None, :], ln1_shift[None, :])
    sums_all = exchange(sums, PART)
    final = pl.pallas_call(
        final_kernel,
        out_shape=jax.ShapeDtypeStruct((share, width), BF),
        in_specs=[VM] * 4,
        out_specs=VM,
        compiler_params=PARAMS,
        name="final",
    )(sums_all, keep, ln2_gain[None, :], ln2_shift[None, :])
    return (final, keys_out, values_out)


def solution(mesh):
    fine = Mesh(mesh.devices.reshape(2, 4, 2, 4, 2), GROUP + PART)
    in_specs = (
        P(GROUP, None),
        P(GROUP),
        P(GROUP + PART, None),
        P(GROUP + PART, None),
        P(GROUP + PART, None),
        P(GROUP + PART, None),
        P(),
        P(),
        P(),
        P(),
    )
    out_specs = (P(GROUP + PART, None), P(GROUP, PART), P(GROUP, PART))
    return jax.shard_map(body, mesh=fine, in_specs=in_specs, out_specs=out_specs, check_vma=False)
```

time: 346 us -> 114 us (0.33)
  waiting for transfers between devices: 225 us -> 31.7 us
  Pallas kernels: 0 us -> 21.2 us
  between operations: 17.7 us -> 0.67 us
  matrix products: 11.2 us -> 0 us
  other arithmetic: 11.5 us -> 0.61 us
  starting transfers between devices: 20.4 us -> 10.4 us
  local copies, waits for them, and re-layouts: 9.31 us -> 2.65 us
  blocking collectives: 49.9 us -> 46.4 us
    psum x2 -> x0, waiting for transfers between devices: 160 us -> none  [combine(): summed = lax.psum(term_fn(0, tok_rows), 'mp')]
    all_gather x2 -> x0, blocking collectives: 49.9 us -> none  [the longest x1 27.8 us: body(): lax.all_gather(pieces[1], 'group', axis=0, tiled=True)]
    all_to_all x0 -> x1, blocking collectives: none -> 46.4 us  [exchange(): return lax.all_to_all(value, axes, split_axis=0, concat_axis=0, tiled=True)]
    all_gather x2 -> x0, waiting for transfers between devices: 30.2 us -> none  [the longest x1 30.2 us: body(): lax.all_gather(pieces[3], 'group', axis=0, tiled=True)]
    pallas_call x0 -> x5, Pallas kernels: none -> 21.2 us  [the longest x1 7.54 us: body(): pl.pallas_call(feed_kernel, out_shape=(jax.ShapeDtypeStruct((shards, shar...]
    dot_general x7 -> x0, matrix products: 11.2 us -> none  [the longest x1 5.93 us: feed_term(): lax.dot_general(activated, down_local, (((1,), (1,)), ((), ())), preferre...]
    all_to_all x4 -> x2, starting transfers between devices: 18.6 us -> 7.8 us  [exchange(): return lax.all_to_all(value, axes, split_axis=0, concat_axis=0, tiled=True)]
    all_to_all x4 -> x2, waiting for transfers between devices: 34.4 us -> 25 us  [exchange(): return lax.all_to_all(value, axes, split_axis=0, concat_axis=0, tiled=True)]
  transfers between devices with their start and end apart: 10 -> 6, of which waited for: 5 -> 5; matrix products, arithmetic and copies ran while one was open for 5% -> 1% of each run, Pallas kernels for 0% -> 8%
where the time goes in v1:
time: 114 us
  blocking collectives  46.4 us (41%)
  waiting for transfers between devices  31.7 us (28%)
  Pallas kernels  21.2 us (19%)
  starting transfers between devices  10.4 us (9%)
  local copies, waits for them, and re-layouts  2.65 us (2%)
    all_to_all x1, blocking collectives, exchange(): return lax.all_to_all(value, axes, split_axis=0, concat_axis=0, tiled=True)  46.4 us
    all_to_all x2, waiting for transfers between devices, exchange(): return lax.all_to_all(value, axes, split_axis=0, concat_axis=0, tiled=True)  25 us
    all_to_all x2, starting transfers between devices, exchange(): return lax.all_to_all(value, axes, split_axis=0, concat_axis=0, tiled=True)  7.8 us
    pallas_call x1, Pallas kernels, body(): pl.pallas_call(feed_kernel, out_shape=(jax.ShapeDtypeStruct((shards, shar...  7.54 us
    pallas_call x1, Pallas kernels, body(): pl.pallas_call(attend_kernel, grid=(1,), out_shape=(jax.ShapeDtypeStruct(...  6.85 us
    ppermute x4, waiting for transfers between devices, swapped(): return lax.ppermute(value, 'cc', [(0, 1), (1, 0)])  6.71 us
    pallas_call x1, Pallas kernels, body(): pl.pallas_call(pack_kernel, out_shape=jax.ShapeDtypeStruct((groups // 2,...  2.74 us
    ppermute x4, starting transfers between devices, swapped(): return lax.ppermute(value, 'cc', [(0, 1), (1, 0)])  2.59 us
  transfers between devices with their start and end apart: 6, of which 5 were waited for; matrix products, arithmetic and copies ran while one was open for 1% of the time, Pallas kernels for 8%

profile of v1, /device:TPU:1, one launch (start us, length us, event | category | flops | bytes accessed | tf_op | source)
XLA Modules:
  0.0 113.7 jit_solution(18185210714150164513)
XLA Ops:
  0.6 2.7 %pack.1 = bf16[8,16,8,1280]{3,2,1,0:T(8,128)(2,1)} custom-call(f32[8,3072]{1,0:T(8,128)} %qkv_ref.1, f32[8,1024]{1,0:T(8,128)} %out_ref.1, f32[8,4096]{1,0:T(8,128)} %up_ref.1, f32[8,4096]{1,0:T(8,128)} %down_ref.1), custom_call_target="tpu_custom_call" | custom-call | tf_op jit(solution)/shard_map/pack/pallas_call | solution.py:192
  3.4 0.0 copy-start.4
  3.4 46.4 %all_to_all.15 = bf16[128,8,1280]{2,1,0:T(8,128)(2,1)S(1)} all-to-all(bf16[128,8,1280]{2,1,0:T(8,128)(2,1)} %bitcast.14), channel_id=1, replica_groups=mesh['yh'=2,'xx'=4,'cc'=2,'zz'=4,'yl'=2] {'yh','xx','cc','zz','yl'}, dimensions={0} | all-to-all | bytes 5242880 | tf_op jit(solution)/shard_map/all_to_all | solution.py:173
  49.8 0.0 copy-start
  49.8 1.2 %collective-permute-start.2 = (bf16[1024,1280]{1,0:T(8,128)(2,1)S(1)}, bf16[1024,1280]{1,0:T(8,128)(2,1)}, u32[]{:S(2)}, u32[]{:S(2)}) collective-permute-start(bf16[1024,1280]{1,0:T(8,128)(2,1)S(1)} %bitcast.11), channel_id=1, source_target_pairs={{0,8},{8,0},{1,9},{9,1},{2,10},{10,2},{3,11},{11,3},{4,12},{12,4},... | collective-permute-start | bytes 7864328 | tf_op jit(solution)/shard_map/ppermute | solution.py:177
  51.0 0.0 collective-permute-start
  51.0 0.0 copy-done.4
  51.0 0.5 collective-permute-start.1
  51.5 3.9 %collective-permute-done.1 = s32[512]{0:T(512)S(1)} collective-permute-done((s32[512]{0:T(512)S(1)}, s32[512]{0:T(512)S(1)}, u32[]{:S(2)}, u32[]{:S(2)}) %collective-permute-start.1) | collective-permute-done | bytes 2080 | tf_op jit(solution)/shard_map/ppermute | solution.py:177
  55.4 0.0 copy-start.3
  55.4 1.8 %collective-permute-done.other_ref = bf16[512,1024]{1,0:T(8,128)(2,1)} collective-permute-done((bf16[512,1024]{1,0:T(8,128)(2,1)}, bf16[512,1024]{1,0:T(8,128)(2,1)}, u32[]{:S(2)}, u32[]{:S(2)}) %collective-permute-start) | collective-permute-done | bytes 1048608 | tf_op jit(solution)/shard_map/ppermute | solution.py:177
  57.2 1.0 broadcast_in_dim.21.idc_ref
  58.2 0.0 copy-done
  58.2 0.0 copy-done.3
  58.2 6.9 %attend.1 = (bf16[2,8,256,128]{3,2,1,0:T(8,128)(2,1)}, bf16[512,128]{1,0:T(8,128)(2,1)}, bf16[512,128]{1,0:T(8,128)(2,1)}) custom-call(s32[1]{0:T(128)} %bitcast.core_ref, bf16[512,1024]{1,0:T(8,128)(2,1)} %x_ref.1, bf16[512,1024]{1,0:T(8,128)(2,1)} %collective-permute-done.other_ref, bf16[1024,1280]{1,0:T(8,128)(2,1)} %bitcast.12, ...), custom_call_target="tpu_custom_call" | custom-call | tf_op jit(solution)/shard_map/attend/pallas_call | solution.py:209
  65.1 4.2 %all-to-all-start.1 = ((bf16[16,256,128]{2,1,0:T(8,128)(2,1)}), bf16[16,256,128]{2,1,0:T(8,128)(2,1)}, u32[]{:S(2)}, u32[]{:S(2)}) async-start(bf16[16,256,128]{2,1,0:T(8,128)(2,1)} %bitcast.15), calls=%async_computation.1 | async-start | bytes 2097152 | tf_op jit(solution)/shard_map/all_to_all | solution.py:173
  69.3 0.6 pad_add_fusion.place_ref
  70.0 14.5 %all-to-all-done.1 = bf16[16,256,128]{2,1,0:T(8,128)(2,1)} async-done(((bf16[16,256,128]{2,1,0:T(8,128)(2,1)}), bf16[16,256,128]{2,1,0:T(8,128)(2,1)}, u32[]{:S(2)}, u32[]{:S(2)}) %all-to-all-start.1) | async-done | bytes 1048608 | tf_op jit(solution)/shard_map/all_to_all | solution.py:173
  84.4 0.0 collective-permute-done.2.theirs_ref
  84.4 0.0 copy-start.5
  84.4 7.5 %feed.1 = (bf16[8,64,1024]{2,1,0:T(8,128)(2,1)}, bf16[64,1024]{1,0:T(8,128)(2,1)}) custom-call(s32[2]{0:T(128)} %pad_add_fusion.place_ref, bf16[2,8,256,128]{3,2,1,0:T(8,128)(2,1)} %bitcast.6.att_ref, bf16[1024,1280]{1,0:T(8,128)(2,1)} %bitcast.13, bf16[1024,1280]{1,0:T(8,128)(2,1)} %collective-permute-done.2.theirs_ref, bf16[512,1024]{1,0:T(8,128)(2,1)} %x_ref.1, ...), custom_call_target="tpu_custom_call" | custom-call | tf_op jit(solution)/shard_map/feed/pallas_call | solution.py:238
  92.0 3.6 %all-to-all-start.2 = ((bf16[8,64,1024]{2,1,0:T(8,128)(2,1)}), bf16[8,64,1024]{2,1,0:T(8,128)(2,1)S(1)}, u32[]{:S(2)}, u32[]{:S(2)}) async-start(bf16[8,64,1024]{2,1,0:T(8,128)(2,1)} %get-tuple-element.11), calls=%async_computation.2 | async-start | bytes 2097152 | tf_op jit(solution)/shard_map/all_to_all | solution.py:173
  95.5 0.0 copy-done.5
  95.6 0.9 collective-permute-start.3
  96.4 1.0 collective-permute-done.3.got_ref
  97.4 0.0 copy-start.2
  97.4 0.6 copy-done.2
  98.1 1.8 %cache.1 = (bf16[512,128]{1,0:T(8,128)(2,1)}, bf16[512,128]{1,0:T(8,128)(2,1)}) custom-call(s32[1]{0:T(128)} %bitcast.core_ref, bf16[512,128]{1,0:T(8,128)(2,1)} %get-tuple-element.13.own_ref, bf16[512,128]{1,0:T(8,128)(2,1)} %copy-done.2), custom_call_target="tpu_custom_call" | custom-call | tf_op jit(solution)/shard_map/cache/pallas_call | solution.py:228
  99.9 10.5 %all-to-all-done.2.sums_ref = bf16[8,64,1024]{2,1,0:T(8,128)(2,1)S(1)} async-done(((bf16[8,64,1024]{2,1,0:T(8,128)(2,1)}), bf16[8,64,1024]{2,1,0:T(8,128)(2,1)S(1)}, u32[]{:S(2)}, u32[]{:S(2)}) %all-to-all-start.2) | async-done | bytes 1048608 | tf_op jit(solution)/shard_map/all_to_all | solution.py:173
  110.4 0.0 copy-start.1
  110.4 1.0 copy-done.1
  111.4 2.3 %final.1 = bf16[64,1024]{1,0:T(8,128)(2,1)} custom-call(bf16[8,64,1024]{2,1,0:T(8,128)(2,1)} %copy-done.1, bf16[64,1024]{1,0:T(8,128)(2,1)} %get-tuple-element.12.keep_ref, f32[1,1024]{1,0:T(1,128)} %bitcast.19, f32[1,1024]{1,0:T(1,128)} %bitcast.20), custom_call_target="tpu_custom_call" | custom-call | tf_op jit(solution)/shard_map/final/pallas_call | solution.py:251
  (3 shorter events, 0.0 us)
Async XLA Ops:
  3.4 47.6 %copy-start.4 = (s32[512]{0:T(512)S(1)}, s32[512]{0:T(512)}, u32[]{:S(2)}) copy-start(s32[512]{0:T(512)} %param.11) | copy-start | bytes 6148
  49.8 8.5 %copy-start = (bf16[128,8,1280]{2,1,0:T(8,128)(2,1)}, bf16[128,8,1280]{2,1,0:T(8,128)(2,1)S(1)}, u32[]{:S(2)}) copy-start(bf16[128,8,1280]{2,1,0:T(8,128)(2,1)S(1)} %all_to_all.15) | copy-start | bytes 7864324
  49.8 34.7 %collective-permute-start.2 = (bf16[1024,1280]{1,0:T(8,128)(2,1)S(1)}, bf16[1024,1280]{1,0:T(8,128)(2,1)}, u32[]{:S(2)}, u32[]{:S(2)}) collective-permute-start(bf16[1024,1280]{1,0:T(8,128)(2,1)S(1)} %bitcast.11), channel_id=1, source_target_pairs={{0,8},{8,0},{1,9},{9,1},{2,10},{10,2},{3,11},{11,3},{4,12},{12,4},... | collective-permute-start | bytes 7864328 | tf_op jit(solution)/shard_map/ppermute | solution.py:177
  51.0 6.2 %collective-permute-start = (bf16[512,1024]{1,0:T(8,128)(2,1)}, bf16[512,1024]{1,0:T(8,128)(2,1)}, u32[]{:S(2)}, u32[]{:S(2)}) collective-permute-start(bf16[512,1024]{1,0:T(8,128)(2,1)} %x_ref.1), channel_id=1, source_target_pairs={{0,8},{8,0},{1,9},{9,1},{2,10},{10,2},{3,11},{11,3},{4,12},{12,4},... | collective-permute-start | bytes 3145736 | tf_op jit(solution)/shard_map/ppermute | solution.py:177
  51.0 4.4 %collective-permute-start.1 = (s32[512]{0:T(512)S(1)}, s32[512]{0:T(512)S(1)}, u32[]{:S(2)}, u32[]{:S(2)}) collective-permute-start(s32[512]{0:T(512)S(1)} %copy-done.4), channel_id=1, source_target_pairs={{0,8},{8,0},{1,9},{9,1},{2,10},{10,2},{3,11},{11,3},{4,12},{12,4},... | collective-permute-start | bytes 6152 | tf_op jit(solution)/shard_map/ppermute | solution.py:177
  55.4 2.9 %copy-start.3 = (s32[1024]{0:T(1024)}, s32[1024]{0:T(1024)S(1)}, u32[]{:S(2)}) copy-start(s32[1024]{0:T(1024)S(1)} %constant_dynamic-update-slice_fusion) | copy-start | bytes 12292
  65.1 19.3 %all-to-all-start.1 = ((bf16[16,256,128]{2,1,0:T(8,128)(2,1)}), bf16[16,256,128]{2,1,0:T(8,128)(2,1)}, u32[]{:S(2)}, u32[]{:S(2)}) async-start(bf16[16,256,128]{2,1,0:T(8,128)(2,1)} %bitcast.15), calls=%async_computation.1 | async-start | bytes 2097152 | tf_op jit(solution)/shard_map/all_to_all | solution.py:173
  84.4 11.1 %copy-start.5 = (bf16[512,128]{1,0:T(8,128)(2,1)S(1)}, bf16[512,128]{1,0:T(8,128)(2,1)}, u32[]{:S(2)}) copy-start(bf16[512,128]{1,0:T(8,128)(2,1)} %get-tuple-element.14) | copy-start | bytes 393220
  92.0 18.4 %all-to-all-start.2 = ((bf16[8,64,1024]{2,1,0:T(8,128)(2,1)}), bf16[8,64,1024]{2,1,0:T(8,128)(2,1)S(1)}, u32[]{:S(2)}, u32[]{:S(2)}) async-start(bf16[8,64,1024]{2,1,0:T(8,128)(2,1)} %get-tuple-element.11), calls=%async_computation.2 | async-start | bytes 2097152 | tf_op jit(solution)/shard_map/all_to_all | solution.py:173
  95.6 1.9 %collective-permute-start.3 = (bf16[512,128]{1,0:T(8,128)(2,1)S(1)}, bf16[512,128]{1,0:T(8,128)(2,1)S(1)}, u32[]{:S(2)}, u32[]{:S(2)}) collective-permute-start(bf16[512,128]{1,0:T(8,128)(2,1)S(1)} %copy-done.5), channel_id=1, source_target_pairs={{0,8},{8,0},{1,9},{9,1},{2,10},{10,2},{3,11},{11,3},{4,12},{12,4},... | collective-permute-start | bytes 393224 | tf_op jit(solution)/shard_map/ppermute | solution.py:177
  97.4 0.6 copy-start.2
  110.4 1.0 copy-start.1

commit v2 on v1

v2 whole, which is shorter than its diff:
```python
import jax
import jax.numpy as jnp
from jax import lax
from jax.experimental import pallas as pl
from jax.experimental.pallas import tpu as pltpu
from jax.sharding import Mesh
from jax.sharding import PartitionSpec as P

HD = 64
BF = jnp.bfloat16
F32 = jnp.float32
EPS = 1e-05
NT = (((1,), (1,)), ((), ()))
GROUP = ("yh", "xx", "cc")
PART = ("zz", "yl")
PARAMS = pltpu.CompilerParams(vmem_limit_bytes=24 * 1024 * 1024)
VM = pl.BlockSpec(memory_space=pltpu.VMEM)
SM = pl.BlockSpec(memory_space=pltpu.SMEM)


def low_lanes(shape):
    return lax.broadcasted_iota(jnp.int32, shape, len(shape) - 1) < HD


def turned(value):
    return pltpu.roll(value, HD, len(value.shape) - 1)


def pack_qkv_kernel(qkv_ref, packed_ref):
    rows = qkv_ref.shape[0]
    width = qkv_ref.shape[1] // 3
    copies, targets = packed_ref.shape[:2]
    shards = targets // 2
    low = low_lanes((rows, 128))
    for part in range(shards):
        q_tile = qkv_ref[:, part * 128 : part * 128 + 128]
        k_tile = qkv_ref[:, width + part * 128 : width + part * 128 + 128]
        v_tile = qkv_ref[:, 2 * width + part * 128 : 2 * width + part * 128 + 128]
        for core in range(2):
            if core == 0:
                qk = jnp.where(low, q_tile, turned(k_tile))
                vz = jnp.where(low, v_tile, 0.0)
            else:
                qk = jnp.where(low, turned(q_tile), k_tile)
                vz = jnp.where(low, turned(v_tile), 0.0)
            row = jnp.concatenate([qk.astype(BF), vz.astype(BF)], axis=1)
            for copy in range(copies):
                packed_ref[copy, core * shards + part] = row


def pack_rest_kernel(out_ref, up_ref, down_ref, packed_ref):
    width = out_ref.shape[1]
    copies, targets = packed_ref.shape[:2]
    shards = targets // 2
    hidden = up_ref.shape[1] // shards
    half_w, half_h = width // 2, hidden // 2
    for core in range(2):
        out_half = out_ref[:, core * half_w : core * half_w + half_w].astype(BF)
        for part in range(shards):
            start = part * hidden + core * half_h
            up_half = up_ref[:, start : start + half_h].astype(BF)
            down_half = down_ref[:, start : start + half_h].astype(BF)
            row = jnp.concatenate([out_half, up_half, down_half], axis=1)
            for copy in range(copies):
                packed_ref[copy, core * shards + part] = row


def attend_kernel(own_ref, other_ref, weight_ref, idc_ref, idr_ref, att_ref, kv_ref, send_ref, q_scr, k_scr, v_scr):
    rows = own_ref.shape[0]
    half = rows // 2
    weight = weight_ref[...]
    low = low_lanes((rows, 128))
    for side, x_ref in enumerate((own_ref, other_ref)):
        projected = jnp.dot(x_ref[...], weight, preferred_element_type=F32)
        projected = projected.astype(BF).astype(F32)
        qk = projected[:, :128]
        vv = projected[:, 128:]
        keys = turned(qk)
        span = slice(side * rows, (side + 1) * rows)
        q_scr[span] = jnp.where(low, qk * (HD ** (-0.5)), 0.0).astype(BF)
        k_scr[span] = keys.astype(BF)
        v_scr[span] = jnp.where(low, vv, 1.0).astype(BF)
        both = jnp.where(low, keys, turned(vv)).astype(BF)
        if side == 0:
            kv_ref[...] = both
        else:
            send_ref[half:] = both
    all_keys = k_scr[...]
    all_values = v_scr[...]
    ids_row = idr_ref[...]
    step = 128
    low_step = low_lanes((step, 128))

    def chunk(start):
        scores = lax.dot_general(q_scr[start : start + step], all_keys, NT, preferred_element_type=F32)
        same = idc_ref[start : start + step, 0:1] == ids_row
        scores = jnp.where(same, scores, -1e30)
        peak = jnp.max(scores, axis=1, keepdims=True)
        weights = jnp.exp(scores - peak).astype(BF)
        mixed = jnp.dot(weights, all_values, preferred_element_type=F32)
        return mixed / mixed[:, HD : HD + 1]

    for side in range(2):
        for begin in range(0, half, step):
            first = chunk(side * rows + begin)
            second = chunk(side * rows + half + begin)
            packed = jnp.where(low_step, first, turned(second)).astype(BF)
            if side == 0:
                att_ref[begin : begin + step] = packed
            else:
                send_ref[begin : begin + step] = packed


def join_kernel(core_ref, own_ref, got_ref, both_ref):
    half = own_ref.shape[0]
    low = low_lanes(own_ref.shape)
    own = own_ref[...].astype(F32)
    got = got_ref[:half].astype(F32)
    even = core_ref[0] == 0
    first = jnp.where(even, own, got)
    second = jnp.where(even, got, own)
    both_ref[:half] = jnp.where(low, first, turned(second)).astype(BF)
    both_ref[half:] = jnp.where(low, turned(first), second).astype(BF)


def normed(values, gain, shift):
    center = values - jnp.mean(values, axis=-1, keepdims=True)
    spread = jnp.mean(center * center, axis=-1, keepdims=True)
    return center * lax.rsqrt(spread + EPS) * gain + shift


def gelu(value):
    return 0.5 * value * (1.0 + lax.erf(value * (2.0 ** (-0.5))))


def feed_kernel(place_ref, *refs):
    (*piece_refs, mine_ref, theirs_ref, x_ref, gain_ref, shift_ref, part_ref, keep_ref, att_scr, norm_scr) = refs
    core = place_ref[0]
    part = place_ref[1]
    shards = len(piece_refs)
    rows, width = x_ref.shape
    half_w = width // 2
    half_h = (mine_ref.shape[1] - half_w) // 2
    for index, piece_ref in enumerate(piece_refs):
        source = part ^ index
        lanes = pl.ds(pl.multiple_of(source % (shards // 2) * 128, 128), 128)
        att_scr[source // (shards // 2), :, lanes] = piece_ref[...]
    gain = gain_ref[...]
    shift = shift_ref[...]
    step = rows // 2
    share = rows // shards
    for begin in range(0, rows, step):
        span = slice(begin, begin + step)
        total = x_ref[span].astype(F32)
        for side, ref in ((core, mine_ref), (1 - core, theirs_ref)):
            total += lax.dot_general(att_scr[side, span], ref[:, :half_w], NT, preferred_element_type=F32)
        norm = normed(total, gain, shift).astype(BF)
        norm_scr[span] = norm
        result = jnp.zeros((step, width), F32)
        for ref in (mine_ref, theirs_ref):
            up = jnp.dot(norm, ref[:, half_w : half_w + half_h], preferred_element_type=F32)
            active = gelu(up).astype(BF)
            result += lax.dot_general(active, ref[:, half_w + half_h : half_w + 2 * half_h], NT, preferred_element_type=F32)
        for row in range(0, step, share):
            part_ref[(begin + row) // share] = result[row : row + share].astype(BF)
    keep_ref[...] = norm_scr[pl.ds(pl.multiple_of(part * share, share), share)]


def final_kernel(sums_ref, keep_ref, gain_ref, shift_ref, out_ref):
    total = keep_ref[...].astype(F32)
    for shard in range(sums_ref.shape[0]):
        total += sums_ref[shard].astype(F32)
    out_ref[...] = normed(total, gain_ref[...], shift_ref[...]).astype(BF)


def cache_kernel(core_ref, own_ref, got_ref, keys_ref, values_ref):
    low = low_lanes(own_ref.shape)
    own = own_ref[...].astype(F32)
    got = got_ref[got_ref.shape[0] - own.shape[0] :].astype(F32)
    even = core_ref[0] == 0
    first = jnp.where(even, own, got)
    second = jnp.where(even, got, own)
    keys_ref[...] = jnp.where(low, first, turned(second)).astype(BF)
    values_ref[...] = jnp.where(low, turned(first), second).astype(BF)


def exchange(value, axes):
    return lax.all_to_all(value, axes, split_axis=0, concat_axis=0, tiled=True)


def swapped(value):
    return lax.ppermute(value, "cc", [(0, 1), (1, 0)])


def crossed(value, bits, shards):
    return lax.ppermute(value, PART, [(i, i ^ bits) for i in range(shards)])


def body(hidden_in, request_ids, w_qkv, w_out, w_up, w_down, ln1_gain, ln1_shift, ln2_gain, ln2_shift):
    groups = lax.axis_size("yh") * lax.axis_size("xx") * lax.axis_size("cc")
    shards = lax.axis_size("zz") * lax.axis_size("yl")
    rows, width = hidden_in.shape
    part_rows = w_qkv.shape[0]
    hidden = w_up.shape[1] // shards
    columns = width // 2 + hidden
    core = lax.axis_index("cc")
    part = lax.axis_index("zz") * lax.axis_size("yl") + lax.axis_index("yl")
    place_arg = jnp.stack([core, part]).astype(jnp.int32)

    def call(kernel, name, out_shape, in_specs, work=0, **more):
        more["cost_estimate"] = pl.CostEstimate(flops=work, bytes_accessed=2**20, transcendentals=0)
        flat = isinstance(out_shape, tuple)
        out_specs = (VM,) * len(out_shape) if flat else VM
        return pl.pallas_call(kernel, out_shape=out_shape, in_specs=in_specs, out_specs=out_specs, compiler_params=PARAMS, name=name, **more)

    def shape(*dims):
        return jax.ShapeDtypeStruct(dims, BF)

    packed_qkv = call(pack_qkv_kernel, "pack_qkv", shape(groups // 2, 2 * shards, part_rows, 256), [VM])(w_qkv)
    served_qkv = exchange(packed_qkv.reshape(groups * shards, part_rows, 256), GROUP + PART).reshape(width, 256)
    other_hidden = swapped(hidden_in)
    other_ids = swapped(request_ids)
    w_out, w_up, w_down, other_hidden, other_ids = lax.optimization_barrier((w_out, w_up, w_down, other_hidden, other_ids))
    packed_rest = call(pack_rest_kernel, "pack_rest", shape(groups // 2, 2 * shards, part_rows, columns), [VM] * 3)(w_out, w_up, w_down)
    packed_rest, served_qkv = lax.optimization_barrier((packed_rest, served_qkv))
    served = exchange(packed_rest.reshape(groups * shards, part_rows, columns), GROUP + PART).reshape(width, columns)
    ids = jnp.concatenate([request_ids, other_ids])
    ids_col = jnp.broadcast_to(ids[:, None], (2 * rows, 128))
    ids_row = ids[None, :]

    att_own, kv_own, send = call(
        attend_kernel,
        "attend",
        (shape(rows // 2, 128), shape(rows, 128), shape(rows // 2 + rows, 128)),
        [VM] * 5,
        6 * 10**9,
        scratch_shapes=[pltpu.VMEM((2 * rows, 128), BF)] * 3,
    )(hidden_in, other_hidden, served_qkv, ids_col, ids_row)
    got = swapped(send)
    pieces = {0: call(join_kernel, "join", shape(rows, 128), [SM, VM, VM])(place_arg, att_own, got)}
    for bits in (1, 2, 4, 6):
        pieces[bits] = crossed(pieces[0], bits, shards)
    for bits in (2, 4, 6):
        pieces[1 ^ bits] = crossed(pieces[1], bits, shards)
    early = tuple(i for i in pieces if i != shards - 1)
    served, held = lax.optimization_barrier((served, tuple(pieces[i] for i in early)))
    pieces.update(zip(early, held))
    served_other = swapped(served)

    keys_out, values_out = call(cache_kernel, "cache", (shape(rows, 128),) * 2, [SM, VM, VM])(place_arg, kv_own, got)

    share = rows // shards
    sums, keep = call(
        feed_kernel,
        "feed",
        (shape(shards, share, width), shape(share, width)),
        [SM] + [VM] * (shards + 5),
        6 * 10**9,
        scratch_shapes=[pltpu.VMEM((2, rows, width // 2), BF), pltpu.VMEM((rows, width), BF)],
    )(place_arg, *(pieces[i] for i in range(shards)), served, served_other, hidden_in, ln1_gain[None, :], ln1_shift[None, :])
    sums_all = exchange(sums, PART)
    final = call(final_kernel, "final", shape(share, width), [VM] * 4)(sums_all, keep, ln2_gain[None, :], ln2_shift[None, :])
    return (final, keys_out, values_out)


def solution(mesh):
    fine = Mesh(mesh.devices.reshape(2, 4, 2, 4, 2), GROUP + PART)
    in_specs = (
        P(GROUP, None),
        P(GROUP),
        P(GROUP + PART, None),
        P(GROUP + PART, None),
        P(GROUP + PART, None),
        P(GROUP + PART, None),
        P(),
        P(),
        P(),
        P(),
    )
    out_specs = (P(GROUP + PART, None), P(GROUP, PART), P(GROUP, PART))
    return jax.shard_map(body, mesh=fine, in_specs=in_specs, out_specs=out_specs, check_vma=False)
```

time: 114 us -> 104 us (0.912)
  blocking collectives: 46.4 us -> 0 us
  starting transfers between devices: 10.4 us -> 34.5 us
  waiting for transfers between devices: 31.7 us -> 45.6 us
  Pallas kernels: 21.2 us -> 14.8 us
  local copies, waits for them, and re-layouts: 2.65 us -> 7.35 us
    all_to_all x1 -> x0, blocking collectives: 46.4 us -> none  [exchange(): return lax.all_to_all(value, axes, split_axis=0, concat_axis=0, tiled=True)]
    ppermute x0 -> x7, waiting for transfers between devices: none -> 23.2 us  [crossed(): return lax.ppermute(value, PART, [(i, i ^ bits) for i in range(shards)])]
    all_to_all x2 -> x3, starting transfers between devices: 7.8 us -> 19 us  [exchange(): return lax.all_to_all(value, axes, split_axis=0, concat_axis=0, tiled=True)]
    ppermute x0 -> x7, starting transfers between devices: none -> 10.2 us  [crossed(): return lax.ppermute(value, PART, [(i, i ^ bits) for i in range(shards)])]
    pallas_call x5 -> x7, Pallas kernels: 21.2 us -> 14.8 us  [the longest x1 5.17 us: body(): call(feed_kernel, 'feed', (shape(shards, share, width), shape(share, widt...]
    unnamed x13 -> x27, local copies, waits for them, and re-layouts: 1.64 us -> 7.15 us
    ppermute x4, waiting for transfers between devices: 6.71 us -> 2.03 us  [swapped(): return lax.ppermute(value, 'cc', [(0, 1), (1, 0)])]
    all_to_all x2 -> x3, waiting for transfers between devices: 25 us -> 20.4 us  [exchange(): return lax.all_to_all(value, axes, split_axis=0, concat_axis=0, tiled=True)]
  transfers between devices with their start and end apart: 6 -> 14, of which waited for: 5 -> 9; matrix products, arithmetic and copies ran while one was open for 1% -> 0% of each run, Pallas kernels for 8% -> 8%
where the time goes in v2:
time: 104 us; the launch traced here: 103 us
  waiting for transfers between devices  45.6 us (44%)
  starting transfers between devices  34.5 us (33%)
  Pallas kernels  14.8 us (14%)
  local copies, waits for them, and re-layouts  7.35 us (7%)
    ppermute x7, waiting for transfers between devices, crossed(): return lax.ppermute(value, PART, [(i, i ^ bits) for i in range(shards)])  23.2 us
    all_to_all x3, waiting for transfers between devices, exchange(): return lax.all_to_all(value, axes, split_axis=0, concat_axis=0, tiled=True)  20.4 us
    all_to_all x3, starting transfers between devices, exchange(): return lax.all_to_all(value, axes, split_axis=0, concat_axis=0, tiled=True)  19 us
    ppermute x7, starting transfers between devices, crossed(): return lax.ppermute(value, PART, [(i, i ^ bits) for i in range(shards)])  10.2 us
    unnamed x27, local copies, waits for them, and re-layouts  7.15 us
    ppermute x4, starting transfers between devices, swapped(): return lax.ppermute(value, 'cc', [(0, 1), (1, 0)])  5.21 us
    pallas_call x1, Pallas kernels, body(): call(feed_kernel, 'feed', (shape(shards, share, width), shape(share, widt...  5.17 us
    pallas_call x1, Pallas kernels, body(): call(attend_kernel, 'attend', (shape(rows // 2, 128), shape(rows, 128), s...  4 us
  transfers between devices with their start and end apart: 14, of which 9 were waited for; matrix products, arithmetic and copies ran while one was open for 0% of the time, Pallas kernels for 8%

profile of v2, /device:TPU:1, one launch (start us, length us, event | category | flops | bytes accessed | tf_op | source)
XLA Modules:
  0.0 103.0 jit_solution(6584163806847100952)
XLA Ops:
  0.6 1.5 %collective-permute-start = (bf16[512,1024]{1,0:T(8,128)(2,1)}, bf16[512,1024]{1,0:T(8,128)(2,1)S(1)}, u32[]{:S(2)}, u32[]{:S(2)}) collective-permute-start(bf16[512,1024]{1,0:T(8,128)(2,1)} %refs_10_.1), channel_id=1, source_target_pairs={{0,8},{8,0},{1,9},{9,1},{2,10},{10,2},{3,11},{11,3},{4,12},{12,4},... | collective-permute-start | bytes 3145736 | tf_op jit(solution)/shard_map/ppermute | solution.py:192
  2.1 0.9 copy-done.2
  3.0 0.9 pack_qkv.1
  3.9 10.2 %all-to-all-start = ((bf16[128,8,256]{2,1,0:T(8,128)(2,1)}), bf16[128,8,256]{2,1,0:T(8,128)(2,1)S(1)}, u32[]{:S(2)}, u32[]{:S(2)}) async-start(bf16[128,8,256]{2,1,0:T(8,128)(2,1)} %bitcast.2), calls=%async_computation | async-start | bytes 1048576 | tf_op jit(solution)/shard_map/all_to_all | solution.py:188
  14.1 1.1 %collective-permute-start.1 = (s32[512]{0:T(512)}, s32[512]{0:T(512)S(1)}, u32[]{:S(2)}, u32[]{:S(2)}) collective-permute-start(s32[512]{0:T(512)} %param.11), channel_id=1, source_target_pairs={{0,8},{8,0},{1,9},{9,1},{2,10},{10,2},{3,11},{11,3},{4,12},{12,4},... | collective-permute-start | bytes 6152 | tf_op jit(solution)/shard_map/ppermute | solution.py:192
  15.3 1.0 %collective-permute-done.1 = s32[512]{0:T(512)S(1)} collective-permute-done((s32[512]{0:T(512)}, s32[512]{0:T(512)S(1)}, u32[]{:S(2)}, u32[]{:S(2)}) %collective-permute-start.1) | collective-permute-done | bytes 2080 | tf_op jit(solution)/shard_map/ppermute | solution.py:192
  16.3 0.9 copy-done
  17.2 0.9 copy-done.1
  18.1 0.8 copy-done.3
  18.9 1.7 %pack_rest.1 = bf16[8,16,8,1024]{3,2,1,0:T(8,128)(2,1)} custom-call(f32[8,1024]{1,0:T(8,128)S(1)} %copy-done.3, f32[8,4096]{1,0:T(8,128)S(1)} %copy-done, f32[8,4096]{1,0:T(8,128)S(1)} %copy-done.1), custom_call_target="tpu_custom_call" | custom-call | bytes 1048576 | tf_op jit(solution)/shard_map/pack_rest/pallas_call | solution.py:224
  20.6 6.7 %all-to-all-done = bf16[128,8,256]{2,1,0:T(8,128)(2,1)S(1)} async-done(((bf16[128,8,256]{2,1,0:T(8,128)(2,1)}), bf16[128,8,256]{2,1,0:T(8,128)(2,1)S(1)}, u32[]{:S(2)}, u32[]{:S(2)}) %all-to-all-start) | async-done | bytes 524320 | tf_op jit(solution)/shard_map/all_to_all | solution.py:188
  27.3 5.2 %all-to-all-start.1 = ((bf16[128,8,1024]{2,1,0:T(8,128)(2,1)}), bf16[128,8,1024]{2,1,0:T(8,128)(2,1)S(1)}, u32[]{:S(2)}, u32[]{:S(2)}) async-start(bf16[128,8,1024]{2,1,0:T(8,128)(2,1)} %bitcast.4), calls=%async_computation.1 | async-start | bytes 4194304 | tf_op jit(solution)/shard_map/all_to_all | solution.py:188
  32.7 1.2 %copy-done.6 = bf16[512,1024]{1,0:T(8,128)(2,1)S(1)} copy-done((bf16[512,1024]{1,0:T(8,128)(2,1)S(1)}, bf16[512,1024]{1,0:T(8,128)(2,1)}, u32[]{:S(2)}) %copy-start.6) | copy-done | bytes 1048600
  34.0 1.2 %copy-done.9 = bf16[512,1024]{1,0:T(8,128)(2,1)S(1)} copy-done((bf16[512,1024]{1,0:T(8,128)(2,1)S(1)}, bf16[512,1024]{1,0:T(8,128)(2,1)}, u32[]{:S(2)}) %copy-start.9) | copy-done | bytes 1048600
  35.2 4.0 %attend.1 = (bf16[256,128]{1,0:T(8,128)(2,1)S(1)}, bf16[512,128]{1,0:T(8,128)(2,1)S(1)}, bf16[768,128]{1,0:T(8,128)(2,1)S(1)}) custom-call(bf16[512,1024]{1,0:T(8,128)(2,1)S(1)} %copy-done.6, bf16[512,1024]{1,0:T(8,128)(2,1)S(1)} %copy-done.9, bf16[1024,256]{1,0:T(8,128)(2,1)S(1)} %bitcast.13, s32[1024,128]{1,0:T(8,128)S(1)} %broadcast_in_dim.21.idc_ref, ...), custom_call_target="tpu_custom_call" | custom-call | flops 6000000000 | bytes 1048576 | tf_op jit(solution)/shard_map/attend/pallas_call | solution.py:231
  39.2 1.1 %collective-permute-start.2 = (bf16[768,128]{1,0:T(8,128)(2,1)S(1)}, bf16[768,128]{1,0:T(8,128)(2,1)S(1)}, u32[]{:S(2)}, u32[]{:S(2)}) collective-permute-start(bf16[768,128]{1,0:T(8,128)(2,1)S(1)} %get-tuple-element.33), channel_id=1, source_target_pairs={{0,8},{8,0},{1,9},{9,1},{2,10},{10,2},{3,11},{11,3},{4,12},{12,4},... | collective-permute-start | bytes 589832 | tf_op jit(solution)/shard_map/ppermute | solution.py:192
  40.4 1.0 collective-permute-done.2.got_ref
  42.1 0.8 collective-permute-start.3
  42.8 3.1 %collective-permute-start.6 = (bf16[512,128]{1,0:T(8,128)(2,1)S(1)}, bf16[512,128]{1,0:T(8,128)(2,1)S(1)}, u32[]{:S(2)}, u32[]{:S(2)}) collective-permute-start(bf16[512,128]{1,0:T(8,128)(2,1)S(1)} %join.1.refs_0_), channel_id=1, source_target_pairs={{0,6},{1,7},{2,4},{3,5},{4,2},{5,3},{6,0},{7,1},{8,14},{9,15},{10,... | collective-permute-start | bytes 393224 | tf_op jit(solution)/shard_map/ppermute | solution.py:196
  46.5 12.5 %collective-permute-done.3.refs_1_ = bf16[512,128]{1,0:T(8,128)(2,1)S(1)} collective-permute-done((bf16[512,128]{1,0:T(8,128)(2,1)S(1)}, bf16[512,128]{1,0:T(8,128)(2,1)S(1)}, u32[]{:S(2)}, u32[]{:S(2)}) %collective-permute-start.3) | collective-permute-done | bytes 131104 | tf_op jit(solution)/shard_map/ppermute | solution.py:196
  59.1 3.1 %collective-permute-start.8 = (bf16[512,128]{1,0:T(8,128)(2,1)S(1)}, bf16[512,128]{1,0:T(8,128)(2,1)S(1)}, u32[]{:S(2)}, u32[]{:S(2)}) collective-permute-start(bf16[512,128]{1,0:T(8,128)(2,1)S(1)} %collective-permute-done.3.refs_1_), channel_id=1, source_target_pairs={{0,4},{1,5},{2,6},{3,7},{4,0},{5,1},{6,2},{7,3},{8,12},{9,13},{10,... | collective-permute-start | bytes 393224 | tf_op jit(solution)/shard_map/ppermute | solution.py:196
  63.0 2.3 %collective-permute-done.6.refs_6_ = bf16[512,128]{1,0:T(8,128)(2,1)S(1)} collective-permute-done((bf16[512,128]{1,0:T(8,128)(2,1)S(1)}, bf16[512,128]{1,0:T(8,128)(2,1)S(1)}, u32[]{:S(2)}, u32[]{:S(2)}) %collective-permute-start.6) | collective-permute-done | bytes 131104 | tf_op jit(solution)/shard_map/ppermute | solution.py:196
  65.3 3.5 %collective-permute-done.8.refs_5_ = bf16[512,128]{1,0:T(8,128)(2,1)S(1)} collective-permute-done((bf16[512,128]{1,0:T(8,128)(2,1)S(1)}, bf16[512,128]{1,0:T(8,128)(2,1)S(1)}, u32[]{:S(2)}, u32[]{:S(2)}) %collective-permute-start.8) | collective-permute-done | bytes 131104 | tf_op jit(solution)/shard_map/ppermute | solution.py:196
  69.2 1.4 %collective-permute-start.10 = (bf16[1024,1024]{1,0:T(8,128)(2,1)S(1)}, bf16[1024,1024]{1,0:T(8,128)(2,1)S(1)}, u32[]{:S(2)}, u32[]{:S(2)}) collective-permute-start(bf16[1024,1024]{1,0:T(8,128)(2,1)S(1)} %bitcast.11), channel_id=1, source_target_pairs={{0,8},{8,0},{1,9},{9,1},{2,10},{10,2},{3,11},{11,3},{4,12},{12,4},... | collective-permute-start | bytes 6291464 | tf_op jit(solution)/shard_map/ppermute | solution.py:192
  70.6 1.9 %collective-permute-start.9 = (bf16[512,128]{1,0:T(8,128)(2,1)S(1)}, bf16[512,128]{1,0:T(8,128)(2,1)S(1)}, u32[]{:S(2)}, u32[]{:S(2)}) collective-permute-start(bf16[512,128]{1,0:T(8,128)(2,1)S(1)} %collective-permute-done.3.refs_1_), channel_id=1, source_target_pairs={{0,6},{1,7},{2,4},{3,5},{4,2},{5,3},{6,0},{7,1},{8,14},{9,15},{10,... | collective-permute-start | bytes 393224 | tf_op jit(solution)/shard_map/ppermute | solution.py:196
  72.5 4.5 %collective-permute-done.9.refs_7_ = bf16[512,128]{1,0:T(8,128)(2,1)S(1)} collective-permute-done((bf16[512,128]{1,0:T(8,128)(2,1)S(1)}, bf16[512,128]{1,0:T(8,128)(2,1)S(1)}, u32[]{:S(2)}, u32[]{:S(2)}) %collective-permute-start.9) | collective-permute-done | bytes 131104 | tf_op jit(solution)/shard_map/ppermute | solution.py:196
  77.0 1.2 %copy-done.7 = bf16[512,1024]{1,0:T(8,128)(2,1)S(1)} copy-done((bf16[512,1024]{1,0:T(8,128)(2,1)S(1)}, bf16[512,1024]{1,0:T(8,128)(2,1)}, u32[]{:S(2)}) %copy-start.7) | copy-done | bytes 1048600
  78.2 5.2 %feed.1 = (bf16[8,64,1024]{2,1,0:T(8,128)(2,1)}, bf16[64,1024]{1,0:T(8,128)(2,1)S(1)}) custom-call(s32[2]{0:T(128)S(1)} %pad_add_fusion.core_ref.place_ref, bf16[512,128]{1,0:T(8,128)(2,1)S(1)} %join.1.refs_0_, bf16[512,128]{1,0:T(8,128)(2,1)S(1)} %collective-permute-done.3.refs_1_, bf16[512,128]{1,0:T(8,128)(2,1)S(1)} %collective-permute-done.4.refs_2_, ...), custom_call_target="tpu_custom_call" | custom-call | flops 6000000000 | bytes 1048576 | tf_op jit(solution)/shard_map/feed/pallas_call | solution.py:253
  83.3 3.7 %all-to-all-start.2 = ((bf16[8,64,1024]{2,1,0:T(8,128)(2,1)}), bf16[8,64,1024]{2,1,0:T(8,128)(2,1)S(1)}, u32[]{:S(2)}, u32[]{:S(2)}) async-start(bf16[8,64,1024]{2,1,0:T(8,128)(2,1)} %get-tuple-element.42), calls=%async_computation.2 | async-start | bytes 2097152 | tf_op jit(solution)/shard_map/all_to_all | solution.py:188
  87.0 1.4 %cache.1 = (bf16[512,128]{1,0:T(8,128)(2,1)}, bf16[512,128]{1,0:T(8,128)(2,1)}) custom-call(s32[2]{0:T(128)S(1)} %pad_add_fusion.core_ref.place_ref, bf16[512,128]{1,0:T(8,128)(2,1)S(1)} %get-tuple-element.44.own_ref, bf16[768,128]{1,0:T(8,128)(2,1)S(1)} %collective-permute-done.2.got_ref), custom_call_target="tpu_custom_call" | custom-call | bytes 1048576 | tf_op jit(solution)/shard_map/cache/pallas_call | solution.py:250
  88.4 13.6 %all-to-all-done.2.sums_ref = bf16[8,64,1024]{2,1,0:T(8,128)(2,1)S(1)} async-done(((bf16[8,64,1024]{2,1,0:T(8,128)(2,1)}), bf16[8,64,1024]{2,1,0:T(8,128)(2,1)S(1)}, u32[]{:S(2)}, u32[]{:S(2)}) %all-to-all-start.2) | async-done | bytes 1048608 | tf_op jit(solution)/shard_map/all_to_all | solution.py:188
  102.0 1.0 final.1
  (34 shorter events, 2.6 us)
Async XLA Ops:
  0.6 15.7 %collective-permute-start = (bf16[512,1024]{1,0:T(8,128)(2,1)}, bf16[512,1024]{1,0:T(8,128)(2,1)S(1)}, u32[]{:S(2)}, u32[]{:S(2)}) collective-permute-start(bf16[512,1024]{1,0:T(8,128)(2,1)} %refs_10_.1), channel_id=1, source_target_pairs={{0,8},{8,0},{1,9},{9,1},{2,10},{10,2},{3,11},{11,3},{4,12},{12,4},... | collective-permute-start | bytes 3145736 | tf_op jit(solution)/shard_map/ppermute | solution.py:192
  2.1 0.9 copy-start.2
  3.9 23.4 %all-to-all-start = ((bf16[128,8,256]{2,1,0:T(8,128)(2,1)}), bf16[128,8,256]{2,1,0:T(8,128)(2,1)S(1)}, u32[]{:S(2)}, u32[]{:S(2)}) async-start(bf16[128,8,256]{2,1,0:T(8,128)(2,1)} %bitcast.2), calls=%async_computation | async-start | bytes 1048576 | tf_op jit(solution)/shard_map/all_to_all | solution.py:188
  14.1 2.2 %collective-permute-start.1 = (s32[512]{0:T(512)}, s32[512]{0:T(512)S(1)}, u32[]{:S(2)}, u32[]{:S(2)}) collective-permute-start(s32[512]{0:T(512)} %param.11), channel_id=1, source_target_pairs={{0,8},{8,0},{1,9},{9,1},{2,10},{10,2},{3,11},{11,3},{4,12},{12,4},... | collective-permute-start | bytes 6152 | tf_op jit(solution)/shard_map/ppermute | solution.py:192
  16.3 0.9 copy-start
  17.2 0.9 copy-start.1
  18.1 0.8 copy-start.3
  18.9 8.4 %copy-start.8 = (bf16[512,1024]{1,0:T(8,128)(2,1)}, bf16[512,1024]{1,0:T(8,128)(2,1)S(1)}, u32[]{:S(2)}) copy-start(bf16[512,1024]{1,0:T(8,128)(2,1)S(1)} %collective-permute-done.other_ref) | copy-start | bytes 3145732
  27.3 5.2 %copy-start.12 = (s32[512]{0:T(512)S(1)}, s32[512]{0:T(512)}, u32[]{:S(2)}) copy-start(s32[512]{0:T(512)} %param.11) | copy-start | bytes 6148
  27.3 41.9 %all-to-all-start.1 = ((bf16[128,8,1024]{2,1,0:T(8,128)(2,1)}), bf16[128,8,1024]{2,1,0:T(8,128)(2,1)S(1)}, u32[]{:S(2)}, u32[]{:S(2)}) async-start(bf16[128,8,1024]{2,1,0:T(8,128)(2,1)} %bitcast.4), calls=%async_computation.1 | async-start | bytes 4194304 | tf_op jit(solution)/shard_map/all_to_all | solution.py:188
  32.7 1.2 %copy-start.6 = (bf16[512,1024]{1,0:T(8,128)(2,1)S(1)}, bf16[512,1024]{1,0:T(8,128)(2,1)}, u32[]{:S(2)}) copy-start(bf16[512,1024]{1,0:T(8,128)(2,1)} %refs_10_.1) | copy-start | bytes 3145732
  34.0 1.2 %copy-start.9 = (bf16[512,1024]{1,0:T(8,128)(2,1)S(1)}, bf16[512,1024]{1,0:T(8,128)(2,1)}, u32[]{:S(2)}) copy-start(bf16[512,1024]{1,0:T(8,128)(2,1)} %copy-done.8) | copy-start | bytes 3145732
  35.2 41.8 %copy-start.10 = (f32[1024]{0:T(1024)S(1)}, f32[1024]{0:T(1024)}, u32[]{:S(2)}) copy-start(f32[1024]{0:T(1024)} %param.16) | copy-start | bytes 12292
  35.2 41.8 %copy-start.11 = (f32[1024]{0:T(1024)S(1)}, f32[1024]{0:T(1024)}, u32[]{:S(2)}) copy-start(f32[1024]{0:T(1024)} %param.17) | copy-start | bytes 12292
  39.2 2.2 %collective-permute-start.2 = (bf16[768,128]{1,0:T(8,128)(2,1)S(1)}, bf16[768,128]{1,0:T(8,128)(2,1)S(1)}, u32[]{:S(2)}, u32[]{:S(2)}) collective-permute-start(bf16[768,128]{1,0:T(8,128)(2,1)S(1)} %get-tuple-element.33), channel_id=1, source_target_pairs={{0,8},{8,0},{1,9},{9,1},{2,10},{10,2},{3,11},{11,3},{4,12},{12,4},... | collective-permute-start | bytes 589832 | tf_op jit(solution)/shard_map/ppermute | solution.py:192
  42.1 17.0 %collective-permute-start.3 = (bf16[512,128]{1,0:T(8,128)(2,1)S(1)}, bf16[512,128]{1,0:T(8,128)(2,1)S(1)}, u32[]{:S(2)}, u32[]{:S(2)}) collective-permute-start(bf16[512,128]{1,0:T(8,128)(2,1)S(1)} %join.1.refs_0_), channel_id=1, source_target_pairs={{0,1},{1,0},{2,3},{3,2},{4,5},{5,4},{6,7},{7,6},{8,9},{9,8},{10,11... | collective-permute-start | bytes 393224 | tf_op jit(solution)/shard_map/ppermute | solution.py:196
  42.8 22.5 %collective-permute-start.6 = (bf16[512,128]{1,0:T(8,128)(2,1)S(1)}, bf16[512,128]{1,0:T(8,128)(2,1)S(1)}, u32[]{:S(2)}, u32[]{:S(2)}) collective-permute-start(bf16[512,128]{1,0:T(8,128)(2,1)S(1)} %join.1.refs_0_), channel_id=1, source_target_pairs={{0,6},{1,7},{2,4},{3,5},{4,2},{5,3},{6,0},{7,1},{8,14},{9,15},{10,... | collective-permute-start | bytes 393224 | tf_op jit(solution)/shard_map/ppermute | solution.py:196
  46.0 19.3 %collective-permute-start.5 = (bf16[512,128]{1,0:T(8,128)(2,1)S(1)}, bf16[512,128]{1,0:T(8,128)(2,1)S(1)}, u32[]{:S(2)}, u32[]{:S(2)}) collective-permute-start(bf16[512,128]{1,0:T(8,128)(2,1)S(1)} %join.1.refs_0_), channel_id=1, source_target_pairs={{0,4},{1,5},{2,6},{3,7},{4,0},{5,1},{6,2},{7,3},{8,12},{9,13},{10,... | collective-permute-start | bytes 393224 | tf_op jit(solution)/shard_map/ppermute | solution.py:196
  46.0 19.3 %collective-permute-start.4 = (bf16[512,128]{1,0:T(8,128)(2,1)S(1)}, bf16[512,128]{1,0:T(8,128)(2,1)S(1)}, u32[]{:S(2)}, u32[]{:S(2)}) collective-permute-start(bf16[512,128]{1,0:T(8,128)(2,1)S(1)} %join.1.refs_0_), channel_id=1, source_target_pairs={{0,2},{1,3},{2,0},{3,1},{4,6},{5,7},{6,4},{7,5},{8,10},{9,11},{10,... | collective-permute-start | bytes 393224 | tf_op jit(solution)/shard_map/ppermute | solution.py:196
  59.1 9.7 %collective-permute-start.8 = (bf16[512,128]{1,0:T(8,128)(2,1)S(1)}, bf16[512,128]{1,0:T(8,128)(2,1)S(1)}, u32[]{:S(2)}, u32[]{:S(2)}) collective-permute-start(bf16[512,128]{1,0:T(8,128)(2,1)S(1)} %collective-permute-done.3.refs_1_), channel_id=1, source_target_pairs={{0,4},{1,5},{2,6},{3,7},{4,0},{5,1},{6,2},{7,3},{8,12},{9,13},{10,... | collective-permute-start | bytes 393224 | tf_op jit(solution)/shard_map/ppermute | solution.py:196
  62.2 7.0 %collective-permute-start.7 = (bf16[512,128]{1,0:T(8,128)(2,1)S(1)}, bf16[512,128]{1,0:T(8,128)(2,1)S(1)}, u32[]{:S(2)}, u32[]{:S(2)}) collective-permute-start(bf16[512,128]{1,0:T(8,128)(2,1)S(1)} %collective-permute-done.3.refs_1_), channel_id=1, source_target_pairs={{0,2},{1,3},{2,0},{3,1},{4,6},{5,7},{6,4},{7,5},{8,10},{9,11},{10,... | collective-permute-start | bytes 393224 | tf_op jit(solution)/shard_map/ppermute | solution.py:196
  69.2 7.8 %collective-permute-start.10 = (bf16[1024,1024]{1,0:T(8,128)(2,1)S(1)}, bf16[1024,1024]{1,0:T(8,128)(2,1)S(1)}, u32[]{:S(2)}, u32[]{:S(2)}) collective-permute-start(bf16[1024,1024]{1,0:T(8,128)(2,1)S(1)} %bitcast.11), channel_id=1, source_target_pairs={{0,8},{8,0},{1,9},{9,1},{2,10},{10,2},{3,11},{11,3},{4,12},{12,4},... | collective-permute-start | bytes 6291464 | tf_op jit(solution)/shard_map/ppermute | solution.py:192
  70.6 6.3 %collective-permute-start.9 = (bf16[512,128]{1,0:T(8,128)(2,1)S(1)}, bf16[512,128]{1,0:T(8,128)(2,1)S(1)}, u32[]{:S(2)}, u32[]{:S(2)}) collective-permute-start(bf16[512,128]{1,0:T(8,128)(2,1)S(1)} %collective-permute-done.3.refs_1_), channel_id=1, source_target_pairs={{0,6},{1,7},{2,4},{3,5},{4,2},{5,3},{6,0},{7,1},{8,14},{9,15},{10,... | collective-permute-start | bytes 393224 | tf_op jit(solution)/shard_map/ppermute | solution.py:196
  76.9 1.2 %copy-start.7 = (bf16[512,1024]{1,0:T(8,128)(2,1)S(1)}, bf16[512,1024]{1,0:T(8,128)(2,1)}, u32[]{:S(2)}) copy-start(bf16[512,1024]{1,0:T(8,128)(2,1)} %refs_10_.1) | copy-start | bytes 3145732
  83.3 18.7 %copy-start.4 = (f32[1024]{0:T(1024)S(1)}, f32[1024]{0:T(1024)}, u32[]{:S(2)}) copy-start(f32[1024]{0:T(1024)} %param.18) | copy-start | bytes 12292
  83.3 18.7 %copy-start.5 = (f32[1024]{0:T(1024)S(1)}, f32[1024]{0:T(1024)}, u32[]{:S(2)}) copy-start(f32[1024]{0:T(1024)} %param.19) | copy-start | bytes 12292
  83.3 18.7 %all-to-all-start.2 = ((bf16[8,64,1024]{2,1,0:T(8,128)(2,1)}), bf16[8,64,1024]{2,1,0:T(8,128)(2,1)S(1)}, u32[]{:S(2)}, u32[]{:S(2)}) async-start(bf16[8,64,1024]{2,1,0:T(8,128)(2,1)} %get-tuple-element.42), calls=%async_computation.2 | async-start | bytes 2097152 | tf_op jit(solution)/shard_map/all_to_all | solution.py:188

commit v3 on v2

v3 whole, which is shorter than its diff:
```python
import jax
import jax.numpy as jnp
from jax import lax
from jax.experimental import pallas as pl
from jax.experimental.pallas import tpu as pltpu
from jax.sharding import Mesh
from jax.sharding import PartitionSpec as P

HD = 64
BF = jnp.bfloat16
F32 = jnp.float32
EPS = 1e-05
NT = (((1,), (1,)), ((), ()))
GROUP = ("yh", "xx", "cc")
PART = ("zz", "yl")
PARAMS = pltpu.CompilerParams(vmem_limit_bytes=24 * 1024 * 1024)
VM = pl.BlockSpec(memory_space=pltpu.VMEM)
SM = pl.BlockSpec(memory_space=pltpu.SMEM)


def low_lanes(shape):
    return lax.broadcasted_iota(jnp.int32, shape, len(shape) - 1) < HD


def turned(value):
    return pltpu.roll(value, HD, len(value.shape) - 1)


def spread():
    rows = lax.broadcasted_iota(jnp.int32, (128, 128), 0)
    cols = lax.broadcasted_iota(jnp.int32, (128, 128), 1)
    block, inner = cols // HD, cols % HD
    source = block * HD + inner % 32 // 8 * 16 + inner // 32 * 8 + inner % 8
    return jnp.where(rows == source, 1.0, 0.0)


def spread_rows(ref):
    moved = jnp.dot(ref[...], spread(), preferred_element_type=F32, precision=lax.Precision.HIGHEST)
    return jnp.concatenate([moved[i : i + 1] for i in range(ref.shape[0])], axis=1)


def pack_qkv_kernel(qkv_ref, packed_ref):
    rows = qkv_ref.shape[0]
    width = qkv_ref.shape[1] // 3
    copies, cores, depth, twins = packed_ref.shape[:4]
    low = low_lanes((rows, 128))

    def tile(kind, number):
        start = kind * width + number * 128
        return qkv_ref[:, start : start + 128]

    for z in range(depth):
        for core in range(cores):
            parts = []
            for twin in range(2):
                q_tile, k_tile = tile(0, 2 * z + twin), tile(1, 2 * z + twin)
                if core == 0:
                    parts.append(jnp.where(low, q_tile, turned(k_tile)))
                else:
                    parts.append(jnp.where(low, turned(q_tile), k_tile))
            one, two = tile(2, 2 * z), tile(2, 2 * z + 1)
            if core == 0:
                parts.append(jnp.where(low, one, turned(two)))
            else:
                parts.append(jnp.where(low, turned(one), two))
            row = jnp.concatenate(parts, axis=1).astype(BF)
            for copy in range(copies):
                for twin in range(twins):
                    packed_ref[copy, core, z, twin] = row


def pack_depth_kernel(place_ref, out_ref, up_ref, down_ref, *piece_refs):
    depth = len(piece_refs)
    width = out_ref.shape[1]
    span = up_ref.shape[1] // depth
    out_rows = out_ref[...].astype(BF)
    for bits, piece_ref in enumerate(piece_refs):
        start = pl.multiple_of((place_ref[1] ^ bits) * span, span)
        piece_ref[:, :width] = out_rows
        piece_ref[:, width : width + span] = up_ref[:, pl.ds(start, span)].astype(BF)
        piece_ref[:, width + span :] = down_ref[:, pl.ds(start, span)].astype(BF)


def pack_rest_kernel(place_ref, *refs):
    *piece_refs, packed_ref = refs
    copies, cores, twins, depth = packed_ref.shape[:4]
    half_w = packed_ref.shape[5] // 2
    half_h = half_w // 2
    width = 2 * half_w
    for bits, piece_ref in enumerate(piece_refs):
        z = place_ref[1] ^ bits
        for core in range(cores):
            for twin in range(twins):
                start = width + twin * 2 * half_h + core * half_h
                row = jnp.concatenate(
                    [
                        piece_ref[:, core * half_w : core * half_w + half_w],
                        piece_ref[:, start : start + half_h],
                        piece_ref[:, start + 2 * twins * half_h : start + 2 * twins * half_h + half_h],
                    ],
                    axis=1,
                )
                for copy in range(copies):
                    packed_ref[copy, core, twin, z] = row


def attend_kernel(place_ref, own_ref, other_ref, weight_ref, idc_ref, idr_ref, att_ref, kv_ref, send_ref, q_scr, k_scr, v_scr):
    rows = own_ref.shape[0]
    weight = weight_ref[...]
    low = low_lanes((rows, 128))
    first_twin = place_ref[2] == 0
    for side, x_ref in enumerate((own_ref, other_ref)):
        projected = jnp.dot(x_ref[...], weight, preferred_element_type=F32)
        projected = projected.astype(BF).astype(F32)
        vv = projected[:, 256:]
        span = slice(side * rows, (side + 1) * rows)
        v_scr[0, span] = jnp.where(low, vv, 1.0).astype(BF)
        v_scr[1, span] = jnp.where(low, 1.0, vv).astype(BF)
        cached = []
        for head in range(2):
            qk = projected[:, head * 128 : head * 128 + 128]
            keys = turned(qk)
            q_scr[head, span] = jnp.where(low, qk * (HD ** (-0.5)), 0.0).astype(BF)
            k_scr[head, span] = keys.astype(BF)
            cached.append(jnp.where(low, keys, vv if head else turned(vv)))
        both = jnp.where(first_twin, cached[0], cached[1]).astype(BF)
        if side == 0:
            kv_ref[...] = both
        else:
            send_ref[rows:] = both
    ids_row = idr_ref[...]
    step = 128
    low_step = low_lanes((step, 128))
    for start in range(0, 2 * rows, step):
        same = idc_ref[start : start + step, 0:1] == ids_row
        mixed = []
        for head in range(2):
            scores = lax.dot_general(q_scr[head, start : start + step], k_scr[head], NT, preferred_element_type=F32)
            scores = jnp.where(same, scores, -1e30)
            peak = jnp.max(scores, axis=1, keepdims=True)
            weights = jnp.exp(scores - peak).astype(BF)
            both = jnp.dot(weights, v_scr[head], preferred_element_type=F32)
            mixed.append(both / both[:, HD - head * HD : HD - head * HD + 1])
        packed = jnp.where(low_step, mixed[0], mixed[1]).astype(BF)
        if start < rows:
            att_ref[start : start + step] = packed
        else:
            send_ref[start - rows : start - rows + step] = packed


def join_kernel(place_ref, own_ref, got_ref, both_ref):
    rows = own_ref.shape[0]
    low = low_lanes(own_ref.shape)
    own = own_ref[...].astype(F32)
    got = got_ref[:rows].astype(F32)
    even = place_ref[0] == 0
    first = jnp.where(even, own, got)
    second = jnp.where(even, got, own)
    both_ref[:, :128] = jnp.where(low, first, turned(second)).astype(BF)
    both_ref[:, 128:] = jnp.where(low, turned(first), second).astype(BF)


def normed(values, gain, shift):
    center = values - jnp.mean(values, axis=-1, keepdims=True)
    spread = jnp.mean(center * center, axis=-1, keepdims=True)
    return center * lax.rsqrt(spread + EPS) * gain + shift


def gelu(value):
    return 0.5 * value * (1.0 + lax.erf(value * (2.0 ** (-0.5))))


def feed_kernel(place_ref, *refs):
    (*piece_refs, mine_ref, theirs_ref, x_ref, gain_ref, shift_ref, part_ref, keep_ref, att_scr, norm_scr, x_scr) = refs
    core = place_ref[0]
    depth = len(piece_refs)
    shards = part_ref.shape[0]
    part = place_ref[1] * (shards // depth) + place_ref[2]
    rows, width = x_ref.shape
    half_w = width // 2
    half_h = (mine_ref.shape[1] - half_w) // 2
    block = width // depth
    for bits, piece_ref in enumerate(piece_refs):
        source = place_ref[1] ^ bits
        lanes = pl.ds(pl.multiple_of(source % (depth // 2) * block, block), block)
        att_scr[source // (depth // 2), :, lanes] = piece_ref[...]
    moved = spread().astype(BF)
    for lane in range(0, width, 128):
        x_scr[:, lane : lane + 128] = jnp.dot(x_ref[:, lane : lane + 128], moved, preferred_element_type=F32)
    gain = spread_rows(gain_ref)
    shift = spread_rows(shift_ref)
    step = rows // 2
    share = rows // shards
    for begin in range(0, rows, step):
        span = slice(begin, begin + step)
        total = x_scr[span]
        for side, ref in ((core, mine_ref), (1 - core, theirs_ref)):
            total += lax.dot_general(att_scr[side, span], ref[:, :half_w], NT, preferred_element_type=F32)
        norm = normed(total, gain, shift).astype(BF)
        norm_scr[span] = norm
        result = jnp.zeros((step, width), F32)
        for ref in (mine_ref, theirs_ref):
            up = jnp.dot(norm, ref[:, half_w : half_w + half_h], preferred_element_type=F32)
            active = gelu(up).astype(BF)
            result += lax.dot_general(active, ref[:, half_w + half_h : half_w + 2 * half_h], NT, preferred_element_type=F32)
        for row in range(0, step, share):
            part_ref[(begin + row) // share] = result[row : row + share].astype(BF)
    keep_ref[...] = norm_scr[pl.ds(pl.multiple_of(part * share, share), share)]


def final_kernel(sums_ref, keep_ref, gain_ref, shift_ref, out_ref):
    total = keep_ref[...].astype(F32)
    for shard in range(sums_ref.shape[0]):
        total += sums_ref[shard].astype(F32)
    result = normed(total, spread_rows(gain_ref), spread_rows(shift_ref)).astype(BF)
    moved = spread().astype(BF)
    for lane in range(0, total.shape[1], 128):
        tile = lax.dot_general(result[:, lane : lane + 128], moved, NT, preferred_element_type=F32)
        out_ref[:, lane : lane + 128] = tile.astype(BF)


def cache_kernel(place_ref, own_ref, got_ref, keys_ref, values_ref):
    low = low_lanes(own_ref.shape)
    own = own_ref[...].astype(F32)
    got = got_ref[got_ref.shape[0] - own.shape[0] :].astype(F32)
    even = place_ref[0] == 0
    first = jnp.where(even, own, got)
    second = jnp.where(even, got, own)
    keys_ref[...] = jnp.where(low, first, turned(second)).astype(BF)
    values_ref[...] = jnp.where(low, turned(first), second).astype(BF)


def exchange(value, axes):
    return lax.all_to_all(value, axes, split_axis=0, concat_axis=0, tiled=True)


def swapped(value):
    return lax.ppermute(value, "cc", [(0, 1), (1, 0)])


def crossed(value, bits):
    return lax.ppermute(value, "zz", [(i, i ^ bits) for i in range(lax.axis_size("zz"))])


def body(hidden_in, request_ids, w_qkv, w_out, w_up, w_down, ln1_gain, ln1_shift, ln2_gain, ln2_shift):
    copies = lax.axis_size("yh") * lax.axis_size("xx")
    cores = lax.axis_size("cc")
    depth = lax.axis_size("zz")
    twins = lax.axis_size("yl")
    shards = depth * twins
    rows, width = hidden_in.shape
    part_rows = w_qkv.shape[0]
    hidden = w_up.shape[1] // shards
    columns = width // 2 + hidden
    place = jnp.stack([lax.axis_index("cc"), lax.axis_index("zz"), lax.axis_index("yl")]).astype(jnp.int32)

    def call(kernel, name, out_shape, in_specs, work=0, **more):
        more["cost_estimate"] = pl.CostEstimate(flops=work, bytes_accessed=2**20, transcendentals=0)
        flat = isinstance(out_shape, tuple)
        out_specs = (VM,) * len(out_shape) if flat else VM
        return pl.pallas_call(kernel, out_shape=out_shape, in_specs=in_specs, out_specs=out_specs, compiler_params=PARAMS, name=name, **more)

    def shape(*dims):
        return jax.ShapeDtypeStruct(dims, BF)

    packed_qkv = call(pack_qkv_kernel, "pack_qkv", shape(copies, cores, depth, twins, part_rows, 384), [VM])(w_qkv)
    served_qkv = exchange(packed_qkv.reshape(-1, part_rows, 384), GROUP + PART).reshape(width, 384)
    other_hidden = swapped(hidden_in)
    other_ids = swapped(request_ids)
    span = 2 * hidden * twins + width
    sent = call(pack_depth_kernel, "pack_depth", (shape(part_rows, span),) * depth, [SM] + [VM] * 3)(place, w_out, w_up, w_down)
    held = [sent[0]] + [crossed(sent[bits], bits) for bits in range(1, depth)]
    held, other_hidden, other_ids = lax.optimization_barrier((held, other_hidden, other_ids))
    packed_rest = call(pack_rest_kernel, "pack_rest", shape(copies, cores, twins, depth, part_rows, columns), [SM] + [VM] * depth)(place, *held)
    packed_rest, served_qkv = lax.optimization_barrier((packed_rest, served_qkv))
    served = exchange(packed_rest.reshape(-1, depth, part_rows, columns), GROUP + ("yl",)).reshape(width, columns)
    ids = jnp.concatenate([request_ids, other_ids])
    ids_col = jnp.broadcast_to(ids[:, None], (2 * rows, 128))
    ids_row = ids[None, :]

    att_own, kv_own, send = call(
        attend_kernel,
        "attend",
        (shape(rows, 128), shape(rows, 128), shape(2 * rows, 128)),
        [SM] + [VM] * 5,
        6 * 10**9,
        scratch_shapes=[pltpu.VMEM((2, 2 * rows, 128), BF)] * 3,
    )(place, hidden_in, other_hidden, served_qkv, ids_col, ids_row)
    got = swapped(send)
    pieces = [call(join_kernel, "join", shape(rows, 256), [SM, VM, VM])(place, att_own, got)]
    pieces += [crossed(pieces[0], bits) for bits in range(1, depth)]
    served, pieces = lax.optimization_barrier((served, pieces))
    served_other = swapped(served)

    keys_out, values_out = call(cache_kernel, "cache", (shape(rows, 128),) * 2, [SM, VM, VM])(place, kv_own, got)

    share = rows // shards
    tiles = (width // 128, 128)
    sums, keep = call(
        feed_kernel,
        "feed",
        (shape(shards, share, width), shape(share, width)),
        [SM] + [VM] * (depth + 5),
        6 * 10**9,
        scratch_shapes=[pltpu.VMEM((2, rows, width // 2), BF), pltpu.VMEM((rows, width), BF), pltpu.VMEM((rows, width), F32)],
    )(place, *pieces, served, served_other, hidden_in, ln1_gain.reshape(tiles), ln1_shift.reshape(tiles))
    sums_all = exchange(sums, PART)
    final = call(final_kernel, "final", shape(share, width), [VM] * 4)(sums_all, keep, ln2_gain.reshape(tiles), ln2_shift.reshape(tiles))
    return (final, keys_out, values_out)


def solution(mesh):
    fine = Mesh(mesh.devices.reshape(2, 4, 2, 4, 2), GROUP + PART)
    in_specs = (
        P(GROUP, None),
        P(GROUP),
        P(GROUP + PART, None),
        P(GROUP + PART, None),
        P(GROUP + PART, None),
        P(GROUP + PART, None),
        P(),
        P(),
        P(),
        P(),
    )
    out_specs = (P(GROUP + PART, None), P(GROUP, PART), P(GROUP, PART))
    return jax.shard_map(body, mesh=fine, in_specs=in_specs, out_specs=out_specs, check_vma=False)
```

time: 104 us -> 100 us (0.962)
  waiting for transfers between devices: 45.6 us -> 39.7 us
  Pallas kernels: 14.8 us -> 20.2 us
  starting transfers between devices: 34.5 us -> 32.5 us
    all_to_all x3, waiting for transfers between devices: 20.4 us -> 14 us  [exchange(): return lax.all_to_all(value, axes, split_axis=0, concat_axis=0, tiled=True)]
    pallas_call x4 -> x5, Pallas kernels: 7.24 us -> 12 us  [the longest x1 7.69 us: body(): call(attend_kernel, 'attend', (shape(rows, 128), shape(rows, 128), shape(...]
    ppermute x4, waiting for transfers between devices: 2.03 us -> 5.91 us  [swapped(): return lax.ppermute(value, 'cc', [(0, 1), (1, 0)])]
    ppermute x7 -> x6, waiting for transfers between devices: 23.2 us -> 19.8 us  [crossed(): lax.ppermute(value, 'zz', [(i, i ^ bits) for i in range(lax.axis_size('zz...]
    ppermute x7 -> x6, starting transfers between devices: 10.2 us -> 7.85 us  [crossed(): lax.ppermute(value, 'zz', [(i, i ^ bits) for i in range(lax.axis_size('zz...]
    all_to_all x3, starting transfers between devices: 19 us -> 20.2 us  [exchange(): return lax.all_to_all(value, axes, split_axis=0, concat_axis=0, tiled=True)]
    unnamed x27 -> x31, local copies, waits for them, and re-layouts: 7.15 us -> 6.26 us
  transfers between devices with their start and end apart: 14 -> 13, of which waited for: 9 -> 9; matrix products, arithmetic and copies ran while one was open for 0% -> 0% of each run, Pallas kernels for 8% -> 13%
where the time goes in v3:
time: 100 us; the launch traced here: 99.7 us
  waiting for transfers between devices  39.7 us (40%)
  starting transfers between devices  32.5 us (32%)
  Pallas kernels  20.2 us (20%)
  local copies, waits for them, and re-layouts  6.46 us (6%)
    all_to_all x3, starting transfers between devices, exchange(): return lax.all_to_all(value, axes, split_axis=0, concat_axis=0, tiled=True)  20.2 us
    ppermute x6, waiting for transfers between devices, crossed(): lax.ppermute(value, 'zz', [(i, i ^ bits) for i in range(lax.axis_size('zz...  19.8 us
    all_to_all x3, waiting for transfers between devices, exchange(): return lax.all_to_all(value, axes, split_axis=0, concat_axis=0, tiled=True)  14 us
    ppermute x6, starting transfers between devices, crossed(): lax.ppermute(value, 'zz', [(i, i ^ bits) for i in range(lax.axis_size('zz...  7.85 us
    pallas_call x1, Pallas kernels, body(): call(attend_kernel, 'attend', (shape(rows, 128), shape(rows, 128), shape(...  7.69 us
    unnamed x31, local copies, waits for them, and re-layouts  6.26 us
    ppermute x4, waiting for transfers between devices, swapped(): return lax.ppermute(value, 'cc', [(0, 1), (1, 0)])  5.91 us
    pallas_call x1, Pallas kernels, body(): call(feed_kernel, 'feed', (shape(shards, share, width), shape(share, widt...  5.55 us
  transfers between devices with their start and end apart: 13, of which 9 were waited for; matrix products, arithmetic and copies ran while one was open for 0% of the time, Pallas kernels for 13%

profile of v3, /device:TPU:1, one launch (start us, length us, event | category | flops | bytes accessed | tf_op | source)
XLA Modules:
  0.0 99.7 jit_solution(18122848255344259738)
XLA Ops:
  0.7 1.5 %collective-permute-start.3 = (bf16[512,1024]{1,0:T(8,128)(2,1)}, bf16[512,1024]{1,0:T(8,128)(2,1)S(1)}, u32[]{:S(2)}, u32[]{:S(2)}) collective-permute-start(bf16[512,1024]{1,0:T(8,128)(2,1)} %refs_6_.1), channel_id=1, source_target_pairs={{0,8},{8,0},{1,9},{9,1},{2,10},{10,2},{3,11},{11,3},{4,12},{12,4},... | collective-permute-start | bytes 3145736 | tf_op jit(solution)/shard_map/ppermute | solution.py:238
  2.2 0.9 copy-done.2
  3.1 1.0 %pack_qkv.1 = bf16[8,2,4,2,8,384]{5,4,3,2,1,0:T(8,128)(2,1)} custom-call(f32[8,3072]{1,0:T(8,128)S(1)} %copy-done.2), custom_call_target="tpu_custom_call" | custom-call | bytes 1048576 | tf_op jit(solution)/shard_map/pack_qkv/pallas_call | solution.py:266
  4.1 10.2 %all-to-all-start = ((bf16[128,8,384]{2,1,0:T(8,128)(2,1)}), bf16[128,8,384]{2,1,0:T(8,128)(2,1)S(1)}, u32[]{:S(2)}, u32[]{:S(2)}) async-start(bf16[128,8,384]{2,1,0:T(8,128)(2,1)} %bitcast.3), calls=%async_computation | async-start | bytes 1572864 | tf_op jit(solution)/shard_map/all_to_all | solution.py:234
  14.4 0.6 pack_depth.1
  14.9 1.6 %collective-permute-start = (bf16[8,3072]{1,0:T(8,128)(2,1)S(1)}, bf16[8,3072]{1,0:T(8,128)(2,1)S(1)}, u32[]{:S(2)}, u32[]{:S(2)}) collective-permute-start(bf16[8,3072]{1,0:T(8,128)(2,1)S(1)} %get-tuple-element.28), channel_id=1, source_target_pairs={{0,2},{2,0},{4,6},{6,4},{1,3},{3,1},{5,7},{7,5},{8,10},{10,8},{12,... | collective-permute-start | bytes 147464 | tf_op jit(solution)/shard_map/ppermute | solution.py:242
  16.5 2.9 %collective-permute-start.1 = (bf16[8,3072]{1,0:T(8,128)(2,1)S(1)}, bf16[8,3072]{1,0:T(8,128)(2,1)S(1)}, u32[]{:S(2)}, u32[]{:S(2)}) collective-permute-start(bf16[8,3072]{1,0:T(8,128)(2,1)S(1)} %get-tuple-element.29), channel_id=1, source_target_pairs={{0,4},{2,6},{4,0},{6,2},{1,5},{3,7},{5,1},{7,3},{8,12},{10,14},{12... | collective-permute-start | bytes 147464 | tf_op jit(solution)/shard_map/ppermute | solution.py:242
  19.5 1.3 %collective-permute-start.4 = (s32[512]{0:T(512)S(1)}, s32[512]{0:T(512)S(1)}, u32[]{:S(2)}, u32[]{:S(2)}) collective-permute-start(s32[512]{0:T(512)S(1)} %copy-done.14), channel_id=1, source_target_pairs={{0,8},{8,0},{1,9},{9,1},{2,10},{10,2},{3,11},{11,3},{4,12},{12,4},... | collective-permute-start | bytes 6152 | tf_op jit(solution)/shard_map/ppermute | solution.py:238
  20.8 0.8 collective-permute-done.4
  21.6 7.2 %collective-permute-done.1.refs_2_ = bf16[8,3072]{1,0:T(8,128)(2,1)S(1)} collective-permute-done((bf16[8,3072]{1,0:T(8,128)(2,1)S(1)}, bf16[8,3072]{1,0:T(8,128)(2,1)S(1)}, u32[]{:S(2)}, u32[]{:S(2)}) %collective-permute-start.1) | collective-permute-done | bytes 49184 | tf_op jit(solution)/shard_map/ppermute | solution.py:242
  28.8 1.0 %collective-permute-done.2.refs_3_ = bf16[8,3072]{1,0:T(8,128)(2,1)S(1)} collective-permute-done((bf16[8,3072]{1,0:T(8,128)(2,1)S(1)}, bf16[8,3072]{1,0:T(8,128)(2,1)S(1)}, u32[]{:S(2)}, u32[]{:S(2)}) %collective-permute-start.2) | collective-permute-done | bytes 49184 | tf_op jit(solution)/shard_map/ppermute | solution.py:242
  29.8 2.0 %pack_rest.1 = bf16[8,2,2,4,8,1024]{5,4,3,2,1,0:T(8,128)(2,1)} custom-call(s32[3]{0:T(128)S(1)} %pad_add_fusion.place_ref, bf16[8,3072]{1,0:T(8,128)(2,1)S(1)} %get-tuple-element.31.refs_0_, bf16[8,3072]{1,0:T(8,128)(2,1)S(1)} %collective-permute-done.refs_1_, bf16[8,3072]{1,0:T(8,128)(2,1)S(1)} %collective-permute-done.1.refs_2_, ...), custom_call_target="tpu_custom_call" | custom-call | bytes 1048576 | tf_op jit(solution)/shard_map/pack_rest/pallas_call | solution.py:274
  31.9 6.3 %all-to-all-start.1 = ((bf16[32,4,8,1024]{3,2,1,0:T(8,128)(2,1)}), bf16[32,4,8,1024]{3,2,1,0:T(8,128)(2,1)S(1)}, u32[]{:S(2)}, u32[]{:S(2)}) async-start(bf16[32,4,8,1024]{3,2,1,0:T(8,128)(2,1)} %bitcast.5), calls=%async_computation.1 | async-start | bytes 4194304 | tf_op jit(solution)/shard_map/all_to_all | solution.py:234
  38.4 1.2 %copy-done.6 = bf16[512,1024]{1,0:T(8,128)(2,1)S(1)} copy-done((bf16[512,1024]{1,0:T(8,128)(2,1)S(1)}, bf16[512,1024]{1,0:T(8,128)(2,1)}, u32[]{:S(2)}) %copy-start.6) | copy-done | bytes 1048600
  39.7 1.2 %copy-done.9 = bf16[512,1024]{1,0:T(8,128)(2,1)S(1)} copy-done((bf16[512,1024]{1,0:T(8,128)(2,1)S(1)}, bf16[512,1024]{1,0:T(8,128)(2,1)}, u32[]{:S(2)}) %copy-start.9) | copy-done | bytes 1048600
  40.9 7.7 %attend.1 = (bf16[512,128]{1,0:T(8,128)(2,1)S(1)}, bf16[512,128]{1,0:T(8,128)(2,1)S(1)}, bf16[1024,128]{1,0:T(8,128)(2,1)S(1)}) custom-call(s32[3]{0:T(128)S(1)} %pad_add_fusion.place_ref, bf16[512,1024]{1,0:T(8,128)(2,1)S(1)} %copy-done.6, bf16[512,1024]{1,0:T(8,128)(2,1)S(1)} %copy-done.9, bf16[1024,384]{1,0:T(8,128)(2,1)S(1)} %bitcast.14, ...), custom_call_target="tpu_custom_call" | custom-call | flops 6000000000 | bytes 1048576 | tf_op jit(solution)/shard_map/attend/pallas_call | solution.py:281
  48.9 1.3 %collective-permute-done.5.got_ref = bf16[1024,128]{1,0:T(8,128)(2,1)S(1)} collective-permute-done((bf16[1024,128]{1,0:T(8,128)(2,1)S(1)}, bf16[1024,128]{1,0:T(8,128)(2,1)S(1)}, u32[]{:S(2)}, u32[]{:S(2)}) %collective-permute-start.5) | collective-permute-done | bytes 262176 | tf_op jit(solution)/shard_map/ppermute | solution.py:238
  50.2 0.7 join.1.refs_0_
  50.9 0.7 collective-permute-start.8
  51.6 1.7 %collective-permute-start.7 = (bf16[512,256]{1,0:T(8,128)(2,1)S(1)}, bf16[512,256]{1,0:T(8,128)(2,1)S(1)}, u32[]{:S(2)}, u32[]{:S(2)}) collective-permute-start(bf16[512,256]{1,0:T(8,128)(2,1)S(1)} %join.1.refs_0_), channel_id=1, source_target_pairs={{0,4},{2,6},{4,0},{6,2},{1,5},{3,7},{5,1},{7,3},{8,12},{10,14},{12... | collective-permute-start | bytes 786440 | tf_op jit(solution)/shard_map/ppermute | solution.py:242
  53.3 0.9 collective-permute-start.6
  54.2 11.2 %collective-permute-done.8.refs_3_ = bf16[512,256]{1,0:T(8,128)(2,1)S(1)} collective-permute-done((bf16[512,256]{1,0:T(8,128)(2,1)S(1)}, bf16[512,256]{1,0:T(8,128)(2,1)S(1)}, u32[]{:S(2)}, u32[]{:S(2)}) %collective-permute-start.8) | collective-permute-done | bytes 262176 | tf_op jit(solution)/shard_map/ppermute | solution.py:242
  65.8 0.7 copy-done.10
  66.6 1.3 %collective-permute-start.9 = (bf16[1024,1024]{1,0:T(8,128)(2,1)S(1)}, bf16[1024,1024]{1,0:T(8,128)(2,1)S(1)}, u32[]{:S(2)}, u32[]{:S(2)}) collective-permute-start(bf16[1024,1024]{1,0:T(8,128)(2,1)S(1)} %bitcast.12), channel_id=1, source_target_pairs={{0,8},{8,0},{1,9},{9,1},{2,10},{10,2},{3,11},{11,3},{4,12},{12,4},... | collective-permute-start | bytes 6291464 | tf_op jit(solution)/shard_map/ppermute | solution.py:238
  67.9 3.8 %collective-permute-done.9.refs_5_ = bf16[1024,1024]{1,0:T(8,128)(2,1)S(1)} collective-permute-done((bf16[1024,1024]{1,0:T(8,128)(2,1)S(1)}, bf16[1024,1024]{1,0:T(8,128)(2,1)S(1)}, u32[]{:S(2)}, u32[]{:S(2)}) %collective-permute-start.9) | collective-permute-done | bytes 2097184 | tf_op jit(solution)/shard_map/ppermute | solution.py:238
  71.7 1.2 %copy-done.7 = bf16[512,1024]{1,0:T(8,128)(2,1)S(1)} copy-done((bf16[512,1024]{1,0:T(8,128)(2,1)S(1)}, bf16[512,1024]{1,0:T(8,128)(2,1)}, u32[]{:S(2)}) %copy-start.7) | copy-done | bytes 1048600
  72.9 0.9 copy-done.11
  73.8 5.6 %feed.1 = (bf16[8,64,1024]{2,1,0:T(8,128)(2,1)}, bf16[64,1024]{1,0:T(8,128)(2,1)S(1)}) custom-call(s32[3]{0:T(128)S(1)} %pad_add_fusion.place_ref, bf16[512,256]{1,0:T(8,128)(2,1)S(1)} %join.1.refs_0_, bf16[512,256]{1,0:T(8,128)(2,1)S(1)} %copy-done.11, bf16[512,256]{1,0:T(8,128)(2,1)S(1)} %collective-permute-done.7.refs_2_, ...), custom_call_target="tpu_custom_call" | custom-call | flops 6000000000 | bytes 1048576 | tf_op jit(solution)/shard_map/feed/pallas_call | solution.py:299
  79.4 3.7 %all-to-all-start.2 = ((bf16[8,64,1024]{2,1,0:T(8,128)(2,1)}), bf16[8,64,1024]{2,1,0:T(8,128)(2,1)S(1)}, u32[]{:S(2)}, u32[]{:S(2)}) async-start(bf16[8,64,1024]{2,1,0:T(8,128)(2,1)} %get-tuple-element.46), calls=%async_computation.2 | async-start | bytes 2097152 | tf_op jit(solution)/shard_map/all_to_all | solution.py:234
  83.1 1.4 %cache.1 = (bf16[512,128]{1,0:T(8,128)(2,1)}, bf16[512,128]{1,0:T(8,128)(2,1)}) custom-call(s32[3]{0:T(128)S(1)} %pad_add_fusion.place_ref, bf16[512,128]{1,0:T(8,128)(2,1)S(1)} %get-tuple-element.48.own_ref, bf16[1024,128]{1,0:T(8,128)(2,1)S(1)} %collective-permute-done.5.got_ref), custom_call_target="tpu_custom_call" | custom-call | bytes 1048576 | tf_op jit(solution)/shard_map/cache/pallas_call | solution.py:295
  84.5 14.0 %all-to-all-done.2.sums_ref = bf16[8,64,1024]{2,1,0:T(8,128)(2,1)S(1)} async-done(((bf16[8,64,1024]{2,1,0:T(8,128)(2,1)}), bf16[8,64,1024]{2,1,0:T(8,128)(2,1)S(1)}, u32[]{:S(2)}, u32[]{:S(2)}) %all-to-all-start.2) | async-done | bytes 1048608 | tf_op jit(solution)/shard_map/all_to_all | solution.py:234
  98.4 1.3 %final.1 = bf16[64,1024]{1,0:T(8,128)(2,1)} custom-call(bf16[8,64,1024]{2,1,0:T(8,128)(2,1)S(1)} %all-to-all-done.2.sums_ref, bf16[64,1024]{1,0:T(8,128)(2,1)S(1)} %get-tuple-element.47.keep_ref, f32[8,128]{1,0:T(8,128)S(1)} %bitcast.15, f32[8,128]{1,0:T(8,128)S(1)} %bitcast.16), custom_call_target="tpu_custom_call" | custom-call | bytes 1048576 | tf_op jit(solution)/shard_map/final/pallas_call | solution.py:308
  (37 shorter events, 1.0 us)
Async XLA Ops:
  0.6 13.7 %copy-start.1 = (f32[8,4096]{1,0:T(8,128)S(1)}, f32[8,4096]{1,0:T(8,128)}, u32[]{:S(2)}) copy-start(f32[8,4096]{1,0:T(8,128)} %down_ref.1) | copy-start | bytes 393220
  0.6 13.7 %copy-start = (f32[8,4096]{1,0:T(8,128)S(1)}, f32[8,4096]{1,0:T(8,128)}, u32[]{:S(2)}) copy-start(f32[8,4096]{1,0:T(8,128)} %up_ref.1) | copy-start | bytes 393220
  0.7 29.2 %collective-permute-start.3 = (bf16[512,1024]{1,0:T(8,128)(2,1)}, bf16[512,1024]{1,0:T(8,128)(2,1)S(1)}, u32[]{:S(2)}, u32[]{:S(2)}) collective-permute-start(bf16[512,1024]{1,0:T(8,128)(2,1)} %refs_6_.1), channel_id=1, source_target_pairs={{0,8},{8,0},{1,9},{9,1},{2,10},{10,2},{3,11},{11,3},{4,12},{12,4},... | collective-permute-start | bytes 3145736 | tf_op jit(solution)/shard_map/ppermute | solution.py:238
  2.2 0.9 copy-start.2
  3.0 11.3 %copy-start.3 = (f32[8,1024]{1,0:T(8,128)S(1)}, f32[8,1024]{1,0:T(8,128)}, u32[]{:S(2)}) copy-start(f32[8,1024]{1,0:T(8,128)} %out_ref.1) | copy-start | bytes 98308
  3.0 16.4 %copy-start.14 = (s32[512]{0:T(512)S(1)}, s32[512]{0:T(512)}, u32[]{:S(2)}) copy-start(s32[512]{0:T(512)} %param.11) | copy-start | bytes 6148
  4.1 27.8 %all-to-all-start = ((bf16[128,8,384]{2,1,0:T(8,128)(2,1)}), bf16[128,8,384]{2,1,0:T(8,128)(2,1)S(1)}, u32[]{:S(2)}, u32[]{:S(2)}) async-start(bf16[128,8,384]{2,1,0:T(8,128)(2,1)} %bitcast.3), calls=%async_computation | async-start | bytes 1572864 | tf_op jit(solution)/shard_map/all_to_all | solution.py:234
  14.9 6.7 %collective-permute-start = (bf16[8,3072]{1,0:T(8,128)(2,1)S(1)}, bf16[8,3072]{1,0:T(8,128)(2,1)S(1)}, u32[]{:S(2)}, u32[]{:S(2)}) collective-permute-start(bf16[8,3072]{1,0:T(8,128)(2,1)S(1)} %get-tuple-element.28), channel_id=1, source_target_pairs={{0,2},{2,0},{4,6},{6,4},{1,3},{3,1},{5,7},{7,5},{8,10},{10,8},{12,... | collective-permute-start | bytes 147464 | tf_op jit(solution)/shard_map/ppermute | solution.py:242
  16.5 12.3 %collective-permute-start.1 = (bf16[8,3072]{1,0:T(8,128)(2,1)S(1)}, bf16[8,3072]{1,0:T(8,128)(2,1)S(1)}, u32[]{:S(2)}, u32[]{:S(2)}) collective-permute-start(bf16[8,3072]{1,0:T(8,128)(2,1)S(1)} %get-tuple-element.29), channel_id=1, source_target_pairs={{0,4},{2,6},{4,0},{6,2},{1,5},{3,7},{5,1},{7,3},{8,12},{10,14},{12... | collective-permute-start | bytes 147464 | tf_op jit(solution)/shard_map/ppermute | solution.py:242
  19.5 10.4 %collective-permute-start.2 = (bf16[8,3072]{1,0:T(8,128)(2,1)S(1)}, bf16[8,3072]{1,0:T(8,128)(2,1)S(1)}, u32[]{:S(2)}, u32[]{:S(2)}) collective-permute-start(bf16[8,3072]{1,0:T(8,128)(2,1)S(1)} %get-tuple-element.30), channel_id=1, source_target_pairs={{0,6},{2,4},{4,2},{6,0},{1,7},{3,5},{5,3},{7,1},{8,14},{10,12},{12... | collective-permute-start | bytes 147464 | tf_op jit(solution)/shard_map/ppermute | solution.py:242
  19.5 2.1 %collective-permute-start.4 = (s32[512]{0:T(512)S(1)}, s32[512]{0:T(512)S(1)}, u32[]{:S(2)}, u32[]{:S(2)}) collective-permute-start(s32[512]{0:T(512)S(1)} %copy-done.14), channel_id=1, source_target_pairs={{0,8},{8,0},{1,9},{9,1},{2,10},{10,2},{3,11},{11,3},{4,12},{12,4},... | collective-permute-start | bytes 6152 | tf_op jit(solution)/shard_map/ppermute | solution.py:238
  29.8 2.0 %copy-start.8 = (bf16[512,1024]{1,0:T(8,128)(2,1)}, bf16[512,1024]{1,0:T(8,128)(2,1)S(1)}, u32[]{:S(2)}) copy-start(bf16[512,1024]{1,0:T(8,128)(2,1)S(1)} %collective-permute-done.3.other_ref) | copy-start | bytes 3145732
  31.9 34.7 %all-to-all-start.1 = ((bf16[32,4,8,1024]{3,2,1,0:T(8,128)(2,1)}), bf16[32,4,8,1024]{3,2,1,0:T(8,128)(2,1)S(1)}, u32[]{:S(2)}, u32[]{:S(2)}) async-start(bf16[32,4,8,1024]{3,2,1,0:T(8,128)(2,1)} %bitcast.5), calls=%async_computation.1 | async-start | bytes 4194304 | tf_op jit(solution)/shard_map/all_to_all | solution.py:234
  38.4 1.2 %copy-start.6 = (bf16[512,1024]{1,0:T(8,128)(2,1)S(1)}, bf16[512,1024]{1,0:T(8,128)(2,1)}, u32[]{:S(2)}) copy-start(bf16[512,1024]{1,0:T(8,128)(2,1)} %refs_6_.1) | copy-start | bytes 3145732
  39.7 1.2 %copy-start.9 = (bf16[512,1024]{1,0:T(8,128)(2,1)S(1)}, bf16[512,1024]{1,0:T(8,128)(2,1)}, u32[]{:S(2)}) copy-start(bf16[512,1024]{1,0:T(8,128)(2,1)} %copy-done.8) | copy-start | bytes 3145732
  40.9 30.8 %copy-start.12 = (f32[1024]{0:T(1024)S(1)}, f32[1024]{0:T(1024)}, u32[]{:S(2)}) copy-start(f32[1024]{0:T(1024)} %param.16) | copy-start | bytes 12292
  40.9 30.8 %copy-start.13 = (f32[1024]{0:T(1024)S(1)}, f32[1024]{0:T(1024)}, u32[]{:S(2)}) copy-start(f32[1024]{0:T(1024)} %param.17) | copy-start | bytes 12292
  48.6 1.6 %collective-permute-start.5 = (bf16[1024,128]{1,0:T(8,128)(2,1)S(1)}, bf16[1024,128]{1,0:T(8,128)(2,1)S(1)}, u32[]{:S(2)}, u32[]{:S(2)}) collective-permute-start(bf16[1024,128]{1,0:T(8,128)(2,1)S(1)} %get-tuple-element.40), channel_id=1, source_target_pairs={{0,8},{8,0},{1,9},{9,1},{2,10},{10,2},{3,11},{11,3},{4,12},{12,4},... | collective-permute-start | bytes 786440 | tf_op jit(solution)/shard_map/ppermute | solution.py:238
  50.9 14.6 %collective-permute-start.8 = (bf16[512,256]{1,0:T(8,128)(2,1)S(1)}, bf16[512,256]{1,0:T(8,128)(2,1)S(1)}, u32[]{:S(2)}, u32[]{:S(2)}) collective-permute-start(bf16[512,256]{1,0:T(8,128)(2,1)S(1)} %join.1.refs_0_), channel_id=1, source_target_pairs={{0,6},{2,4},{4,2},{6,0},{1,7},{3,5},{5,3},{7,1},{8,14},{10,12},{12... | collective-permute-start | bytes 786440 | tf_op jit(solution)/shard_map/ppermute | solution.py:242
  51.6 13.9 %collective-permute-start.7 = (bf16[512,256]{1,0:T(8,128)(2,1)S(1)}, bf16[512,256]{1,0:T(8,128)(2,1)S(1)}, u32[]{:S(2)}, u32[]{:S(2)}) collective-permute-start(bf16[512,256]{1,0:T(8,128)(2,1)S(1)} %join.1.refs_0_), channel_id=1, source_target_pairs={{0,4},{2,6},{4,0},{6,2},{1,5},{3,7},{5,1},{7,3},{8,12},{10,14},{12... | collective-permute-start | bytes 786440 | tf_op jit(solution)/shard_map/ppermute | solution.py:242
  53.3 12.5 %collective-permute-start.6 = (bf16[512,256]{1,0:T(8,128)(2,1)S(1)}, bf16[512,256]{1,0:T(8,128)(2,1)S(1)}, u32[]{:S(2)}, u32[]{:S(2)}) collective-permute-start(bf16[512,256]{1,0:T(8,128)(2,1)S(1)} %join.1.refs_0_), channel_id=1, source_target_pairs={{0,2},{2,0},{4,6},{6,4},{1,3},{3,1},{5,7},{7,5},{8,10},{10,8},{12,... | collective-permute-start | bytes 786440 | tf_op jit(solution)/shard_map/ppermute | solution.py:242
  65.8 0.7 copy-start.10
  66.6 5.1 %collective-permute-start.9 = (bf16[1024,1024]{1,0:T(8,128)(2,1)S(1)}, bf16[1024,1024]{1,0:T(8,128)(2,1)S(1)}, u32[]{:S(2)}, u32[]{:S(2)}) collective-permute-start(bf16[1024,1024]{1,0:T(8,128)(2,1)S(1)} %bitcast.12), channel_id=1, source_target_pairs={{0,8},{8,0},{1,9},{9,1},{2,10},{10,2},{3,11},{11,3},{4,12},{12,4},... | collective-permute-start | bytes 6291464 | tf_op jit(solution)/shard_map/ppermute | solution.py:238
  71.7 1.2 %copy-start.7 = (bf16[512,1024]{1,0:T(8,128)(2,1)S(1)}, bf16[512,1024]{1,0:T(8,128)(2,1)}, u32[]{:S(2)}) copy-start(bf16[512,1024]{1,0:T(8,128)(2,1)} %refs_6_.1) | copy-start | bytes 3145732
  72.9 0.9 copy-start.11
  79.4 19.0 %copy-start.4 = (f32[1024]{0:T(1024)S(1)}, f32[1024]{0:T(1024)}, u32[]{:S(2)}) copy-start(f32[1024]{0:T(1024)} %param.18) | copy-start | bytes 12292
  79.4 19.0 %copy-start.5 = (f32[1024]{0:T(1024)S(1)}, f32[1024]{0:T(1024)}, u32[]{:S(2)}) copy-start(f32[1024]{0:T(1024)} %param.19) | copy-start | bytes 12292
  79.4 19.0 %all-to-all-start.2 = ((bf16[8,64,1024]{2,1,0:T(8,128)(2,1)}), bf16[8,64,1024]{2,1,0:T(8,128)(2,1)S(1)}, u32[]{:S(2)}, u32[]{:S(2)}) async-start(bf16[8,64,1024]{2,1,0:T(8,128)(2,1)} %get-tuple-element.46), calls=%async_computation.2 | async-start | bytes 2097152 | tf_op jit(solution)/shard_map/all_to_all | solution.py:234

commit v4 on v3

v4 whole, which is shorter than its diff:
```python
import jax
import jax.numpy as jnp
from jax import lax
from jax.experimental import pallas as pl
from jax.experimental.pallas import tpu as pltpu
from jax.sharding import Mesh
from jax.sharding import PartitionSpec as P

HD = 64
BF = jnp.bfloat16
F32 = jnp.float32
EPS = 1e-05
NT = (((1,), (1,)), ((), ()))
GROUP = ("yh", "xx", "cc")
PART = ("zz", "yl")
VM = pl.BlockSpec(memory_space=pltpu.VMEM)
SM = pl.BlockSpec(memory_space=pltpu.SMEM)
HB = pl.BlockSpec(memory_space=pltpu.HBM)
CORE, DEEP, TWIN = range(3)


def low_lanes(shape):
    return lax.broadcasted_iota(jnp.int32, shape, len(shape) - 1) < HD


def turned(value):
    return pltpu.roll(value, HD, len(value.shape) - 1)


def spread():
    rows = lax.broadcasted_iota(jnp.int32, (128, 128), 0)
    cols = lax.broadcasted_iota(jnp.int32, (128, 128), 1)
    inner = cols % 64
    source = cols - inner + inner % 32 // 8 * 16 + inner // 32 * 8 + inner % 8
    return jnp.where(rows == source, 1.0, 0.0).astype(BF)


def rearranged(value, back):
    moved = spread()
    tiles = []
    for lane in range(0, value.shape[1], 128):
        tile = value[:, lane : lane + 128]
        if back:
            tiles.append(lax.dot_general(tile, moved, NT, preferred_element_type=F32).astype(BF))
        else:
            tiles.append(jnp.dot(tile, moved, preferred_element_type=F32).astype(BF))
    return jnp.concatenate(tiles, axis=1)


def pack_first_kernel(qkv_ref, out_ref, packed_ref):
    rows = qkv_ref.shape[0]
    width = qkv_ref.shape[1] // 3
    copies, cores, depth, twins = packed_ref.shape[:4]
    low = low_lanes((rows, 128))

    def tile(kind, number):
        start = kind * width + number * 128
        return qkv_ref[:, start : start + 128]

    for core in range(cores):
        for z in range(depth):
            start = core * (width // cores) + z * 128
            parts = [out_ref[:, start : start + 128]]
            for twin in range(2):
                q_tile, k_tile = tile(0, 2 * z + twin), tile(1, 2 * z + twin)
                if core == 0:
                    parts.append(jnp.where(low, q_tile, turned(k_tile)))
                else:
                    parts.append(jnp.where(low, turned(q_tile), k_tile))
            one, two = tile(2, 2 * z), tile(2, 2 * z + 1)
            if core == 0:
                parts.append(jnp.where(low, one, turned(two)))
            else:
                parts.append(jnp.where(low, turned(one), two))
            row = jnp.concatenate(parts, axis=1).astype(BF)
            for copy in range(copies):
                for twin in range(twins):
                    packed_ref[copy, core, z, twin] = row


def pack_depth_kernel(place_ref, up_ref, down_ref, *piece_refs):
    depth = len(piece_refs)
    span = up_ref.shape[1] // depth
    for bits, piece_ref in enumerate(piece_refs):
        start = pl.multiple_of((place_ref[DEEP] ^ bits) * span, span)
        piece_ref[:, :span] = up_ref[:, pl.ds(start, span)].astype(BF)
        piece_ref[:, span:] = down_ref[:, pl.ds(start, span)].astype(BF)


def pack_rest_kernel(place_ref, *refs):
    *piece_refs, packed_ref = refs
    copies, cores, twins = packed_ref.shape[:3]
    half_h = packed_ref.shape[5] // 2
    for bits, piece_ref in enumerate(piece_refs):
        z = place_ref[DEEP] ^ bits
        span = piece_ref.shape[1] // 2
        for core in range(cores):
            start = core * half_h
            row = jnp.concatenate([piece_ref[:, start : start + half_h], piece_ref[:, span + start : span + start + half_h]], axis=1)
            for copy in range(copies):
                for twin in range(twins):
                    packed_ref[copy, core, twin, z] = row


def take_kernel(served_ref, part_ref):
    part_ref[...] = served_ref[...]


def assemble_kernel(place_ref, *refs):
    *part_refs, whole_ref = refs
    for bits, part_ref in enumerate(part_refs):
        lanes = pl.ds(pl.multiple_of((place_ref[DEEP] ^ bits) * 128, 128), 128)
        whole_ref[:, lanes] = part_ref[...]


def attend_kernel(place_ref, own_hbm, other_hbm, weight_ref, own_ids_ref, other_ids_ref, att_ref, kv_ref, send_ref, x_scr, q_scr, k_scr, v_scr, id_scr, sems):
    copies = [pltpu.make_async_copy(ref, x_scr.at[side], sems.at[side]) for side, ref in enumerate((own_hbm, other_hbm))]
    for copy in copies:
        copy.start()
    rows = own_hbm.shape[0]
    step = 128
    tiles = rows // step
    share = att_ref.shape[0] // tiles
    twin = place_ref[TWIN]
    weight = weight_ref[:, 128:]
    low = low_lanes((rows, 128))
    for side, ids_ref in enumerate((own_ids_ref, other_ids_ref)):
        id_scr[side * tiles : (side + 1) * tiles] = ids_ref[...].astype(F32)
        copies[side].wait()
        projected = jnp.dot(x_scr[side], weight, preferred_element_type=F32)
        projected = projected.astype(BF).astype(F32)
        vv = projected[:, 256:]
        span = slice(side * rows, (side + 1) * rows)
        v_scr[0, span] = jnp.where(low, vv, 1.0).astype(BF)
        v_scr[1, span] = jnp.where(low, 1.0, vv).astype(BF)
        cached = []
        for head in range(2):
            qk = projected[:, head * 128 : head * 128 + 128]
            keys = turned(qk)
            q_scr[head, span] = jnp.where(low, qk * (HD ** (-0.5)), 0.0).astype(BF)
            k_scr[head, span] = keys.astype(BF)
            cached.append(jnp.where(low, keys, vv if head else turned(vv)))
        both = jnp.where(twin == 0, cached[0], cached[1]).astype(BF)
        if side == 0:
            kv_ref[...] = both
        else:
            send_ref[att_ref.shape[0] :] = both
    ids_row = jnp.concatenate([id_scr[i : i + 1] for i in range(2 * tiles)], axis=1)
    low_step = low_lanes((step, 128))
    row_at = lax.broadcasted_iota(jnp.int32, (step, 128), 0)
    lane_at = lax.broadcasted_iota(jnp.int32, (step, 128), 1)
    picked = lane_at == twin * share + row_at % share
    for side in range(2):
        for pair in range(tiles // 2):
            one = side * tiles + 2 * pair
            ids_two = jnp.where(row_at < share, id_scr[one : one + 1], id_scr[one + 1 : one + 2])
            ids_col = jnp.sum(jnp.where(picked, ids_two, 0.0), axis=1, keepdims=True)
            same = ids_col == ids_row
            spans = [pl.ds(pl.multiple_of((one + i) * step + twin * share, share), share) for i in range(2)]
            mixed = []
            for head in range(2):
                queries = jnp.concatenate([q_scr[head, span] for span in spans], axis=0)
                scores = lax.dot_general(queries, k_scr[head], NT, preferred_element_type=F32)
                scores = jnp.where(same, scores, -1e30)
                peak = jnp.max(scores, axis=1, keepdims=True)
                weights = jnp.exp(scores - peak).astype(BF)
                both = jnp.dot(weights, v_scr[head], preferred_element_type=F32)
                mixed.append(both / both[:, HD - head * HD : HD - head * HD + 1])
            packed = jnp.where(low_step, mixed[0], mixed[1]).astype(BF)
            ref = send_ref if side else att_ref
            ref[pair * step : (pair + 1) * step] = packed


def join_kernel(place_ref, own_ref, got_ref, both_ref):
    rows = own_ref.shape[0]
    low = low_lanes(own_ref.shape)
    own = own_ref[...].astype(F32)
    got = got_ref[:rows].astype(F32)
    even = place_ref[CORE] == 0
    first = jnp.where(even, own, got)
    second = jnp.where(even, got, own)
    both_ref[:, :128] = jnp.where(low, first, turned(second)).astype(BF)
    both_ref[:, 128:] = jnp.where(low, turned(first), second).astype(BF)


def normed(values, gain, shift):
    center = values - jnp.mean(values, axis=-1, keepdims=True)
    spread_out = jnp.mean(center * center, axis=-1, keepdims=True)
    return center * lax.rsqrt(spread_out + EPS) * gain + shift


def gelu(value):
    return 0.5 * value * (1.0 + lax.erf(value * (2.0 ** (-0.5))))


def project_kernel(place_ref, *refs):
    (*piece_refs, mine_ref, theirs_ref, x_hbm, gain_ref, shift_ref, norm_ref, keep_ref, att_scr, x_ref, sems) = refs
    depth = len(piece_refs)
    rows, width = norm_ref.shape
    share = rows // depth
    twins = x_hbm.shape[0] // rows
    copies = []
    for z in range(depth):
        start = pl.multiple_of((z * twins + place_ref[TWIN]) * share, share)
        copies.append(pltpu.make_async_copy(x_hbm.at[pl.ds(start, share)], x_ref.at[pl.ds(z * share, share)], sems.at[z]))
        copies[-1].start()
    core = place_ref[CORE]
    block = width // depth
    for bits, piece_ref in enumerate(piece_refs):
        source = place_ref[DEEP] ^ bits
        lanes = pl.ds(pl.multiple_of(source % (depth // 2) * block, block), block)
        att_scr[source // (depth // 2), :, lanes] = piece_ref[...]
    for copy in copies:
        copy.wait()
    total = x_ref[...].astype(F32)
    for side, ref in ((core, mine_ref), (1 - core, theirs_ref)):
        total += lax.dot_general(att_scr[side], ref[...], NT, preferred_element_type=F32)
    norm_ref[...] = normed(total, gain_ref[...], shift_ref[...]).astype(BF)
    keep_ref[...] = norm_ref[pl.ds(pl.multiple_of(place_ref[DEEP] * share, share), share)]


def feed_kernel(place_ref, norm_ref, mine_ref, theirs_ref, *refs):
    *sum_refs, sum_scr = refs
    half_h = mine_ref.shape[1] // 2
    share = sum_refs[0].shape[0]
    arrived = rearranged(norm_ref[...], False)
    result = jnp.zeros(norm_ref.shape, F32)
    for ref in (mine_ref, theirs_ref):
        up = jnp.dot(arrived, ref[:, :half_h], preferred_element_type=F32)
        active = gelu(up).astype(BF)
        result += lax.dot_general(active, ref[:, half_h:], NT, preferred_element_type=F32)
    sum_scr[...] = rearranged(result.astype(BF), True)
    for bits, sum_ref in enumerate(sum_refs):
        sum_ref[...] = sum_scr[pl.ds(pl.multiple_of((place_ref[DEEP] ^ bits) * share, share), share)]


def final_kernel(*refs):
    *sum_refs, keep_ref, gain_ref, shift_ref, out_ref = refs
    total = keep_ref[...].astype(F32)
    for sum_ref in sum_refs:
        total += sum_ref[...].astype(F32)
    out_ref[...] = normed(total, gain_ref[...], shift_ref[...]).astype(BF)


def cache_kernel(place_ref, own_ref, got_ref, keys_ref, values_ref):
    low = low_lanes(own_ref.shape)
    own = own_ref[...].astype(F32)
    got = got_ref[got_ref.shape[0] - own.shape[0] :].astype(F32)
    even = place_ref[CORE] == 0
    first = jnp.where(even, own, got)
    second = jnp.where(even, got, own)
    keys_ref[...] = jnp.where(low, first, turned(second)).astype(BF)
    values_ref[...] = jnp.where(low, turned(first), second).astype(BF)


def exchange(value, axes):
    return lax.all_to_all(value, axes, split_axis=0, concat_axis=0, tiled=True)


def swapped(value):
    return lax.ppermute(value, "cc", [(0, 1), (1, 0)])


def crossed(values):
    size = len(values)
    return [values[0]] + [lax.ppermute(values[bits], "zz", [(i, i ^ bits) for i in range(size)]) for bits in range(1, size)]


def body(hidden_in, request_ids, w_qkv, w_out, w_up, w_down, ln1_gain, ln1_shift, ln2_gain, ln2_shift):
    copies = lax.axis_size("yh") * lax.axis_size("xx")
    cores = lax.axis_size("cc")
    depth = lax.axis_size("zz")
    twins = lax.axis_size("yl")
    rows, width = hidden_in.shape
    unit = w_qkv.shape[0]
    hidden = w_up.shape[1] // depth
    place = jnp.stack([lax.axis_index("cc"), lax.axis_index("zz"), lax.axis_index("yl")]).astype(jnp.int32)

    def call(kernel, name, out_shape, in_specs, work=0, room=8, **more):
        more["cost_estimate"] = pl.CostEstimate(flops=work, bytes_accessed=2**20, transcendentals=0)
        flat = isinstance(out_shape, tuple)
        more.setdefault("out_specs", (VM,) * len(out_shape) if flat else VM)
        params = pltpu.CompilerParams(vmem_limit_bytes=room * 2**20)
        return pl.pallas_call(kernel, out_shape=out_shape, in_specs=in_specs, compiler_params=params, name=name, **more)

    def shape(*dims):
        return jax.ShapeDtypeStruct(dims, BF)

    first_cols = 128 + 384
    packed = call(pack_first_kernel, "pack_first", shape(copies, cores, depth, twins, unit, first_cols), [VM, VM])(w_qkv, w_out)
    served = exchange(packed.reshape(-1, unit, first_cols), GROUP + PART).reshape(width, first_cols)
    other_hidden = swapped(hidden_in)
    other_ids = swapped(request_ids)
    held = crossed(call(pack_depth_kernel, "pack_depth", (shape(unit, 2 * hidden),) * depth, [SM, VM, VM])(place, w_up, w_down))
    held, other_hidden, other_ids = lax.optimization_barrier((held, other_hidden, other_ids))
    packed_rest = call(pack_rest_kernel, "pack_rest", shape(copies, cores, twins, depth, unit, hidden), [SM] + [VM] * depth)(place, *held)
    packed_rest, served = lax.optimization_barrier((packed_rest, served))
    rest = exchange(packed_rest.reshape(-1, depth, unit, hidden), GROUP + ("yl",)).reshape(width, hidden)

    out_part = call(take_kernel, "take", shape(width, 128), [pl.BlockSpec((width, 128), lambda i: (0, 0))], grid=(1,), out_specs=pl.BlockSpec((width, 128), lambda i: (0, 0)))(served)
    out_parts = crossed([out_part] * depth)
    id_tiles = (rows // 128, 128)
    few = rows // twins
    att_own, kv_own, send = call(
        attend_kernel,
        "attend",
        (shape(few, 128), shape(rows, 128), shape(few + rows, 128)),
        [SM, HB, HB, VM, VM, VM],
        5 * 10**9,
        16,
        scratch_shapes=[pltpu.VMEM((2, rows, width), BF)]
        + [pltpu.VMEM((2, 2 * rows, 128), BF)] * 3
        + [pltpu.VMEM((2 * rows // 128, 128), F32), pltpu.SemaphoreType.DMA((2,))],
    )(place, hidden_in, other_hidden, served, request_ids.reshape(id_tiles), other_ids.reshape(id_tiles))
    got = swapped(send)
    joined = call(join_kernel, "join", shape(few, 256), [SM, VM, VM])(place, att_own, got)
    pieces = crossed([joined] * depth)
    rest, out_parts, pieces = lax.optimization_barrier((rest, out_parts, pieces))
    mine_out = call(assemble_kernel, "assemble", shape(width, width // cores), [SM] + [VM] * depth)(place, *out_parts)
    theirs_out = swapped(mine_out)
    theirs = swapped(rest)
    keys_out, values_out = call(cache_kernel, "cache", (shape(rows, 128),) * 2, [SM, VM, VM], 10**9)(place, kv_own, got)

    share = few // depth
    norm, keep = call(
        project_kernel,
        "project",
        (shape(few, width), shape(share, width)),
        [SM] + [VM] * (depth + 2) + [HB, VM, VM],
        2 * 10**9,
        16,
        scratch_shapes=[pltpu.VMEM((2, few, width // 2), BF), pltpu.VMEM((few, width), BF), pltpu.SemaphoreType.DMA((depth,))],
    )(place, *pieces, mine_out, theirs_out, hidden_in, ln1_gain[None, :], ln1_shift[None, :])
    sums = call(
        feed_kernel,
        "feed",
        (shape(share, width),) * depth,
        [SM] + [VM] * 3,
        3 * 10**9,
        20,
        scratch_shapes=[pltpu.VMEM((few, width), BF)],
    )(place, norm, rest, theirs)
    sums = crossed(sums)
    final = call(final_kernel, "final", shape(share, width), [VM] * (depth + 3))(*sums, keep, ln2_gain[None, :], ln2_shift[None, :])
    return (final, keys_out, values_out)


def solution(mesh):
    fine = Mesh(mesh.devices.reshape(2, 4, 2, 4, 2), GROUP + PART)
    in_specs = (
        P(GROUP, None),
        P(GROUP),
        P(GROUP + PART, None),
        P(GROUP + PART, None),
        P(GROUP + PART, None),
        P(GROUP + PART, None),
        P(),
        P(),
        P(),
        P(),
    )
    out_specs = (P(GROUP + PART, None), P(GROUP, PART), P(GROUP, PART))
    return jax.shard_map(body, mesh=fine, in_specs=in_specs, out_specs=out_specs, check_vma=False)
```

time: 100 us -> 95.2 us (0.952)
  waiting for transfers between devices: 39.7 us -> 31.1 us
  starting transfers between devices: 32.5 us -> 37.8 us
  Pallas kernels: 20.2 us -> 17.6 us
    all_to_all x3 -> x2, waiting for transfers between devices: 14 us -> 0.46 us  [exchange(): return lax.all_to_all(value, axes, split_axis=0, concat_axis=0, tiled=True)]
    ppermute x6 -> x12, starting transfers between devices: 7.85 us -> 15.1 us  [crossed(): lax.ppermute(values[bits], 'zz', [(i, i ^ bits) for i in range(size)])]
    ppermute x6 -> x12, waiting for transfers between devices: 19.8 us -> 26.5 us  [crossed(): lax.ppermute(values[bits], 'zz', [(i, i ^ bits) for i in range(size)])]
    pallas_call x8 -> x11, Pallas kernels: 20.2 us -> 17.6 us  [the longest x1 5.47 us: body(): call(attend_kernel, 'attend', (shape(few, 128), shape(rows, 128), shape(f...]
    all_to_all x3 -> x2, starting transfers between devices: 20.2 us -> 18.1 us  [exchange(): return lax.all_to_all(value, axes, split_axis=0, concat_axis=0, tiled=True)]
    ppermute x4 -> x5, waiting for transfers between devices: 5.91 us -> 4.16 us  [swapped(): return lax.ppermute(value, 'cc', [(0, 1), (1, 0)])]
    unnamed x31 -> x42, local copies, waits for them, and re-layouts: 6.26 us -> 7.37 us
    ppermute x4 -> x5, starting transfers between devices: 4.43 us -> 4.55 us  [swapped(): return lax.ppermute(value, 'cc', [(0, 1), (1, 0)])]
  transfers between devices with their start and end apart: 13 -> 19, of which waited for: 9 -> 11; matrix products, arithmetic and copies ran while one was open for 0% -> 0% of each run, Pallas kernels for 13% -> 15%
where the time goes in v4:
time: 95.2 us; the launch traced here: 94.7 us
  starting transfers between devices  37.8 us (40%)
  waiting for transfers between devices  31.1 us (33%)
  Pallas kernels  17.6 us (18%)
  local copies, waits for them, and re-layouts  7.37 us (8%)
    ppermute x12, waiting for transfers between devices, crossed(): lax.ppermute(values[bits], 'zz', [(i, i ^ bits) for i in range(size)])  26.5 us
    all_to_all x2, starting transfers between devices, exchange(): return lax.all_to_all(value, axes, split_axis=0, concat_axis=0, tiled=True)  18.1 us
    ppermute x12, starting transfers between devices, crossed(): lax.ppermute(values[bits], 'zz', [(i, i ^ bits) for i in range(size)])  15.1 us
    unnamed x42, local copies, waits for them, and re-layouts  7.37 us
    pallas_call x1, Pallas kernels, body(): call(attend_kernel, 'attend', (shape(few, 128), shape(rows, 128), shape(f...  5.47 us
    ppermute x5, starting transfers between devices, swapped(): return lax.ppermute(value, 'cc', [(0, 1), (1, 0)])  4.55 us
    ppermute x5, waiting for transfers between devices, swapped(): return lax.ppermute(value, 'cc', [(0, 1), (1, 0)])  4.16 us
    pallas_call x1, Pallas kernels, body(): call(project_kernel, 'project', (shape(few, width), shape(share, width)),...  2.36 us
  transfers between devices with their start and end apart: 19, of which 11 were waited for; matrix products, arithmetic and copies ran while one was open for 0% of the time, Pallas kernels for 15%

profile of v4, /device:TPU:1, one launch (start us, length us, event | category | flops | bytes accessed | tf_op | source)
XLA Modules:
  0.0 94.7 jit_solution(383407470291037039)
XLA Ops:
  0.7 1.5 %collective-permute-start.3 = (bf16[512,1024]{1,0:T(8,128)(2,1)}, bf16[512,1024]{1,0:T(8,128)(2,1)S(1)}, u32[]{:S(2)}, u32[]{:S(2)}) collective-permute-start(bf16[512,1024]{1,0:T(8,128)(2,1)} %refs_6_.1), channel_id=1, source_target_pairs={{0,8},{8,0},{1,9},{9,1},{2,10},{10,2},{3,11},{11,3},{4,12},{12,4},... | collective-permute-start | bytes 3145736 | tf_op jit(solution)/shard_map/ppermute | solution.py:261
  3.8 1.1 %pack_first.1 = bf16[8,2,4,2,8,512]{5,4,3,2,1,0:T(8,128)(2,1)} custom-call(f32[8,3072]{1,0:T(8,128)S(1)} %copy-done.4, f32[8,1024]{1,0:T(8,128)S(1)} %copy-done.5), custom_call_target="tpu_custom_call" | custom-call | bytes 1048576 | tf_op jit(solution)/shard_map/pack_first/pallas_call | solution.py:290
  4.9 10.2 %all-to-all-start = ((bf16[128,8,512]{2,1,0:T(8,128)(2,1)}), bf16[128,8,512]{2,1,0:T(8,128)(2,1)S(1)}, u32[]{:S(2)}, u32[]{:S(2)}) async-start(bf16[128,8,512]{2,1,0:T(8,128)(2,1)} %bitcast.3), calls=%async_computation | async-start | bytes 2097152 | tf_op jit(solution)/shard_map/all_to_all | solution.py:257
  15.8 1.6 %collective-permute-start = (bf16[8,2048]{1,0:T(8,128)(2,1)S(1)}, bf16[8,2048]{1,0:T(8,128)(2,1)S(1)}, u32[]{:S(2)}, u32[]{:S(2)}) collective-permute-start(bf16[8,2048]{1,0:T(8,128)(2,1)S(1)} %get-tuple-element.36), channel_id=1, source_target_pairs={{0,2},{2,0},{4,6},{6,4},{1,3},{3,1},{5,7},{7,5},{8,10},{10,8},{12,... | collective-permute-start | bytes 98312 | tf_op jit(solution)/shard_map/ppermute | solution.py:266
  17.4 2.9 %collective-permute-start.1 = (bf16[8,2048]{1,0:T(8,128)(2,1)S(1)}, bf16[8,2048]{1,0:T(8,128)(2,1)S(1)}, u32[]{:S(2)}, u32[]{:S(2)}) collective-permute-start(bf16[8,2048]{1,0:T(8,128)(2,1)S(1)} %get-tuple-element.37), channel_id=1, source_target_pairs={{0,4},{2,6},{4,0},{6,2},{1,5},{3,7},{5,1},{7,3},{8,12},{10,14},{12... | collective-permute-start | bytes 98312 | tf_op jit(solution)/shard_map/ppermute | solution.py:266
  20.3 1.3 %collective-permute-start.4 = (s32[512]{0:T(512)S(1)}, s32[512]{0:T(512)S(1)}, u32[]{:S(2)}, u32[]{:S(2)}) collective-permute-start(s32[512]{0:T(512)S(1)} %copy-done.18), channel_id=1, source_target_pairs={{0,8},{8,0},{1,9},{9,1},{2,10},{10,2},{3,11},{11,3},{4,12},{12,4},... | collective-permute-start | bytes 6152 | tf_op jit(solution)/shard_map/ppermute | solution.py:261
  22.5 1.6 %collective-permute-done.refs_1_ = bf16[8,2048]{1,0:T(8,128)(2,1)S(1)} collective-permute-done((bf16[8,2048]{1,0:T(8,128)(2,1)S(1)}, bf16[8,2048]{1,0:T(8,128)(2,1)S(1)}, u32[]{:S(2)}, u32[]{:S(2)}) %collective-permute-start) | collective-permute-done | bytes 32800 | tf_op jit(solution)/shard_map/ppermute | solution.py:266
  24.1 6.8 %collective-permute-done.1.refs_2_ = bf16[8,2048]{1,0:T(8,128)(2,1)S(1)} collective-permute-done((bf16[8,2048]{1,0:T(8,128)(2,1)S(1)}, bf16[8,2048]{1,0:T(8,128)(2,1)S(1)}, u32[]{:S(2)}, u32[]{:S(2)}) %collective-permute-start.1) | collective-permute-done | bytes 32800 | tf_op jit(solution)/shard_map/ppermute | solution.py:266
  30.8 2.1 %pack_rest.1 = bf16[8,2,2,4,8,1024]{5,4,3,2,1,0:T(8,128)(2,1)} custom-call(s32[3]{0:T(128)S(1)} %pad_add_fusion.place_ref, bf16[8,2048]{1,0:T(8,128)(2,1)S(1)} %get-tuple-element.39.refs_0_, bf16[8,2048]{1,0:T(8,128)(2,1)S(1)} %collective-permute-done.refs_1_, bf16[8,2048]{1,0:T(8,128)(2,1)S(1)} %collective-permute-done.1.refs_2_, ...), custom_call_target="tpu_custom_call" | custom-call | bytes 1048576 | tf_op jit(solution)/shard_map/pack_rest/pallas_call | solution.py:296
  33.4 7.9 %all-to-all-start.1 = ((bf16[32,4,8,1024]{3,2,1,0:T(8,128)(2,1)}), bf16[32,4,8,1024]{3,2,1,0:T(8,128)(2,1)S(1)}, u32[]{:S(2)}, u32[]{:S(2)}) async-start(bf16[32,4,8,1024]{3,2,1,0:T(8,128)(2,1)} %bitcast.5), calls=%async_computation.1 | async-start | bytes 4194304 | tf_op jit(solution)/shard_map/all_to_all | solution.py:257
  42.1 1.2 %copy-done.8 = bf16[512,1024]{1,0:T(8,128)(2,1)S(1)} copy-done((bf16[512,1024]{1,0:T(8,128)(2,1)S(1)}, bf16[512,1024]{1,0:T(8,128)(2,1)}, u32[]{:S(2)}) %copy-start.8) | copy-done | bytes 1048600
  43.3 1.2 %copy-done.11 = bf16[512,1024]{1,0:T(8,128)(2,1)S(1)} copy-done((bf16[512,1024]{1,0:T(8,128)(2,1)S(1)}, bf16[512,1024]{1,0:T(8,128)(2,1)}, u32[]{:S(2)}) %copy-start.11) | copy-done | bytes 1048600
  44.5 5.5 %attend.1 = (bf16[256,128]{1,0:T(8,128)(2,1)S(1)}, bf16[512,128]{1,0:T(8,128)(2,1)S(1)}, bf16[768,128]{1,0:T(8,128)(2,1)S(1)}) custom-call(s32[3]{0:T(128)S(1)} %pad_add_fusion.place_ref, bf16[512,1024]{1,0:T(8,128)(2,1)S(1)} %copy-done.8, bf16[512,1024]{1,0:T(8,128)(2,1)S(1)} %copy-done.11, bf16[1024,512]{1,0:T(8,128)(2,1)S(1)} %bitcast.14, ...), custom_call_target="tpu_custom_call" | custom-call | flops 5000000000 | bytes 1048576 | tf_op jit(solution)/shard_map/attend/pallas_call | solution.py:304
  50.6 1.6 %collective-permute-start.6 = (bf16[1024,128]{1,0:T(8,128)(2,1)S(1)}, bf16[1024,128]{1,0:T(8,128)(2,1)S(1)}, u32[]{:S(2)}, u32[]{:S(2)}) collective-permute-start(bf16[1024,128]{1,0:T(8,128)(2,1)S(1)} %take.1.refs_0_), channel_id=1, source_target_pairs={{0,4},{2,6},{4,0},{6,2},{1,5},{3,7},{5,1},{7,3},{8,12},{10,14},{12... | collective-permute-start | bytes 786440 | tf_op jit(solution)/shard_map/ppermute | solution.py:266
  52.2 1.1 %collective-permute-start.5 = (bf16[1024,128]{1,0:T(8,128)(2,1)S(1)}, bf16[1024,128]{1,0:T(8,128)(2,1)S(1)}, u32[]{:S(2)}, u32[]{:S(2)}) collective-permute-start(bf16[1024,128]{1,0:T(8,128)(2,1)S(1)} %take.1.refs_0_), channel_id=1, source_target_pairs={{0,2},{2,0},{4,6},{6,4},{1,3},{3,1},{5,7},{7,5},{8,10},{10,8},{12,... | collective-permute-start | bytes 786440 | tf_op jit(solution)/shard_map/ppermute | solution.py:266
  54.6 1.6 %collective-permute-start.10 = (bf16[256,256]{1,0:T(8,128)(2,1)S(1)}, bf16[256,256]{1,0:T(8,128)(2,1)S(1)}, u32[]{:S(2)}, u32[]{:S(2)}) collective-permute-start(bf16[256,256]{1,0:T(8,128)(2,1)S(1)} %join.1.refs_0_), channel_id=1, source_target_pairs={{0,4},{2,6},{4,0},{6,2},{1,5},{3,7},{5,1},{7,3},{8,12},{10,14},{12... | collective-permute-start | bytes 393224 | tf_op jit(solution)/shard_map/ppermute | solution.py:266
  56.9 1.1 %collective-permute-start.9 = (bf16[256,256]{1,0:T(8,128)(2,1)S(1)}, bf16[256,256]{1,0:T(8,128)(2,1)S(1)}, u32[]{:S(2)}, u32[]{:S(2)}) collective-permute-start(bf16[256,256]{1,0:T(8,128)(2,1)S(1)} %join.1.refs_0_), channel_id=1, source_target_pairs={{0,2},{2,0},{4,6},{6,4},{1,3},{3,1},{5,7},{7,5},{8,10},{10,8},{12,... | collective-permute-start | bytes 393224 | tf_op jit(solution)/shard_map/ppermute | solution.py:266
  58.0 2.0 %collective-permute-done.6.refs_2_ = bf16[1024,128]{1,0:T(8,128)(2,1)S(1)} collective-permute-done((bf16[1024,128]{1,0:T(8,128)(2,1)S(1)}, bf16[1024,128]{1,0:T(8,128)(2,1)S(1)}, u32[]{:S(2)}, u32[]{:S(2)}) %collective-permute-start.6) | collective-permute-done | bytes 262176 | tf_op jit(solution)/shard_map/ppermute | solution.py:266
  60.0 5.3 %collective-permute-done.5.refs_1_ = bf16[1024,128]{1,0:T(8,128)(2,1)S(1)} collective-permute-done((bf16[1024,128]{1,0:T(8,128)(2,1)S(1)}, bf16[1024,128]{1,0:T(8,128)(2,1)S(1)}, u32[]{:S(2)}, u32[]{:S(2)}) %collective-permute-start.5) | collective-permute-done | bytes 262176 | tf_op jit(solution)/shard_map/ppermute | solution.py:266
  65.3 3.1 %collective-permute-done.10.refs_2_ = bf16[256,256]{1,0:T(8,128)(2,1)S(1)} collective-permute-done((bf16[256,256]{1,0:T(8,128)(2,1)S(1)}, bf16[256,256]{1,0:T(8,128)(2,1)S(1)}, u32[]{:S(2)}, u32[]{:S(2)}) %collective-permute-start.10) | collective-permute-done | bytes 131104 | tf_op jit(solution)/shard_map/ppermute | solution.py:266
  68.5 2.5 %collective-permute-done.9.refs_1_ = bf16[256,256]{1,0:T(8,128)(2,1)S(1)} collective-permute-done((bf16[256,256]{1,0:T(8,128)(2,1)S(1)}, bf16[256,256]{1,0:T(8,128)(2,1)S(1)}, u32[]{:S(2)}, u32[]{:S(2)}) %collective-permute-start.9) | collective-permute-done | bytes 131104 | tf_op jit(solution)/shard_map/ppermute | solution.py:266
  72.5 0.9 %copy-done.1 = bf16[1024,128]{1,0:T(8,128)(2,1)S(1)} copy-done((bf16[1024,128]{1,0:T(8,128)(2,1)S(1)}, bf16[1024,128]{1,0:T(8,128)(2,1)}, u32[]{:S(2)}) %copy-start.1) | copy-done | bytes 262168
  74.4 3.3 %collective-permute-done.12.refs_5_ = bf16[1024,512]{1,0:T(8,128)(2,1)S(1)} collective-permute-done((bf16[1024,512]{1,0:T(8,128)(2,1)S(1)}, bf16[1024,512]{1,0:T(8,128)(2,1)S(1)}, u32[]{:S(2)}, u32[]{:S(2)}) %collective-permute-start.12) | collective-permute-done | bytes 1048608 | tf_op jit(solution)/shard_map/ppermute | solution.py:261
  77.8 0.9 copy-done.13
  78.7 2.4 %project.1 = (bf16[256,1024]{1,0:T(8,128)(2,1)S(1)}, bf16[64,1024]{1,0:T(8,128)(2,1)S(1)}) custom-call(s32[3]{0:T(128)S(1)} %pad_add_fusion.place_ref, bf16[256,256]{1,0:T(8,128)(2,1)S(1)} %join.1.refs_0_, bf16[256,256]{1,0:T(8,128)(2,1)S(1)} %copy-done.15, bf16[256,256]{1,0:T(8,128)(2,1)S(1)} %copy-done.13, ...), custom_call_target="tpu_custom_call" | custom-call | flops 2000000000 | bytes 1048576 | tf_op jit(solution)/shard_map/project/pallas_call | solution.py:325
  81.1 2.3 %feed.1 = (bf16[64,1024]{1,0:T(8,128)(2,1)S(1)}, bf16[64,1024]{1,0:T(8,128)(2,1)S(1)}, bf16[64,1024]{1,0:T(8,128)(2,1)S(1)}, bf16[64,1024]{1,0:T(8,128)(2,1)S(1)}) custom-call(s32[3]{0:T(128)S(1)} %pad_add_fusion.place_ref, bf16[256,1024]{1,0:T(8,128)(2,1)S(1)} %get-tuple-element.57.norm_ref, bf16[1024,1024]{1,0:T(8,128)(2,1)S(1)} %bitcast.16, ...), custom_call_target="tpu_custom_call" | custom-call | flops 3000000000 | bytes 1048576 | tf_op jit(solution)/shard_map/feed/pallas_call | solution.py:334
  83.9 1.4 %collective-permute-start.15 = (bf16[64,1024]{1,0:T(8,128)(2,1)S(1)}, bf16[64,1024]{1,0:T(8,128)(2,1)S(1)}, u32[]{:S(2)}, u32[]{:S(2)}) collective-permute-start(bf16[64,1024]{1,0:T(8,128)(2,1)S(1)} %get-tuple-element.61), channel_id=1, source_target_pairs={{0,4},{2,6},{4,0},{6,2},{1,5},{3,7},{5,1},{7,3},{8,12},{10,14},{12... | collective-permute-start | bytes 393224 | tf_op jit(solution)/shard_map/ppermute | solution.py:266
  85.2 2.1 %collective-permute-start.16 = (bf16[64,1024]{1,0:T(8,128)(2,1)S(1)}, bf16[64,1024]{1,0:T(8,128)(2,1)S(1)}, u32[]{:S(2)}, u32[]{:S(2)}) collective-permute-start(bf16[64,1024]{1,0:T(8,128)(2,1)S(1)} %get-tuple-element.62), channel_id=1, source_target_pairs={{0,6},{2,4},{4,2},{6,0},{1,7},{3,5},{5,3},{7,1},{8,14},{10,12},{12... | collective-permute-start | bytes 393224 | tf_op jit(solution)/shard_map/ppermute | solution.py:266
  87.3 1.4 %cache.1 = (bf16[512,128]{1,0:T(8,128)(2,1)}, bf16[512,128]{1,0:T(8,128)(2,1)}) custom-call(s32[3]{0:T(128)S(1)} %pad_add_fusion.place_ref, bf16[512,128]{1,0:T(8,128)(2,1)S(1)} %copy-done.20, bf16[768,128]{1,0:T(8,128)(2,1)S(1)} %collective-permute-done.8.got_ref), custom_call_target="tpu_custom_call" | custom-call | flops 1000000000 | bytes 1048576 | tf_op jit(solution)/shard_map/cache/pallas_call | solution.py:322
  88.7 2.6 %collective-permute-done.15.refs_2_ = bf16[64,1024]{1,0:T(8,128)(2,1)S(1)} collective-permute-done((bf16[64,1024]{1,0:T(8,128)(2,1)S(1)}, bf16[64,1024]{1,0:T(8,128)(2,1)S(1)}, u32[]{:S(2)}, u32[]{:S(2)}) %collective-permute-start.15) | collective-permute-done | bytes 131104 | tf_op jit(solution)/shard_map/ppermute | solution.py:266
  91.3 2.5 %collective-permute-done.16.refs_3_ = bf16[64,1024]{1,0:T(8,128)(2,1)S(1)} collective-permute-done((bf16[64,1024]{1,0:T(8,128)(2,1)S(1)}, bf16[64,1024]{1,0:T(8,128)(2,1)S(1)}, u32[]{:S(2)}, u32[]{:S(2)}) %collective-permute-start.16) | collective-permute-done | bytes 131104 | tf_op jit(solution)/shard_map/ppermute | solution.py:266
  93.8 0.9 final.1
  (60 shorter events, 10.0 us)
Async XLA Ops:
  0.6 14.6 %copy-start.3 = (f32[8,4096]{1,0:T(8,128)S(1)}, f32[8,4096]{1,0:T(8,128)}, u32[]{:S(2)}) copy-start(f32[8,4096]{1,0:T(8,128)} %down_ref.1) | copy-start | bytes 393220
  0.6 14.6 %copy-start.2 = (f32[8,4096]{1,0:T(8,128)S(1)}, f32[8,4096]{1,0:T(8,128)}, u32[]{:S(2)}) copy-start(f32[8,4096]{1,0:T(8,128)} %up_ref.1) | copy-start | bytes 393220
  0.7 30.2 %collective-permute-start.3 = (bf16[512,1024]{1,0:T(8,128)(2,1)}, bf16[512,1024]{1,0:T(8,128)(2,1)S(1)}, u32[]{:S(2)}, u32[]{:S(2)}) collective-permute-start(bf16[512,1024]{1,0:T(8,128)(2,1)} %refs_6_.1), channel_id=1, source_target_pairs={{0,8},{8,0},{1,9},{9,1},{2,10},{10,2},{3,11},{11,3},{4,12},{12,4},... | collective-permute-start | bytes 3145736 | tf_op jit(solution)/shard_map/ppermute | solution.py:261
  3.8 16.5 %copy-start.18 = (s32[512]{0:T(512)S(1)}, s32[512]{0:T(512)}, u32[]{:S(2)}) copy-start(s32[512]{0:T(512)} %param.11) | copy-start | bytes 6148
  4.9 28.5 %all-to-all-start = ((bf16[128,8,512]{2,1,0:T(8,128)(2,1)}), bf16[128,8,512]{2,1,0:T(8,128)(2,1)S(1)}, u32[]{:S(2)}, u32[]{:S(2)}) async-start(bf16[128,8,512]{2,1,0:T(8,128)(2,1)} %bitcast.3), calls=%async_computation | async-start | bytes 2097152 | tf_op jit(solution)/shard_map/all_to_all | solution.py:257
  15.8 8.3 %collective-permute-start = (bf16[8,2048]{1,0:T(8,128)(2,1)S(1)}, bf16[8,2048]{1,0:T(8,128)(2,1)S(1)}, u32[]{:S(2)}, u32[]{:S(2)}) collective-permute-start(bf16[8,2048]{1,0:T(8,128)(2,1)S(1)} %get-tuple-element.36), channel_id=1, source_target_pairs={{0,2},{2,0},{4,6},{6,4},{1,3},{3,1},{5,7},{7,5},{8,10},{10,8},{12,... | collective-permute-start | bytes 98312 | tf_op jit(solution)/shard_map/ppermute | solution.py:266
  17.4 13.5 %collective-permute-start.1 = (bf16[8,2048]{1,0:T(8,128)(2,1)S(1)}, bf16[8,2048]{1,0:T(8,128)(2,1)S(1)}, u32[]{:S(2)}, u32[]{:S(2)}) collective-permute-start(bf16[8,2048]{1,0:T(8,128)(2,1)S(1)} %get-tuple-element.37), channel_id=1, source_target_pairs={{0,4},{2,6},{4,0},{6,2},{1,5},{3,7},{5,1},{7,3},{8,12},{10,14},{12... | collective-permute-start | bytes 98312 | tf_op jit(solution)/shard_map/ppermute | solution.py:266
  20.3 10.5 %collective-permute-start.2 = (bf16[8,2048]{1,0:T(8,128)(2,1)S(1)}, bf16[8,2048]{1,0:T(8,128)(2,1)S(1)}, u32[]{:S(2)}, u32[]{:S(2)}) collective-permute-start(bf16[8,2048]{1,0:T(8,128)(2,1)S(1)} %get-tuple-element.38), channel_id=1, source_target_pairs={{0,6},{2,4},{4,2},{6,0},{1,7},{3,5},{5,3},{7,1},{8,14},{10,12},{12... | collective-permute-start | bytes 98312 | tf_op jit(solution)/shard_map/ppermute | solution.py:266
  20.3 2.1 %collective-permute-start.4 = (s32[512]{0:T(512)S(1)}, s32[512]{0:T(512)S(1)}, u32[]{:S(2)}, u32[]{:S(2)}) collective-permute-start(s32[512]{0:T(512)S(1)} %copy-done.18), channel_id=1, source_target_pairs={{0,8},{8,0},{1,9},{9,1},{2,10},{10,2},{3,11},{11,3},{4,12},{12,4},... | collective-permute-start | bytes 6152 | tf_op jit(solution)/shard_map/ppermute | solution.py:261
  30.8 2.6 %copy-start.10 = (bf16[512,1024]{1,0:T(8,128)(2,1)}, bf16[512,1024]{1,0:T(8,128)(2,1)S(1)}, u32[]{:S(2)}) copy-start(bf16[512,1024]{1,0:T(8,128)(2,1)S(1)} %collective-permute-done.3.other_hbm) | copy-start | bytes 3145732
  33.4 38.2 %all-to-all-start.1 = ((bf16[32,4,8,1024]{3,2,1,0:T(8,128)(2,1)}), bf16[32,4,8,1024]{3,2,1,0:T(8,128)(2,1)S(1)}, u32[]{:S(2)}, u32[]{:S(2)}) async-start(bf16[32,4,8,1024]{3,2,1,0:T(8,128)(2,1)} %bitcast.5), calls=%async_computation.1 | async-start | bytes 4194304 | tf_op jit(solution)/shard_map/all_to_all | solution.py:257
  41.4 14.8 %collective-permute-start.7 = (bf16[1024,128]{1,0:T(8,128)(2,1)S(1)}, bf16[1024,128]{1,0:T(8,128)(2,1)S(1)}, u32[]{:S(2)}, u32[]{:S(2)}) collective-permute-start(bf16[1024,128]{1,0:T(8,128)(2,1)S(1)} %take.1.refs_0_), channel_id=1, source_target_pairs={{0,6},{2,4},{4,2},{6,0},{1,7},{3,5},{5,3},{7,1},{8,14},{10,12},{12... | collective-permute-start | bytes 786440 | tf_op jit(solution)/shard_map/ppermute | solution.py:266
  50.0 18.5 %copy-start.19 = (bf16[512,128]{1,0:T(8,128)(2,1)}, bf16[512,128]{1,0:T(8,128)(2,1)S(1)}, u32[]{:S(2)}) copy-start(bf16[512,128]{1,0:T(8,128)(2,1)S(1)} %get-tuple-element.64.own_ref) | copy-start | bytes 393220
  50.0 27.8 %copy-start.16 = (f32[1024]{0:T(1024)S(1)}, f32[1024]{0:T(1024)}, u32[]{:S(2)}) copy-start(f32[1024]{0:T(1024)} %param.16) | copy-start | bytes 12292
  50.0 27.8 %copy-start.17 = (f32[1024]{0:T(1024)S(1)}, f32[1024]{0:T(1024)}, u32[]{:S(2)}) copy-start(f32[1024]{0:T(1024)} %param.17) | copy-start | bytes 12292
  50.0 3.3 %collective-permute-start.8 = (bf16[768,128]{1,0:T(8,128)(2,1)S(1)}, bf16[768,128]{1,0:T(8,128)(2,1)S(1)}, u32[]{:S(2)}, u32[]{:S(2)}) collective-permute-start(bf16[768,128]{1,0:T(8,128)(2,1)S(1)} %get-tuple-element.48), channel_id=1, source_target_pairs={{0,8},{8,0},{1,9},{9,1},{2,10},{10,2},{3,11},{11,3},{4,12},{12,4},... | collective-permute-start | bytes 589832 | tf_op jit(solution)/shard_map/ppermute | solution.py:261
  50.6 9.4 %collective-permute-start.6 = (bf16[1024,128]{1,0:T(8,128)(2,1)S(1)}, bf16[1024,128]{1,0:T(8,128)(2,1)S(1)}, u32[]{:S(2)}, u32[]{:S(2)}) collective-permute-start(bf16[1024,128]{1,0:T(8,128)(2,1)S(1)} %take.1.refs_0_), channel_id=1, source_target_pairs={{0,4},{2,6},{4,0},{6,2},{1,5},{3,7},{5,1},{7,3},{8,12},{10,14},{12... | collective-permute-start | bytes 786440 | tf_op jit(solution)/shard_map/ppermute | solution.py:266
  52.2 13.1 %collective-permute-start.5 = (bf16[1024,128]{1,0:T(8,128)(2,1)S(1)}, bf16[1024,128]{1,0:T(8,128)(2,1)S(1)}, u32[]{:S(2)}, u32[]{:S(2)}) collective-permute-start(bf16[1024,128]{1,0:T(8,128)(2,1)S(1)} %take.1.refs_0_), channel_id=1, source_target_pairs={{0,2},{2,0},{4,6},{6,4},{1,3},{3,1},{5,7},{7,5},{8,10},{10,8},{12,... | collective-permute-start | bytes 786440 | tf_op jit(solution)/shard_map/ppermute | solution.py:266
  54.0 11.4 %collective-permute-start.11 = (bf16[256,256]{1,0:T(8,128)(2,1)S(1)}, bf16[256,256]{1,0:T(8,128)(2,1)S(1)}, u32[]{:S(2)}, u32[]{:S(2)}) collective-permute-start(bf16[256,256]{1,0:T(8,128)(2,1)S(1)} %join.1.refs_0_), channel_id=1, source_target_pairs={{0,6},{2,4},{4,2},{6,0},{1,7},{3,5},{5,3},{7,1},{8,14},{10,12},{12... | collective-permute-start | bytes 393224 | tf_op jit(solution)/shard_map/ppermute | solution.py:266
  54.6 13.8 %collective-permute-start.10 = (bf16[256,256]{1,0:T(8,128)(2,1)S(1)}, bf16[256,256]{1,0:T(8,128)(2,1)S(1)}, u32[]{:S(2)}, u32[]{:S(2)}) collective-permute-start(bf16[256,256]{1,0:T(8,128)(2,1)S(1)} %join.1.refs_0_), channel_id=1, source_target_pairs={{0,4},{2,6},{4,0},{6,2},{1,5},{3,7},{5,1},{7,3},{8,12},{10,14},{12... | collective-permute-start | bytes 393224 | tf_op jit(solution)/shard_map/ppermute | solution.py:266
  56.9 14.0 %collective-permute-start.9 = (bf16[256,256]{1,0:T(8,128)(2,1)S(1)}, bf16[256,256]{1,0:T(8,128)(2,1)S(1)}, u32[]{:S(2)}, u32[]{:S(2)}) collective-permute-start(bf16[256,256]{1,0:T(8,128)(2,1)S(1)} %join.1.refs_0_), channel_id=1, source_target_pairs={{0,2},{2,0},{4,6},{6,4},{1,3},{3,1},{5,7},{7,5},{8,10},{10,8},{12,... | collective-permute-start | bytes 393224 | tf_op jit(solution)/shard_map/ppermute | solution.py:266
  68.5 9.3 %copy-start.12 = (bf16[256,256]{1,0:T(8,128)(2,1)}, bf16[256,256]{1,0:T(8,128)(2,1)S(1)}, u32[]{:S(2)}) copy-start(bf16[256,256]{1,0:T(8,128)(2,1)S(1)} %collective-permute-done.10.refs_2_) | copy-start | bytes 393220
  71.6 9.5 %collective-permute-start.13 = (bf16[1024,1024]{1,0:T(8,128)(2,1)S(1)}, bf16[1024,1024]{1,0:T(8,128)(2,1)S(1)}, u32[]{:S(2)}, u32[]{:S(2)}) collective-permute-start(bf16[1024,1024]{1,0:T(8,128)(2,1)S(1)} %bitcast.15), channel_id=1, source_target_pairs={{0,8},{8,0},{1,9},{9,1},{2,10},{10,2},{3,11},{11,3},{4,12},{12,4},... | collective-permute-start | bytes 6291464 | tf_op jit(solution)/shard_map/ppermute | solution.py:261
  73.4 4.3 %copy-start.9 = (bf16[512,1024]{1,0:T(8,128)(2,1)S(1)}, bf16[512,1024]{1,0:T(8,128)(2,1)}, u32[]{:S(2)}) copy-start(bf16[512,1024]{1,0:T(8,128)(2,1)} %refs_6_.1) | copy-start | bytes 3145732
  73.4 4.3 %copy-start.15 = (bf16[256,256]{1,0:T(8,128)(2,1)S(1)}, bf16[256,256]{1,0:T(8,128)(2,1)}, u32[]{:S(2)}) copy-start(bf16[256,256]{1,0:T(8,128)(2,1)} %copy-done.14) | copy-start | bytes 393220
  74.2 3.6 %collective-permute-start.12 = (bf16[1024,512]{1,0:T(8,128)(2,1)S(1)}, bf16[1024,512]{1,0:T(8,128)(2,1)S(1)}, u32[]{:S(2)}, u32[]{:S(2)}) collective-permute-start(bf16[1024,512]{1,0:T(8,128)(2,1)S(1)} %assemble.1.refs_4_), channel_id=1, source_target_pairs={{0,8},{8,0},{1,9},{9,1},{2,10},{10,2},{3,11},{11,3},{4,12},{12,4},... | collective-permute-start | bytes 3145736 | tf_op jit(solution)/shard_map/ppermute | solution.py:261
  81.1 6.2 %copy-start.20 = (bf16[512,128]{1,0:T(8,128)(2,1)S(1)}, bf16[512,128]{1,0:T(8,128)(2,1)}, u32[]{:S(2)}) copy-start(bf16[512,128]{1,0:T(8,128)(2,1)} %copy-done.19) | copy-start | bytes 393220
  83.4 10.5 %copy-start.6 = (f32[1024]{0:T(1024)S(1)}, f32[1024]{0:T(1024)}, u32[]{:S(2)}) copy-start(f32[1024]{0:T(1024)} %param.18) | copy-start | bytes 12292
  83.4 10.4 %copy-start.7 = (f32[1024]{0:T(1024)S(1)}, f32[1024]{0:T(1024)}, u32[]{:S(2)}) copy-start(f32[1024]{0:T(1024)} %param.19) | copy-start | bytes 12292
  83.4 5.3 %collective-permute-start.14 = (bf16[64,1024]{1,0:T(8,128)(2,1)S(1)}, bf16[64,1024]{1,0:T(8,128)(2,1)S(1)}, u32[]{:S(2)}, u32[]{:S(2)}) collective-permute-start(bf16[64,1024]{1,0:T(8,128)(2,1)S(1)} %get-tuple-element.60), channel_id=1, source_target_pairs={{0,2},{2,0},{4,6},{6,4},{1,3},{3,1},{5,7},{7,5},{8,10},{10,8},{12,... | collective-permute-start | bytes 393224 | tf_op jit(solution)/shard_map/ppermute | solution.py:266
  83.9 7.5 %collective-permute-start.15 = (bf16[64,1024]{1,0:T(8,128)(2,1)S(1)}, bf16[64,1024]{1,0:T(8,128)(2,1)S(1)}, u32[]{:S(2)}, u32[]{:S(2)}) collective-permute-start(bf16[64,1024]{1,0:T(8,128)(2,1)S(1)} %get-tuple-element.61), channel_id=1, source_target_pairs={{0,4},{2,6},{4,0},{6,2},{1,5},{3,7},{5,1},{7,3},{8,12},{10,14},{12... | collective-permute-start | bytes 393224 | tf_op jit(solution)/shard_map/ppermute | solution.py:266
  85.2 8.6 %collective-permute-start.16 = (bf16[64,1024]{1,0:T(8,128)(2,1)S(1)}, bf16[64,1024]{1,0:T(8,128)(2,1)S(1)}, u32[]{:S(2)}, u32[]{:S(2)}) collective-permute-start(bf16[64,1024]{1,0:T(8,128)(2,1)S(1)} %get-tuple-element.62), channel_id=1, source_target_pairs={{0,6},{2,4},{4,2},{6,0},{1,7},{3,5},{5,3},{7,1},{8,14},{10,12},{12... | collective-permute-start | bytes 393224 | tf_op jit(solution)/shard_map/ppermute | solution.py:266
  (8 other events, 7.3 us)

commit v5 on v4

--- a/solution.py
+++ b/solution.py
@@ -219,16 +219,22 @@
     keep_ref[...] = norm_ref[pl.ds(pl.multiple_of(place_ref[DEEP] * share, share), share)]
 
 
-def feed_kernel(place_ref, norm_ref, mine_ref, theirs_ref, *refs):
+def half_feed(arrived, ref):
+    half_h = ref.shape[1] // 2
+    up = jnp.dot(arrived, ref[:, :half_h], preferred_element_type=F32)
+    active = gelu(up).astype(BF)
+    return lax.dot_general(active, ref[:, half_h:], NT, preferred_element_type=F32)
+
+
+def own_feed_kernel(norm_ref, mine_ref, arrived_ref, result_ref):
+    arrived_ref[...] = rearranged(norm_ref[...], False)
+    result_ref[...] = half_feed(arrived_ref[...], mine_ref)
+
+
+def feed_kernel(place_ref, arrived_ref, own_ref, theirs_ref, *refs):
     *sum_refs, sum_scr = refs
-    half_h = mine_ref.shape[1] // 2
     share = sum_refs[0].shape[0]
-    arrived = rearranged(norm_ref[...], False)
-    result = jnp.zeros(norm_ref.shape, F32)
-    for ref in (mine_ref, theirs_ref):
-        up = jnp.dot(arrived, ref[:, :half_h], preferred_element_type=F32)
-        active = gelu(up).astype(BF)
-        result += lax.dot_general(active, ref[:, half_h:], NT, preferred_element_type=F32)
+    result = own_ref[...] + half_feed(arrived_ref[...], theirs_ref)
     sum_scr[...] = rearranged(result.astype(BF), True)
     for bits, sum_ref in enumerate(sum_refs):
         sum_ref[...] = sum_scr[pl.ds(pl.multiple_of((place_ref[DEEP] ^ bits) * share, share), share)]
@@ -286,6 +292,7 @@
     def shape(*dims):
         return jax.ShapeDtypeStruct(dims, BF)
 
+    w_qkv, w_out, w_up, w_down, hidden_in = (pltpu.with_memory_space_constraint(x, pltpu.HBM) for x in (w_qkv, w_out, w_up, w_down, hidden_in))
     first_cols = 128 + 384
     packed = call(pack_first_kernel, "pack_first", shape(copies, cores, depth, twins, unit, first_cols), [VM, VM])(w_qkv, w_out)
     served = exchange(packed.reshape(-1, unit, first_cols), GROUP + PART).reshape(width, first_cols)
@@ -314,11 +321,11 @@
     )(place, hidden_in, other_hidden, served, request_ids.reshape(id_tiles), other_ids.reshape(id_tiles))
     got = swapped(send)
     joined = call(join_kernel, "join", shape(few, 256), [SM, VM, VM])(place, att_own, got)
+    out_parts, got = lax.optimization_barrier((out_parts, got))
+    mine_out = call(assemble_kernel, "assemble", shape(width, width // cores), [SM] + [VM] * depth)(place, *out_parts)
+    mine_out, joined = lax.optimization_barrier((mine_out, joined))
     pieces = crossed([joined] * depth)
-    rest, out_parts, pieces = lax.optimization_barrier((rest, out_parts, pieces))
-    mine_out = call(assemble_kernel, "assemble", shape(width, width // cores), [SM] + [VM] * depth)(place, *out_parts)
     theirs_out = swapped(mine_out)
-    theirs = swapped(rest)
     keys_out, values_out = call(cache_kernel, "cache", (shape(rows, 128),) * 2, [SM, VM, VM], 10**9)(place, kv_own, got)
 
     share = few // depth
@@ -331,6 +338,16 @@
         16,
         scratch_shapes=[pltpu.VMEM((2, few, width // 2), BF), pltpu.VMEM((few, width), BF), pltpu.SemaphoreType.DMA((depth,))],
     )(place, *pieces, mine_out, theirs_out, hidden_in, ln1_gain[None, :], ln1_shift[None, :])
+    rest, norm = lax.optimization_barrier((rest, norm))
+    theirs = swapped(rest)
+    arrived, own_sums = call(
+        own_feed_kernel,
+        "own_feed",
+        (shape(few, width), jax.ShapeDtypeStruct((few, width), F32)),
+        [VM, VM],
+        2 * 10**9,
+        16,
+    )(norm, rest)
     sums = call(
         feed_kernel,
         "feed",
@@ -339,7 +356,7 @@
         3 * 10**9,
         20,
         scratch_shapes=[pltpu.VMEM((few, width), BF)],
-    )(place, norm, rest, theirs)
+    )(place, arrived, own_sums, theirs)
     sums = crossed(sums)
     final = call(final_kernel, "final", shape(share, width), [VM] * (depth + 3))(*sums, keep, ln2_gain[None, :], ln2_shift[None, :])
     return (final, keys_out, values_out)

time: 95.2 us -> 89 us (0.935)
  waiting for transfers between devices: 31.1 us -> 25.5 us
  local copies, waits for them, and re-layouts: 7.37 us -> 1.87 us
  Pallas kernels: 17.6 us -> 20.5 us
  starting transfers between devices: 37.8 us -> 39.8 us
    unnamed x42 -> x16, local copies, waits for them, and re-layouts: 7.37 us -> 1.87 us
    ppermute x12, waiting for transfers between devices: 26.5 us -> 21.3 us  [crossed(): lax.ppermute(values[bits], 'zz', [(i, i ^ bits) for i in range(size)])]
    ppermute x5, starting transfers between devices: 4.55 us -> 6.61 us  [swapped(): return lax.ppermute(value, 'cc', [(0, 1), (1, 0)])]
    pallas_call x1, Pallas kernels: 5.47 us -> 6.48 us  [body(): call(attend_kernel, 'attend', (shape(few, 128), shape(rows, 128), shape(f...]
  transfers between devices with their start and end apart: 19 -> 19, of which waited for: 11 -> 12; matrix products, arithmetic and copies ran while one was open for 0% -> 0% of each run, Pallas kernels for 15% -> 20%
where the time goes in v5:
time: 89 us; the launch traced here: 88.6 us
  starting transfers between devices  39.8 us (45%)
  waiting for transfers between devices  25.5 us (29%)
  Pallas kernels  20.5 us (23%)
  local copies, waits for them, and re-layouts  1.87 us (2%)
    ppermute x12, waiting for transfers between devices, crossed(): lax.ppermute(values[bits], 'zz', [(i, i ^ bits) for i in range(size)])  21.3 us
    all_to_all x2, starting transfers between devices, exchange(): return lax.all_to_all(value, axes, split_axis=0, concat_axis=0, tiled=True)  18.1 us
    ppermute x12, starting transfers between devices, crossed(): lax.ppermute(values[bits], 'zz', [(i, i ^ bits) for i in range(size)])  15.1 us
    ppermute x5, starting transfers between devices, swapped(): return lax.ppermute(value, 'cc', [(0, 1), (1, 0)])  6.61 us
    pallas_call x1, Pallas kernels, body(): call(attend_kernel, 'attend', (shape(few, 128), shape(rows, 128), shape(f...  6.48 us
    ppermute x5, waiting for transfers between devices, swapped(): return lax.ppermute(value, 'cc', [(0, 1), (1, 0)])  3.69 us
    pallas_call x1, Pallas kernels, body(): call(project_kernel, 'project', (shape(few, width), shape(share, width)),...  2.72 us
    pallas_call x1, Pallas kernels, body(): call(pack_rest_kernel, 'pack_rest', shape(copies, cores, twins, depth, un...  2.1 us
  transfers between devices with their start and end apart: 19, of which 12 were waited for; matrix products, arithmetic and copies ran while one was open for 0% of the time, Pallas kernels for 20%

profile of v5, /device:TPU:1, one launch (start us, length us, event | category | flops | bytes accessed | tf_op | source)
XLA Modules:
  0.0 88.6 jit_solution(13785430842443380254)
XLA Ops:
  0.6 1.5 %collective-permute-start.3 = (bf16[512,1024]{1,0:T(8,128)(2,1)}, bf16[512,1024]{1,0:T(8,128)(2,1)S(1)}, u32[]{:S(2)}, u32[]{:S(2)}) collective-permute-start(bf16[512,1024]{1,0:T(8,128)(2,1)} %refs_6_.1), channel_id=1, source_target_pairs={{0,8},{8,0},{1,9},{9,1},{2,10},{10,2},{3,11},{11,3},{4,12},{12,4},... | collective-permute-start | bytes 3145736 | tf_op jit(solution)/shard_map/ppermute | solution.py:267
  2.1 2.0 %pack_first.1 = bf16[8,2,4,2,8,512]{5,4,3,2,1,0:T(8,128)(2,1)} custom-call(f32[8,3072]{1,0:T(8,128)} %qkv_ref.1, f32[8,1024]{1,0:T(8,128)} %out_ref.1), custom_call_target="tpu_custom_call" | custom-call | bytes 1048576 | tf_op jit(solution)/shard_map/pack_first/pallas_call | solution.py:297
  4.2 10.2 %all-to-all-start = ((bf16[128,8,512]{2,1,0:T(8,128)(2,1)}), bf16[128,8,512]{2,1,0:T(8,128)(2,1)S(1)}, u32[]{:S(2)}, u32[]{:S(2)}) async-start(bf16[128,8,512]{2,1,0:T(8,128)(2,1)} %bitcast.3), calls=%async_computation | async-start | bytes 2097152 | tf_op jit(solution)/shard_map/all_to_all | solution.py:263
  14.4 1.0 %pack_depth.1 = (bf16[8,2048]{1,0:T(8,128)(2,1)S(1)}, bf16[8,2048]{1,0:T(8,128)(2,1)S(1)}, bf16[8,2048]{1,0:T(8,128)(2,1)S(1)}, bf16[8,2048]{1,0:T(8,128)(2,1)S(1)}) custom-call(s32[3]{0:T(128)S(1)} %pad_add_fusion.place_ref, f32[8,4096]{1,0:T(8,128)} %up_ref.1, f32[8,4096]{1,0:T(8,128)} %down_ref.1), custom_call_target="tpu_custom_call" | custom-call | bytes 1048576 | tf_op jit(solution)/shard_map/pack_depth/pallas_call | solution.py:301
  15.4 1.6 %collective-permute-start = (bf16[8,2048]{1,0:T(8,128)(2,1)S(1)}, bf16[8,2048]{1,0:T(8,128)(2,1)S(1)}, u32[]{:S(2)}, u32[]{:S(2)}) collective-permute-start(bf16[8,2048]{1,0:T(8,128)(2,1)S(1)} %get-tuple-element.38), channel_id=1, source_target_pairs={{0,2},{2,0},{4,6},{6,4},{1,3},{3,1},{5,7},{7,5},{8,10},{10,8},{12,... | collective-permute-start | bytes 98312 | tf_op jit(solution)/shard_map/ppermute | solution.py:272
  17.0 2.9 %collective-permute-start.1 = (bf16[8,2048]{1,0:T(8,128)(2,1)S(1)}, bf16[8,2048]{1,0:T(8,128)(2,1)S(1)}, u32[]{:S(2)}, u32[]{:S(2)}) collective-permute-start(bf16[8,2048]{1,0:T(8,128)(2,1)S(1)} %get-tuple-element.39), channel_id=1, source_target_pairs={{0,4},{2,6},{4,0},{6,2},{1,5},{3,7},{5,1},{7,3},{8,12},{10,14},{12... | collective-permute-start | bytes 98312 | tf_op jit(solution)/shard_map/ppermute | solution.py:272
  20.0 1.3 %collective-permute-start.4 = (s32[512]{0:T(512)S(1)}, s32[512]{0:T(512)S(1)}, u32[]{:S(2)}, u32[]{:S(2)}) collective-permute-start(s32[512]{0:T(512)S(1)} %copy-done.4), channel_id=1, source_target_pairs={{0,8},{8,0},{1,9},{9,1},{2,10},{10,2},{3,11},{11,3},{4,12},{12,4},... | collective-permute-start | bytes 6152 | tf_op jit(solution)/shard_map/ppermute | solution.py:267
  22.6 7.5 %collective-permute-done.1.refs_2_ = bf16[8,2048]{1,0:T(8,128)(2,1)S(1)} collective-permute-done((bf16[8,2048]{1,0:T(8,128)(2,1)S(1)}, bf16[8,2048]{1,0:T(8,128)(2,1)S(1)}, u32[]{:S(2)}, u32[]{:S(2)}) %collective-permute-start.1) | collective-permute-done | bytes 32800 | tf_op jit(solution)/shard_map/ppermute | solution.py:272
  30.0 2.1 %pack_rest.1 = bf16[8,2,2,4,8,1024]{5,4,3,2,1,0:T(8,128)(2,1)} custom-call(s32[3]{0:T(128)S(1)} %pad_add_fusion.place_ref, bf16[8,2048]{1,0:T(8,128)(2,1)S(1)} %get-tuple-element.41.refs_0_, bf16[8,2048]{1,0:T(8,128)(2,1)S(1)} %collective-permute-done.refs_1_, bf16[8,2048]{1,0:T(8,128)(2,1)S(1)} %collective-permute-done.1.refs_2_, ...), custom_call_target="tpu_custom_call" | custom-call | bytes 1048576 | tf_op jit(solution)/shard_map/pack_rest/pallas_call | solution.py:303
  32.6 7.9 %all-to-all-start.1 = ((bf16[32,4,8,1024]{3,2,1,0:T(8,128)(2,1)}), bf16[32,4,8,1024]{3,2,1,0:T(8,128)(2,1)S(1)}, u32[]{:S(2)}, u32[]{:S(2)}) async-start(bf16[32,4,8,1024]{3,2,1,0:T(8,128)(2,1)} %bitcast.5), calls=%async_computation.1 | async-start | bytes 4194304 | tf_op jit(solution)/shard_map/all_to_all | solution.py:263
  41.3 1.6 %collective-permute-start.6 = (bf16[1024,128]{1,0:T(8,128)(2,1)S(1)}, bf16[1024,128]{1,0:T(8,128)(2,1)S(1)}, u32[]{:S(2)}, u32[]{:S(2)}) collective-permute-start(bf16[1024,128]{1,0:T(8,128)(2,1)S(1)} %take.1.refs_0_), channel_id=1, source_target_pairs={{0,4},{2,6},{4,0},{6,2},{1,5},{3,7},{5,1},{7,3},{8,12},{10,14},{12... | collective-permute-start | bytes 786440 | tf_op jit(solution)/shard_map/ppermute | solution.py:272
  42.9 1.1 %collective-permute-start.5 = (bf16[1024,128]{1,0:T(8,128)(2,1)S(1)}, bf16[1024,128]{1,0:T(8,128)(2,1)S(1)}, u32[]{:S(2)}, u32[]{:S(2)}) collective-permute-start(bf16[1024,128]{1,0:T(8,128)(2,1)S(1)} %take.1.refs_0_), channel_id=1, source_target_pairs={{0,2},{2,0},{4,6},{6,4},{1,3},{3,1},{5,7},{7,5},{8,10},{10,8},{12,... | collective-permute-start | bytes 786440 | tf_op jit(solution)/shard_map/ppermute | solution.py:272
  44.0 6.5 %attend.1 = (bf16[256,128]{1,0:T(8,128)(2,1)S(1)}, bf16[512,128]{1,0:T(8,128)(2,1)S(1)}, bf16[768,128]{1,0:T(8,128)(2,1)S(1)}) custom-call(s32[3]{0:T(128)S(1)} %pad_add_fusion.place_ref, bf16[512,1024]{1,0:T(8,128)(2,1)} %refs_6_.1, bf16[512,1024]{1,0:T(8,128)(2,1)} %copy-done.7, bf16[1024,512]{1,0:T(8,128)(2,1)S(1)} %bitcast.14, s32[4,128]{1,0:T(4,128)S(1)} %bitcast.21, ...), custom_call_target="tpu_custom_call" | custom-call | flops 5000000000 | bytes 1048576 | tf_op jit(solution)/shard_map/attend/pallas_call | solution.py:311
  50.5 1.2 %collective-permute-start.8 = (bf16[768,128]{1,0:T(8,128)(2,1)S(1)}, bf16[768,128]{1,0:T(8,128)(2,1)S(1)}, u32[]{:S(2)}, u32[]{:S(2)}) collective-permute-start(bf16[768,128]{1,0:T(8,128)(2,1)S(1)} %get-tuple-element.49), channel_id=1, source_target_pairs={{0,8},{8,0},{1,9},{9,1},{2,10},{10,2},{3,11},{11,3},{4,12},{12,4},... | collective-permute-start | bytes 589832 | tf_op jit(solution)/shard_map/ppermute | solution.py:267
  51.6 1.1 %collective-permute-done.8.got_ref = bf16[768,128]{1,0:T(8,128)(2,1)S(1)} collective-permute-done((bf16[768,128]{1,0:T(8,128)(2,1)S(1)}, bf16[768,128]{1,0:T(8,128)(2,1)S(1)}, u32[]{:S(2)}, u32[]{:S(2)}) %collective-permute-start.8) | collective-permute-done | bytes 196640 | tf_op jit(solution)/shard_map/ppermute | solution.py:267
  53.3 1.9 %collective-permute-done.7.refs_3_ = bf16[1024,128]{1,0:T(8,128)(2,1)S(1)} collective-permute-done((bf16[1024,128]{1,0:T(8,128)(2,1)S(1)}, bf16[1024,128]{1,0:T(8,128)(2,1)S(1)}, u32[]{:S(2)}, u32[]{:S(2)}) %collective-permute-start.7) | collective-permute-done | bytes 262176 | tf_op jit(solution)/shard_map/ppermute | solution.py:272
  56.3 1.4 %collective-permute-start.12 = (bf16[1024,512]{1,0:T(8,128)(2,1)S(1)}, bf16[1024,512]{1,0:T(8,128)(2,1)S(1)}, u32[]{:S(2)}, u32[]{:S(2)}) collective-permute-start(bf16[1024,512]{1,0:T(8,128)(2,1)S(1)} %assemble.1.refs_4_), channel_id=1, source_target_pairs={{0,8},{8,0},{1,9},{9,1},{2,10},{10,2},{3,11},{11,3},{4,12},{12,4},... | collective-permute-start | bytes 3145736 | tf_op jit(solution)/shard_map/ppermute | solution.py:267
  58.3 1.6 %collective-permute-start.10 = (bf16[256,256]{1,0:T(8,128)(2,1)S(1)}, bf16[256,256]{1,0:T(8,128)(2,1)S(1)}, u32[]{:S(2)}, u32[]{:S(2)}) collective-permute-start(bf16[256,256]{1,0:T(8,128)(2,1)S(1)} %join.1.refs_0_), channel_id=1, source_target_pairs={{0,4},{2,6},{4,0},{6,2},{1,5},{3,7},{5,1},{7,3},{8,12},{10,14},{12... | collective-permute-start | bytes 393224 | tf_op jit(solution)/shard_map/ppermute | solution.py:272
  59.9 1.1 %collective-permute-start.9 = (bf16[256,256]{1,0:T(8,128)(2,1)S(1)}, bf16[256,256]{1,0:T(8,128)(2,1)S(1)}, u32[]{:S(2)}, u32[]{:S(2)}) collective-permute-start(bf16[256,256]{1,0:T(8,128)(2,1)S(1)} %join.1.refs_0_), channel_id=1, source_target_pairs={{0,2},{2,0},{4,6},{6,4},{1,3},{3,1},{5,7},{7,5},{8,10},{10,8},{12,... | collective-permute-start | bytes 393224 | tf_op jit(solution)/shard_map/ppermute | solution.py:272
  61.0 5.8 %collective-permute-done.11.refs_3_ = bf16[256,256]{1,0:T(8,128)(2,1)S(1)} collective-permute-done((bf16[256,256]{1,0:T(8,128)(2,1)S(1)}, bf16[256,256]{1,0:T(8,128)(2,1)S(1)}, u32[]{:S(2)}, u32[]{:S(2)}) %collective-permute-start.11) | collective-permute-done | bytes 131104 | tf_op jit(solution)/shard_map/ppermute | solution.py:272
  67.1 2.7 %project.1 = (bf16[256,1024]{1,0:T(8,128)(2,1)S(1)}, bf16[64,1024]{1,0:T(8,128)(2,1)S(1)}) custom-call(s32[3]{0:T(128)S(1)} %pad_add_fusion.place_ref, bf16[256,256]{1,0:T(8,128)(2,1)S(1)} %join.1.refs_0_, bf16[256,256]{1,0:T(8,128)(2,1)S(1)} %collective-permute-done.9.refs_1_, bf16[256,256]{1,0:T(8,128)(2,1)S(1)} %collective-permute-done.10.refs_2_, ...), custom_call_target="tpu_custom_call" | custom-call | flops 2000000000 | bytes 1048576 | tf_op jit(solution)/shard_map/project/pallas_call | solution.py:332
  70.6 1.2 %collective-permute-start.13 = (bf16[1024,1024]{1,0:T(8,128)(2,1)S(1)}, bf16[1024,1024]{1,0:T(8,128)(2,1)S(1)}, u32[]{:S(2)}, u32[]{:S(2)}) collective-permute-start(bf16[1024,1024]{1,0:T(8,128)(2,1)S(1)} %bitcast.15), channel_id=1, source_target_pairs={{0,8},{8,0},{1,9},{9,1},{2,10},{10,2},{3,11},{11,3},{4,12},{12,4},... | collective-permute-start | bytes 6291464 | tf_op jit(solution)/shard_map/ppermute | solution.py:267
  71.8 1.0 %copy-done.6 = bf16[256,1024]{1,0:T(8,128)(2,1)S(1)} copy-done((bf16[256,1024]{1,0:T(8,128)(2,1)S(1)}, bf16[256,1024]{1,0:T(8,128)(2,1)}, u32[]{:S(2)}) %copy-start.6) | copy-done | bytes 524312
  72.8 0.9 %own_feed.1 = (bf16[256,1024]{1,0:T(8,128)(2,1)S(1)}, f32[256,1024]{1,0:T(8,128)S(1)}) custom-call(bf16[256,1024]{1,0:T(8,128)(2,1)S(1)} %copy-done.6, bf16[1024,1024]{1,0:T(8,128)(2,1)S(1)} %bitcast.16), custom_call_target="tpu_custom_call" | custom-call | flops 2000000000 | bytes 1048576 | tf_op jit(solution)/shard_map/own_feed/pallas_call | solution.py:343
  73.8 1.8 %collective-permute-done.13.theirs_ref = bf16[1024,1024]{1,0:T(8,128)(2,1)S(1)} collective-permute-done((bf16[1024,1024]{1,0:T(8,128)(2,1)S(1)}, bf16[1024,1024]{1,0:T(8,128)(2,1)S(1)}, u32[]{:S(2)}, u32[]{:S(2)}) %collective-permute-start.13) | collective-permute-done | bytes 2097184 | tf_op jit(solution)/shard_map/ppermute | solution.py:267
  75.6 1.6 %feed.1 = (bf16[64,1024]{1,0:T(8,128)(2,1)S(1)}, bf16[64,1024]{1,0:T(8,128)(2,1)S(1)}, bf16[64,1024]{1,0:T(8,128)(2,1)S(1)}, bf16[64,1024]{1,0:T(8,128)(2,1)S(1)}) custom-call(s32[3]{0:T(128)S(1)} %pad_add_fusion.place_ref, bf16[256,1024]{1,0:T(8,128)(2,1)S(1)} %get-tuple-element.60.arrived_ref, f32[256,1024]{1,0:T(8,128)S(1)} %get-tuple-element.61.own_ref, ...), custom_call_target="tpu_custom_call" | custom-call | flops 3000000000 | bytes 1048576 | tf_op jit(solution)/shard_map/feed/pallas_call | solution.py:351
  77.6 1.4 %collective-permute-start.15 = (bf16[64,1024]{1,0:T(8,128)(2,1)S(1)}, bf16[64,1024]{1,0:T(8,128)(2,1)S(1)}, u32[]{:S(2)}, u32[]{:S(2)}) collective-permute-start(bf16[64,1024]{1,0:T(8,128)(2,1)S(1)} %get-tuple-element.64), channel_id=1, source_target_pairs={{0,4},{2,6},{4,0},{6,2},{1,5},{3,7},{5,1},{7,3},{8,12},{10,14},{12... | collective-permute-start | bytes 393224 | tf_op jit(solution)/shard_map/ppermute | solution.py:272
  79.1 2.1 %collective-permute-start.16 = (bf16[64,1024]{1,0:T(8,128)(2,1)S(1)}, bf16[64,1024]{1,0:T(8,128)(2,1)S(1)}, u32[]{:S(2)}, u32[]{:S(2)}) collective-permute-start(bf16[64,1024]{1,0:T(8,128)(2,1)S(1)} %get-tuple-element.65), channel_id=1, source_target_pairs={{0,6},{2,4},{4,2},{6,0},{1,7},{3,5},{5,3},{7,1},{8,14},{10,12},{12... | collective-permute-start | bytes 393224 | tf_op jit(solution)/shard_map/ppermute | solution.py:272
  81.1 1.4 %cache.1 = (bf16[512,128]{1,0:T(8,128)(2,1)}, bf16[512,128]{1,0:T(8,128)(2,1)}) custom-call(s32[3]{0:T(128)S(1)} %pad_add_fusion.place_ref, bf16[512,128]{1,0:T(8,128)(2,1)S(1)} %get-tuple-element.67.own_ref, bf16[768,128]{1,0:T(8,128)(2,1)S(1)} %collective-permute-done.8.got_ref), custom_call_target="tpu_custom_call" | custom-call | flops 1000000000 | bytes 1048576 | tf_op jit(solution)/shard_map/cache/pallas_call | solution.py:329
  82.5 2.7 %collective-permute-done.15.refs_2_ = bf16[64,1024]{1,0:T(8,128)(2,1)S(1)} collective-permute-done((bf16[64,1024]{1,0:T(8,128)(2,1)S(1)}, bf16[64,1024]{1,0:T(8,128)(2,1)S(1)}, u32[]{:S(2)}, u32[]{:S(2)}) %collective-permute-start.15) | collective-permute-done | bytes 131104 | tf_op jit(solution)/shard_map/ppermute | solution.py:272
  85.2 2.5 %collective-permute-done.16.refs_3_ = bf16[64,1024]{1,0:T(8,128)(2,1)S(1)} collective-permute-done((bf16[64,1024]{1,0:T(8,128)(2,1)S(1)}, bf16[64,1024]{1,0:T(8,128)(2,1)S(1)}, u32[]{:S(2)}, u32[]{:S(2)}) %collective-permute-start.16) | collective-permute-done | bytes 131104 | tf_op jit(solution)/shard_map/ppermute | solution.py:272
  87.6 0.9 %final.1 = bf16[64,1024]{1,0:T(8,128)(2,1)} custom-call(bf16[64,1024]{1,0:T(8,128)(2,1)S(1)} %get-tuple-element.62.refs_0_, bf16[64,1024]{1,0:T(8,128)(2,1)S(1)} %collective-permute-done.14.refs_1_, bf16[64,1024]{1,0:T(8,128)(2,1)S(1)} %collective-permute-done.15.refs_2_, bf16[64,1024]{1,0:T(8,128)(2,1)S(1)} %collective-permute-done.16.refs_3_, ...), custom_call_target="tpu_custom_call" | custom-call | bytes 1048576 | tf_op jit(solution)/shard_map/final/pallas_call | solution.py:361
  (35 shorter events, 6.5 us)
Async XLA Ops:
  0.6 19.3 %copy-start.4 = (s32[512]{0:T(512)S(1)}, s32[512]{0:T(512)}, u32[]{:S(2)}) copy-start(s32[512]{0:T(512)} %param.11) | copy-start | bytes 6148
  0.6 29.4 %collective-permute-start.3 = (bf16[512,1024]{1,0:T(8,128)(2,1)}, bf16[512,1024]{1,0:T(8,128)(2,1)S(1)}, u32[]{:S(2)}, u32[]{:S(2)}) collective-permute-start(bf16[512,1024]{1,0:T(8,128)(2,1)} %refs_6_.1), channel_id=1, source_target_pairs={{0,8},{8,0},{1,9},{9,1},{2,10},{10,2},{3,11},{11,3},{4,12},{12,4},... | collective-permute-start | bytes 3145736 | tf_op jit(solution)/shard_map/ppermute | solution.py:267
  4.2 28.5 %all-to-all-start = ((bf16[128,8,512]{2,1,0:T(8,128)(2,1)}), bf16[128,8,512]{2,1,0:T(8,128)(2,1)S(1)}, u32[]{:S(2)}, u32[]{:S(2)}) async-start(bf16[128,8,512]{2,1,0:T(8,128)(2,1)} %bitcast.3), calls=%async_computation | async-start | bytes 2097152 | tf_op jit(solution)/shard_map/all_to_all | solution.py:263
  15.4 7.1 %collective-permute-start = (bf16[8,2048]{1,0:T(8,128)(2,1)S(1)}, bf16[8,2048]{1,0:T(8,128)(2,1)S(1)}, u32[]{:S(2)}, u32[]{:S(2)}) collective-permute-start(bf16[8,2048]{1,0:T(8,128)(2,1)S(1)} %get-tuple-element.38), channel_id=1, source_target_pairs={{0,2},{2,0},{4,6},{6,4},{1,3},{3,1},{5,7},{7,5},{8,10},{10,8},{12,... | collective-permute-start | bytes 98312 | tf_op jit(solution)/shard_map/ppermute | solution.py:272
  17.0 13.0 %collective-permute-start.1 = (bf16[8,2048]{1,0:T(8,128)(2,1)S(1)}, bf16[8,2048]{1,0:T(8,128)(2,1)S(1)}, u32[]{:S(2)}, u32[]{:S(2)}) collective-permute-start(bf16[8,2048]{1,0:T(8,128)(2,1)S(1)} %get-tuple-element.39), channel_id=1, source_target_pairs={{0,4},{2,6},{4,0},{6,2},{1,5},{3,7},{5,1},{7,3},{8,12},{10,14},{12... | collective-permute-start | bytes 98312 | tf_op jit(solution)/shard_map/ppermute | solution.py:272
  20.0 10.1 %collective-permute-start.2 = (bf16[8,2048]{1,0:T(8,128)(2,1)S(1)}, bf16[8,2048]{1,0:T(8,128)(2,1)S(1)}, u32[]{:S(2)}, u32[]{:S(2)}) collective-permute-start(bf16[8,2048]{1,0:T(8,128)(2,1)S(1)} %get-tuple-element.40), channel_id=1, source_target_pairs={{0,6},{2,4},{4,2},{6,0},{1,7},{3,5},{5,3},{7,1},{8,14},{10,12},{12... | collective-permute-start | bytes 98312 | tf_op jit(solution)/shard_map/ppermute | solution.py:272
  20.0 2.1 %collective-permute-start.4 = (s32[512]{0:T(512)S(1)}, s32[512]{0:T(512)S(1)}, u32[]{:S(2)}, u32[]{:S(2)}) collective-permute-start(s32[512]{0:T(512)S(1)} %copy-done.4), channel_id=1, source_target_pairs={{0,8},{8,0},{1,9},{9,1},{2,10},{10,2},{3,11},{11,3},{4,12},{12,4},... | collective-permute-start | bytes 6152 | tf_op jit(solution)/shard_map/ppermute | solution.py:267
  30.0 2.6 %copy-start.7 = (bf16[512,1024]{1,0:T(8,128)(2,1)}, bf16[512,1024]{1,0:T(8,128)(2,1)S(1)}, u32[]{:S(2)}) copy-start(bf16[512,1024]{1,0:T(8,128)(2,1)S(1)} %collective-permute-done.3.other_hbm) | copy-start | bytes 3145732
  32.6 38.0 %all-to-all-start.1 = ((bf16[32,4,8,1024]{3,2,1,0:T(8,128)(2,1)}), bf16[32,4,8,1024]{3,2,1,0:T(8,128)(2,1)S(1)}, u32[]{:S(2)}, u32[]{:S(2)}) async-start(bf16[32,4,8,1024]{3,2,1,0:T(8,128)(2,1)} %bitcast.5), calls=%async_computation.1 | async-start | bytes 4194304 | tf_op jit(solution)/shard_map/all_to_all | solution.py:263
  40.6 14.6 %collective-permute-start.7 = (bf16[1024,128]{1,0:T(8,128)(2,1)S(1)}, bf16[1024,128]{1,0:T(8,128)(2,1)S(1)}, u32[]{:S(2)}, u32[]{:S(2)}) collective-permute-start(bf16[1024,128]{1,0:T(8,128)(2,1)S(1)} %take.1.refs_0_), channel_id=1, source_target_pairs={{0,6},{2,4},{4,2},{6,0},{1,7},{3,5},{5,3},{7,1},{8,14},{10,12},{12... | collective-permute-start | bytes 786440 | tf_op jit(solution)/shard_map/ppermute | solution.py:272
  41.3 13.9 %collective-permute-start.6 = (bf16[1024,128]{1,0:T(8,128)(2,1)S(1)}, bf16[1024,128]{1,0:T(8,128)(2,1)S(1)}, u32[]{:S(2)}, u32[]{:S(2)}) collective-permute-start(bf16[1024,128]{1,0:T(8,128)(2,1)S(1)} %take.1.refs_0_), channel_id=1, source_target_pairs={{0,4},{2,6},{4,0},{6,2},{1,5},{3,7},{5,1},{7,3},{8,12},{10,14},{12... | collective-permute-start | bytes 786440 | tf_op jit(solution)/shard_map/ppermute | solution.py:272
  42.9 12.6 %collective-permute-start.5 = (bf16[1024,128]{1,0:T(8,128)(2,1)S(1)}, bf16[1024,128]{1,0:T(8,128)(2,1)S(1)}, u32[]{:S(2)}, u32[]{:S(2)}) collective-permute-start(bf16[1024,128]{1,0:T(8,128)(2,1)S(1)} %take.1.refs_0_), channel_id=1, source_target_pairs={{0,2},{2,0},{4,6},{6,4},{1,3},{3,1},{5,7},{7,5},{8,10},{10,8},{12,... | collective-permute-start | bytes 786440 | tf_op jit(solution)/shard_map/ppermute | solution.py:272
  50.4 16.6 %copy-start.2 = (f32[1024]{0:T(1024)S(1)}, f32[1024]{0:T(1024)}, u32[]{:S(2)}) copy-start(f32[1024]{0:T(1024)} %param.16) | copy-start | bytes 12292
  50.5 16.6 %copy-start.3 = (f32[1024]{0:T(1024)S(1)}, f32[1024]{0:T(1024)}, u32[]{:S(2)}) copy-start(f32[1024]{0:T(1024)} %param.17) | copy-start | bytes 12292
  50.5 2.2 %collective-permute-start.8 = (bf16[768,128]{1,0:T(8,128)(2,1)S(1)}, bf16[768,128]{1,0:T(8,128)(2,1)S(1)}, u32[]{:S(2)}, u32[]{:S(2)}) collective-permute-start(bf16[768,128]{1,0:T(8,128)(2,1)S(1)} %get-tuple-element.49), channel_id=1, source_target_pairs={{0,8},{8,0},{1,9},{9,1},{2,10},{10,2},{3,11},{11,3},{4,12},{12,4},... | collective-permute-start | bytes 589832 | tf_op jit(solution)/shard_map/ppermute | solution.py:267
  56.3 10.8 %collective-permute-start.12 = (bf16[1024,512]{1,0:T(8,128)(2,1)S(1)}, bf16[1024,512]{1,0:T(8,128)(2,1)S(1)}, u32[]{:S(2)}, u32[]{:S(2)}) collective-permute-start(bf16[1024,512]{1,0:T(8,128)(2,1)S(1)} %assemble.1.refs_4_), channel_id=1, source_target_pairs={{0,8},{8,0},{1,9},{9,1},{2,10},{10,2},{3,11},{11,3},{4,12},{12,4},... | collective-permute-start | bytes 3145736 | tf_op jit(solution)/shard_map/ppermute | solution.py:267
  57.7 9.1 %collective-permute-start.11 = (bf16[256,256]{1,0:T(8,128)(2,1)S(1)}, bf16[256,256]{1,0:T(8,128)(2,1)S(1)}, u32[]{:S(2)}, u32[]{:S(2)}) collective-permute-start(bf16[256,256]{1,0:T(8,128)(2,1)S(1)} %join.1.refs_0_), channel_id=1, source_target_pairs={{0,6},{2,4},{4,2},{6,0},{1,7},{3,5},{5,3},{7,1},{8,14},{10,12},{12... | collective-permute-start | bytes 393224 | tf_op jit(solution)/shard_map/ppermute | solution.py:272
  58.3 8.5 %collective-permute-start.10 = (bf16[256,256]{1,0:T(8,128)(2,1)S(1)}, bf16[256,256]{1,0:T(8,128)(2,1)S(1)}, u32[]{:S(2)}, u32[]{:S(2)}) collective-permute-start(bf16[256,256]{1,0:T(8,128)(2,1)S(1)} %join.1.refs_0_), channel_id=1, source_target_pairs={{0,4},{2,6},{4,0},{6,2},{1,5},{3,7},{5,1},{7,3},{8,12},{10,14},{12... | collective-permute-start | bytes 393224 | tf_op jit(solution)/shard_map/ppermute | solution.py:272
  59.9 7.2 %collective-permute-start.9 = (bf16[256,256]{1,0:T(8,128)(2,1)S(1)}, bf16[256,256]{1,0:T(8,128)(2,1)S(1)}, u32[]{:S(2)}, u32[]{:S(2)}) collective-permute-start(bf16[256,256]{1,0:T(8,128)(2,1)S(1)} %join.1.refs_0_), channel_id=1, source_target_pairs={{0,2},{2,0},{4,6},{6,4},{1,3},{3,1},{5,7},{7,5},{8,10},{10,8},{12,... | collective-permute-start | bytes 393224 | tf_op jit(solution)/shard_map/ppermute | solution.py:272
  69.8 0.8 copy-start.5
  70.6 5.0 %collective-permute-start.13 = (bf16[1024,1024]{1,0:T(8,128)(2,1)S(1)}, bf16[1024,1024]{1,0:T(8,128)(2,1)S(1)}, u32[]{:S(2)}, u32[]{:S(2)}) collective-permute-start(bf16[1024,1024]{1,0:T(8,128)(2,1)S(1)} %bitcast.15), channel_id=1, source_target_pairs={{0,8},{8,0},{1,9},{9,1},{2,10},{10,2},{3,11},{11,3},{4,12},{12,4},... | collective-permute-start | bytes 6291464 | tf_op jit(solution)/shard_map/ppermute | solution.py:267
  71.8 1.0 %copy-start.6 = (bf16[256,1024]{1,0:T(8,128)(2,1)S(1)}, bf16[256,1024]{1,0:T(8,128)(2,1)}, u32[]{:S(2)}) copy-start(bf16[256,1024]{1,0:T(8,128)(2,1)} %copy-done.5) | copy-start | bytes 1572868
  77.2 10.5 %copy-start = (f32[1024]{0:T(1024)S(1)}, f32[1024]{0:T(1024)}, u32[]{:S(2)}) copy-start(f32[1024]{0:T(1024)} %param.18) | copy-start | bytes 12292
  77.2 10.5 %copy-start.1 = (f32[1024]{0:T(1024)S(1)}, f32[1024]{0:T(1024)}, u32[]{:S(2)}) copy-start(f32[1024]{0:T(1024)} %param.19) | copy-start | bytes 12292
  77.2 5.3 %collective-permute-start.14 = (bf16[64,1024]{1,0:T(8,128)(2,1)S(1)}, bf16[64,1024]{1,0:T(8,128)(2,1)S(1)}, u32[]{:S(2)}, u32[]{:S(2)}) collective-permute-start(bf16[64,1024]{1,0:T(8,128)(2,1)S(1)} %get-tuple-element.63), channel_id=1, source_target_pairs={{0,2},{2,0},{4,6},{6,4},{1,3},{3,1},{5,7},{7,5},{8,10},{10,8},{12,... | collective-permute-start | bytes 393224 | tf_op jit(solution)/shard_map/ppermute | solution.py:272
  77.6 7.5 %collective-permute-start.15 = (bf16[64,1024]{1,0:T(8,128)(2,1)S(1)}, bf16[64,1024]{1,0:T(8,128)(2,1)S(1)}, u32[]{:S(2)}, u32[]{:S(2)}) collective-permute-start(bf16[64,1024]{1,0:T(8,128)(2,1)S(1)} %get-tuple-element.64), channel_id=1, source_target_pairs={{0,4},{2,6},{4,0},{6,2},{1,5},{3,7},{5,1},{7,3},{8,12},{10,14},{12... | collective-permute-start | bytes 393224 | tf_op jit(solution)/shard_map/ppermute | solution.py:272
  79.1 8.6 %collective-permute-start.16 = (bf16[64,1024]{1,0:T(8,128)(2,1)S(1)}, bf16[64,1024]{1,0:T(8,128)(2,1)S(1)}, u32[]{:S(2)}, u32[]{:S(2)}) collective-permute-start(bf16[64,1024]{1,0:T(8,128)(2,1)S(1)} %get-tuple-element.65), channel_id=1, source_target_pairs={{0,6},{2,4},{4,2},{6,0},{1,7},{3,5},{5,3},{7,1},{8,14},{10,12},{12... | collective-permute-start | bytes 393224 | tf_op jit(solution)/shard_map/ppermute | solution.py:272

commit v6 on v5

--- a/solution.py
+++ b/solution.py
@@ -1,3 +1,5 @@
+import functools
+
 import jax
 import jax.numpy as jnp
 from jax import lax
@@ -47,10 +49,21 @@
     return jnp.concatenate(tiles, axis=1)
 
 
-def pack_first_kernel(qkv_ref, out_ref, packed_ref):
+def replicate(row_scr, packed_hbm, sems, twin_at):
+    copies = []
+    for copy in range(packed_hbm.shape[0]):
+        for twin in range(packed_hbm.shape[twin_at]):
+            target = packed_hbm.at[copy, :, :, twin] if twin_at == 3 else packed_hbm.at[copy, :, twin]
+            copies.append(pltpu.make_async_copy(row_scr, target, sems.at[copy, twin]))
+            copies[-1].start()
+    for copy in copies:
+        copy.wait()
+
+
+def pack_first_kernel(qkv_ref, out_ref, packed_ref, row_scr, sems):
     rows = qkv_ref.shape[0]
     width = qkv_ref.shape[1] // 3
-    copies, cores, depth, twins = packed_ref.shape[:4]
+    cores, depth = row_scr.shape[:2]
     low = low_lanes((rows, 128))
 
     def tile(kind, number):
@@ -72,10 +85,8 @@
                 parts.append(jnp.where(low, one, turned(two)))
             else:
                 parts.append(jnp.where(low, turned(one), two))
-            row = jnp.concatenate(parts, axis=1).astype(BF)
-            for copy in range(copies):
-                for twin in range(twins):
-                    packed_ref[copy, core, z, twin] = row
+            row_scr[core, z] = jnp.concatenate(parts, axis=1).astype(BF)
+    replicate(row_scr, packed_ref, sems, 3)
 
 
 def pack_depth_kernel(place_ref, up_ref, down_ref, *piece_refs):
@@ -88,29 +99,20 @@
 
 
 def pack_rest_kernel(place_ref, *refs):
-    *piece_refs, packed_ref = refs
-    copies, cores, twins = packed_ref.shape[:3]
-    half_h = packed_ref.shape[5] // 2
+    *piece_refs, packed_ref, row_scr, sems = refs
+    cores = row_scr.shape[0]
+    half_h = row_scr.shape[3] // 2
     for bits, piece_ref in enumerate(piece_refs):
         z = place_ref[DEEP] ^ bits
         span = piece_ref.shape[1] // 2
         for core in range(cores):
             start = core * half_h
-            row = jnp.concatenate([piece_ref[:, start : start + half_h], piece_ref[:, span + start : span + start + half_h]], axis=1)
-            for copy in range(copies):
-                for twin in range(twins):
-                    packed_ref[copy, core, twin, z] = row
+            row_scr[core, z] = jnp.concatenate([piece_ref[:, start : start + half_h], piece_ref[:, span + start : span + start + half_h]], axis=1)
+    replicate(row_scr, packed_ref, sems, 2)
 
 
 def take_kernel(served_ref, part_ref):
     part_ref[...] = served_ref[...]
-
-
-def assemble_kernel(place_ref, *refs):
-    *part_refs, whole_ref = refs
-    for bits, part_ref in enumerate(part_refs):
-        lanes = pl.ds(pl.multiple_of((place_ref[DEEP] ^ bits) * 128, 128), 128)
-        whole_ref[:, lanes] = part_ref[...]
 
 
 def attend_kernel(place_ref, own_hbm, other_hbm, weight_ref, own_ids_ref, other_ids_ref, att_ref, kv_ref, send_ref, x_scr, q_scr, k_scr, v_scr, id_scr, sems):
@@ -194,8 +196,9 @@
 
 
 def project_kernel(place_ref, *refs):
-    (*piece_refs, mine_ref, theirs_ref, x_hbm, gain_ref, shift_ref, norm_ref, keep_ref, att_scr, x_ref, sems) = refs
-    depth = len(piece_refs)
+    (*part_refs, x_hbm, gain_ref, shift_ref, norm_ref, keep_ref, att_scr, w_scr, x_ref, sems) = refs
+    depth = len(part_refs) // 3
+    piece_refs = part_refs[:depth]
     rows, width = norm_ref.shape
     share = rows // depth
     twins = x_hbm.shape[0] // rows
@@ -210,11 +213,14 @@
         source = place_ref[DEEP] ^ bits
         lanes = pl.ds(pl.multiple_of(source % (depth // 2) * block, block), block)
         att_scr[source // (depth // 2), :, lanes] = piece_ref[...]
+        lanes = pl.ds(pl.multiple_of(source * 128, 128), 128)
+        w_scr[0, :, lanes] = part_refs[depth + bits][...]
+        w_scr[1, :, lanes] = part_refs[2 * depth + bits][...]
     for copy in copies:
         copy.wait()
     total = x_ref[...].astype(F32)
-    for side, ref in ((core, mine_ref), (1 - core, theirs_ref)):
-        total += lax.dot_general(att_scr[side], ref[...], NT, preferred_element_type=F32)
+    for index, side in enumerate((core, 1 - core)):
+        total += lax.dot_general(att_scr[side], w_scr[index], NT, preferred_element_type=F32)
     norm_ref[...] = normed(total, gain_ref[...], shift_ref[...]).astype(BF)
     keep_ref[...] = norm_ref[pl.ds(pl.multiple_of(place_ref[DEEP] * share, share), share)]
 
@@ -231,13 +237,14 @@
     result_ref[...] = half_feed(arrived_ref[...], mine_ref)
 
 
-def feed_kernel(place_ref, arrived_ref, own_ref, theirs_ref, *refs):
-    *sum_refs, sum_scr = refs
+def feed_kernel(targets, place_ref, arrived_ref, own_ref, theirs_ref, *sum_refs):
     share = sum_refs[0].shape[0]
-    result = own_ref[...] + half_feed(arrived_ref[...], theirs_ref)
-    sum_scr[...] = rearranged(result.astype(BF), True)
-    for bits, sum_ref in enumerate(sum_refs):
-        sum_ref[...] = sum_scr[pl.ds(pl.multiple_of((place_ref[DEEP] ^ bits) * share, share), share)]
+    spans = [pl.ds(pl.multiple_of((place_ref[DEEP] ^ bits) * share, share), share) for bits in targets]
+    arrived = jnp.concatenate([arrived_ref[span] for span in spans], axis=0)
+    result = jnp.concatenate([own_ref[span] for span in spans], axis=0) + half_feed(arrived, theirs_ref)
+    result = rearranged(result.astype(BF), True)
+    for index, sum_ref in enumerate(sum_refs):
+        sum_ref[...] = result[index * share : (index + 1) * share]
 
 
 def final_kernel(*refs):
@@ -267,9 +274,12 @@
     return lax.ppermute(value, "cc", [(0, 1), (1, 0)])
 
 
+def moved(value, bits):
+    return lax.ppermute(value, "zz", [(i, i ^ bits) for i in range(lax.axis_size("zz"))])
+
+
 def crossed(values):
-    size = len(values)
-    return [values[0]] + [lax.ppermute(values[bits], "zz", [(i, i ^ bits) for i in range(size)]) for bits in range(1, size)]
+    return [values[0]] + [moved(values[bits], bits) for bits in range(1, len(values))]
 
 
 def body(hidden_in, request_ids, w_qkv, w_out, w_up, w_down, ln1_gain, ln1_shift, ln2_gain, ln2_shift):
@@ -294,18 +304,34 @@
 
     w_qkv, w_out, w_up, w_down, hidden_in = (pltpu.with_memory_space_constraint(x, pltpu.HBM) for x in (w_qkv, w_out, w_up, w_down, hidden_in))
     first_cols = 128 + 384
-    packed = call(pack_first_kernel, "pack_first", shape(copies, cores, depth, twins, unit, first_cols), [VM, VM])(w_qkv, w_out)
+    sems = pltpu.SemaphoreType.DMA((copies, twins))
+    packed = call(
+        pack_first_kernel,
+        "pack_first",
+        shape(copies, cores, depth, twins, unit, first_cols),
+        [VM, VM],
+        out_specs=HB,
+        scratch_shapes=[pltpu.VMEM((cores, depth, unit, first_cols), BF), sems],
+    )(w_qkv, w_out)
     served = exchange(packed.reshape(-1, unit, first_cols), GROUP + PART).reshape(width, first_cols)
     other_hidden = swapped(hidden_in)
     other_ids = swapped(request_ids)
     held = crossed(call(pack_depth_kernel, "pack_depth", (shape(unit, 2 * hidden),) * depth, [SM, VM, VM])(place, w_up, w_down))
     held, other_hidden, other_ids = lax.optimization_barrier((held, other_hidden, other_ids))
-    packed_rest = call(pack_rest_kernel, "pack_rest", shape(copies, cores, twins, depth, unit, hidden), [SM] + [VM] * depth)(place, *held)
+    packed_rest = call(
+        pack_rest_kernel,
+        "pack_rest",
+        shape(copies, cores, twins, depth, unit, hidden),
+        [SM] + [VM] * depth,
+        out_specs=HB,
+        scratch_shapes=[pltpu.VMEM((cores, depth, unit, hidden), BF), sems],
+    )(place, *held)
     packed_rest, served = lax.optimization_barrier((packed_rest, served))
     rest = exchange(packed_rest.reshape(-1, depth, unit, hidden), GROUP + ("yl",)).reshape(width, hidden)
 
     out_part = call(take_kernel, "take", shape(width, 128), [pl.BlockSpec((width, 128), lambda i: (0, 0))], grid=(1,), out_specs=pl.BlockSpec((width, 128), lambda i: (0, 0)))(served)
-    out_parts = crossed([out_part] * depth)
+    far = moved(out_part, 3)
+    out_parts = [out_part, moved(out_part, 1), None, far]
     id_tiles = (rows // 128, 128)
     few = rows // twins
     att_own, kv_own, send = call(
@@ -320,12 +346,13 @@
         + [pltpu.VMEM((2 * rows // 128, 128), F32), pltpu.SemaphoreType.DMA((2,))],
     )(place, hidden_in, other_hidden, served, request_ids.reshape(id_tiles), other_ids.reshape(id_tiles))
     got = swapped(send)
+    got, out_parts[1], out_parts[3] = lax.optimization_barrier((got, out_parts[1], out_parts[3]))
+    out_parts[2] = moved(out_parts[3], 1)
     joined = call(join_kernel, "join", shape(few, 256), [SM, VM, VM])(place, att_own, got)
-    out_parts, got = lax.optimization_barrier((out_parts, got))
-    mine_out = call(assemble_kernel, "assemble", shape(width, width // cores), [SM] + [VM] * depth)(place, *out_parts)
-    mine_out, joined = lax.optimization_barrier((mine_out, joined))
+    out_parts[0], out_parts[1], out_parts[3], joined = lax.optimization_barrier((out_parts[0], out_parts[1], out_parts[3], joined))
     pieces = crossed([joined] * depth)
-    theirs_out = swapped(mine_out)
+    out_parts[2], pieces = lax.optimization_barrier((out_parts[2], pieces))
+    their_parts = [swapped(part) for part in out_parts]
     keys_out, values_out = call(cache_kernel, "cache", (shape(rows, 128),) * 2, [SM, VM, VM], 10**9)(place, kv_own, got)
 
     share = few // depth
@@ -333,12 +360,18 @@
         project_kernel,
         "project",
         (shape(few, width), shape(share, width)),
-        [SM] + [VM] * (depth + 2) + [HB, VM, VM],
+        [SM] + [VM] * (3 * depth) + [HB, VM, VM],
         2 * 10**9,
         16,
-        scratch_shapes=[pltpu.VMEM((2, few, width // 2), BF), pltpu.VMEM((few, width), BF), pltpu.SemaphoreType.DMA((depth,))],
-    )(place, *pieces, mine_out, theirs_out, hidden_in, ln1_gain[None, :], ln1_shift[None, :])
+        scratch_shapes=[
+            pltpu.VMEM((2, few, width // 2), BF),
+            pltpu.VMEM((2, width, width // 2), BF),
+            pltpu.VMEM((few, width), BF),
+            pltpu.SemaphoreType.DMA((depth,)),
+        ],
+    )(place, *pieces, *out_parts, *their_parts, hidden_in, ln1_gain[None, :], ln1_shift[None, :])
     rest, norm = lax.optimization_barrier((rest, norm))
+    norm = pltpu.with_memory_space_constraint(norm, pltpu.HBM)
     theirs = swapped(rest)
     arrived, own_sums = call(
         own_feed_kernel,
@@ -348,15 +381,18 @@
         2 * 10**9,
         16,
     )(norm, rest)
-    sums = call(
-        feed_kernel,
-        "feed",
-        (shape(share, width),) * depth,
-        [SM] + [VM] * 3,
-        3 * 10**9,
-        20,
-        scratch_shapes=[pltpu.VMEM((few, width), BF)],
-    )(place, arrived, own_sums, theirs)
+    sums = [None] * depth
+    for targets in ((2, 3), (1, 0)):
+        results = call(
+            functools.partial(feed_kernel, targets),
+            "feed",
+            (shape(share, width),) * len(targets),
+            [SM] + [VM] * 3,
+            10**9,
+            16,
+        )(place, arrived, own_sums, theirs)
+        for bits, result in zip(targets, results):
+            sums[bits] = result
     sums = crossed(sums)
     final = call(final_kernel, "final", shape(share, width), [VM] * (depth + 3))(*sums, keep, ln2_gain[None, :], ln2_shift[None, :])
     return (final, keys_out, values_out)

time: 89 us -> 86.1 us (0.967)
  waiting for transfers between devices: 25.5 us -> 20.1 us
  Pallas kernels: 20.5 us -> 22.3 us
  starting transfers between devices: 39.8 us -> 41.3 us
  local copies, waits for them, and re-layouts: 1.87 us -> 0.82 us
    ppermute x12, waiting for transfers between devices: 21.3 us -> 14.7 us  [moved(): lax.ppermute(value, 'zz', [(i, i ^ bits) for i in range(lax.axis_size('zz...]
    ppermute x5 -> x8, starting transfers between devices: 6.61 us -> 9.56 us  [swapped(): return lax.ppermute(value, 'cc', [(0, 1), (1, 0)])]
    ppermute x12, starting transfers between devices: 15.1 us -> 13.6 us  [moved(): lax.ppermute(value, 'zz', [(i, i ^ bits) for i in range(lax.axis_size('zz...]
    ppermute x5 -> x8, waiting for transfers between devices: 3.69 us -> 4.88 us  [swapped(): return lax.ppermute(value, 'cc', [(0, 1), (1, 0)])]
    pallas_call x1, Pallas kernels: 0.94 us -> 1.99 us  [body(): call(own_feed_kernel, 'own_feed', (shape(few, width), jax.ShapeDtypeStruc...]
    unnamed x16 -> x14, local copies, waits for them, and re-layouts: 1.87 us -> 0.82 us
  transfers between devices with their start and end apart: 19 -> 22, of which waited for: 12 -> 13; matrix products, arithmetic and copies ran while one was open for 0% -> 0% of each run, Pallas kernels for 20% -> 23%
where the time goes in v6:
time: 86.1 us; the launch traced here: 85.4 us
  starting transfers between devices  41.3 us (48%)
  Pallas kernels  22.3 us (26%)
  waiting for transfers between devices  20.1 us (23%)
    all_to_all x2, starting transfers between devices, exchange(): return lax.all_to_all(value, axes, split_axis=0, concat_axis=0, tiled=True)  18.1 us
    ppermute x12, waiting for transfers between devices, moved(): lax.ppermute(value, 'zz', [(i, i ^ bits) for i in range(lax.axis_size('zz...  14.7 us
    ppermute x12, starting transfers between devices, moved(): lax.ppermute(value, 'zz', [(i, i ^ bits) for i in range(lax.axis_size('zz...  13.6 us
    ppermute x8, starting transfers between devices, swapped(): return lax.ppermute(value, 'cc', [(0, 1), (1, 0)])  9.56 us
    pallas_call x1, Pallas kernels, body(): call(attend_kernel, 'attend', (shape(few, 128), shape(rows, 128), shape(f...  6.48 us
    ppermute x8, waiting for transfers between devices, swapped(): return lax.ppermute(value, 'cc', [(0, 1), (1, 0)])  4.88 us
    pallas_call x1, Pallas kernels, body(): call(project_kernel, 'project', (shape(few, width), shape(share, width)),...  2.86 us
    pallas_call x2, Pallas kernels, body(): call(functools.partial(feed_kernel, targets), 'feed', (shape(share, width...  2.8 us
  transfers between devices with their start and end apart: 22, of which 13 were waited for; matrix products, arithmetic and copies ran while one was open for 0% of the time, Pallas kernels for 23%

profile of v6, /device:TPU:1, one launch (start us, length us, event | category | flops | bytes accessed | tf_op | source)
XLA Modules:
  0.0 85.4 jit_solution(1742626477711786290)
XLA Ops:
  0.6 1.5 %collective-permute-start.3 = (bf16[512,1024]{1,0:T(8,128)(2,1)}, bf16[512,1024]{1,0:T(8,128)(2,1)S(1)}, u32[]{:S(2)}, u32[]{:S(2)}) collective-permute-start(bf16[512,1024]{1,0:T(8,128)(2,1)} %refs_12_.1), channel_id=1, source_target_pairs={{0,8},{8,0},{1,9},{9,1},{2,10},{10,2},{3,11},{11,3},{4,12},{12,4},... | collective-permute-start | bytes 3145736 | tf_op jit(solution)/shard_map/ppermute | solution.py:274
  2.1 2.1 %pack_first.1 = bf16[8,2,4,2,8,512]{5,4,3,2,1,0:T(8,128)(2,1)} custom-call(f32[8,3072]{1,0:T(8,128)} %qkv_ref.1, f32[8,1024]{1,0:T(8,128)} %out_ref.1), custom_call_target="tpu_custom_call" | custom-call | bytes 1048576 | tf_op jit(solution)/shard_map/pack_first/pallas_call | solution.py:308
  4.3 10.2 %all-to-all-start = ((bf16[128,8,512]{2,1,0:T(8,128)(2,1)}), bf16[128,8,512]{2,1,0:T(8,128)(2,1)S(1)}, u32[]{:S(2)}, u32[]{:S(2)}) async-start(bf16[128,8,512]{2,1,0:T(8,128)(2,1)} %bitcast.3), calls=%async_computation | async-start | bytes 2097152 | tf_op jit(solution)/shard_map/all_to_all | solution.py:270
  14.5 1.0 %pack_depth.1 = (bf16[8,2048]{1,0:T(8,128)(2,1)S(1)}, bf16[8,2048]{1,0:T(8,128)(2,1)S(1)}, bf16[8,2048]{1,0:T(8,128)(2,1)S(1)}, bf16[8,2048]{1,0:T(8,128)(2,1)S(1)}) custom-call(s32[3]{0:T(128)S(1)} %pad_add_fusion.place_ref, f32[8,4096]{1,0:T(8,128)} %up_ref.1, f32[8,4096]{1,0:T(8,128)} %down_ref.1), custom_call_target="tpu_custom_call" | custom-call | bytes 1048576 | tf_op jit(solution)/shard_map/pack_depth/pallas_call | solution.py:319
  15.5 1.6 %collective-permute-start = (bf16[8,2048]{1,0:T(8,128)(2,1)S(1)}, bf16[8,2048]{1,0:T(8,128)(2,1)S(1)}, u32[]{:S(2)}, u32[]{:S(2)}) collective-permute-start(bf16[8,2048]{1,0:T(8,128)(2,1)S(1)} %get-tuple-element.43), channel_id=1, source_target_pairs={{0,2},{2,0},{4,6},{6,4},{1,3},{3,1},{5,7},{7,5},{8,10},{10,8},{12,... | collective-permute-start | bytes 98312 | tf_op jit(solution)/shard_map/ppermute | solution.py:278
  17.1 2.9 %collective-permute-start.1 = (bf16[8,2048]{1,0:T(8,128)(2,1)S(1)}, bf16[8,2048]{1,0:T(8,128)(2,1)S(1)}, u32[]{:S(2)}, u32[]{:S(2)}) collective-permute-start(bf16[8,2048]{1,0:T(8,128)(2,1)S(1)} %get-tuple-element.44), channel_id=1, source_target_pairs={{0,4},{2,6},{4,0},{6,2},{1,5},{3,7},{5,1},{7,3},{8,12},{10,14},{12... | collective-permute-start | bytes 98312 | tf_op jit(solution)/shard_map/ppermute | solution.py:278
  20.1 1.3 %collective-permute-start.4 = (s32[512]{0:T(512)S(1)}, s32[512]{0:T(512)S(1)}, u32[]{:S(2)}, u32[]{:S(2)}) collective-permute-start(s32[512]{0:T(512)S(1)} %copy-done.4), channel_id=1, source_target_pairs={{0,8},{8,0},{1,9},{9,1},{2,10},{10,2},{3,11},{11,3},{4,12},{12,4},... | collective-permute-start | bytes 6152 | tf_op jit(solution)/shard_map/ppermute | solution.py:274
  21.4 0.8 collective-permute-done.4
  22.7 7.5 %collective-permute-done.1.refs_2_ = bf16[8,2048]{1,0:T(8,128)(2,1)S(1)} collective-permute-done((bf16[8,2048]{1,0:T(8,128)(2,1)S(1)}, bf16[8,2048]{1,0:T(8,128)(2,1)S(1)}, u32[]{:S(2)}, u32[]{:S(2)}) %collective-permute-start.1) | collective-permute-done | bytes 32800 | tf_op jit(solution)/shard_map/ppermute | solution.py:278
  30.1 2.1 %pack_rest.1 = bf16[8,2,2,4,8,1024]{5,4,3,2,1,0:T(8,128)(2,1)} custom-call(s32[3]{0:T(128)S(1)} %pad_add_fusion.place_ref, bf16[8,2048]{1,0:T(8,128)(2,1)S(1)} %get-tuple-element.46.refs_0_, bf16[8,2048]{1,0:T(8,128)(2,1)S(1)} %collective-permute-done.refs_1_, bf16[8,2048]{1,0:T(8,128)(2,1)S(1)} %collective-permute-done.1.refs_2_, ...), custom_call_target="tpu_custom_call" | custom-call | bytes 1048576 | tf_op jit(solution)/shard_map/pack_rest/pallas_call | solution.py:321
  32.7 7.9 %all-to-all-start.1 = ((bf16[32,4,8,1024]{3,2,1,0:T(8,128)(2,1)}), bf16[32,4,8,1024]{3,2,1,0:T(8,128)(2,1)S(1)}, u32[]{:S(2)}, u32[]{:S(2)}) async-start(bf16[32,4,8,1024]{3,2,1,0:T(8,128)(2,1)} %bitcast.5), calls=%async_computation.1 | async-start | bytes 4194304 | tf_op jit(solution)/shard_map/all_to_all | solution.py:270
  41.4 6.5 %attend.1 = (bf16[256,128]{1,0:T(8,128)(2,1)S(1)}, bf16[512,128]{1,0:T(8,128)(2,1)S(1)}, bf16[768,128]{1,0:T(8,128)(2,1)S(1)}) custom-call(s32[3]{0:T(128)S(1)} %pad_add_fusion.place_ref, bf16[512,1024]{1,0:T(8,128)(2,1)} %refs_12_.1, bf16[512,1024]{1,0:T(8,128)(2,1)} %copy-done.6, bf16[1024,512]{1,0:T(8,128)(2,1)S(1)} %bitcast.14, s32[4,128]{1,0:T(4,128)S(1)} %bitcast.21, ...), custom_call_target="tpu_custom_call" | custom-call | flops 5000000000 | bytes 1048576 | tf_op jit(solution)/shard_map/attend/pallas_call | solution.py:337
  48.5 1.1 %collective-permute-done.5.got_ref = bf16[768,128]{1,0:T(8,128)(2,1)S(1)} collective-permute-done((bf16[768,128]{1,0:T(8,128)(2,1)S(1)}, bf16[768,128]{1,0:T(8,128)(2,1)S(1)}, u32[]{:S(2)}, u32[]{:S(2)}) %collective-permute-start.5) | collective-permute-done | bytes 196640 | tf_op jit(solution)/shard_map/ppermute | solution.py:274
  49.7 1.6 %collective-permute-start.8 = (bf16[1024,128]{1,0:T(8,128)(2,1)S(1)}, bf16[1024,128]{1,0:T(8,128)(2,1)S(1)}, u32[]{:S(2)}, u32[]{:S(2)}) collective-permute-start(bf16[1024,128]{1,0:T(8,128)(2,1)S(1)} %collective-permute-done.7.refs_7_), channel_id=1, source_target_pairs={{0,2},{2,0},{4,6},{6,4},{1,3},{3,1},{5,7},{7,5},{8,10},{10,8},{12,... | collective-permute-start | bytes 786440 | tf_op jit(solution)/shard_map/ppermute | solution.py:278
  52.0 2.1 %collective-permute-start.11 = (bf16[256,256]{1,0:T(8,128)(2,1)S(1)}, bf16[256,256]{1,0:T(8,128)(2,1)S(1)}, u32[]{:S(2)}, u32[]{:S(2)}) collective-permute-start(bf16[256,256]{1,0:T(8,128)(2,1)S(1)} %join.1.refs_0_), channel_id=1, source_target_pairs={{0,6},{2,4},{4,2},{6,0},{1,7},{3,5},{5,3},{7,1},{8,14},{10,12},{12... | collective-permute-start | bytes 393224 | tf_op jit(solution)/shard_map/ppermute | solution.py:278
  54.1 1.2 %collective-permute-start.9 = (bf16[256,256]{1,0:T(8,128)(2,1)S(1)}, bf16[256,256]{1,0:T(8,128)(2,1)S(1)}, u32[]{:S(2)}, u32[]{:S(2)}) collective-permute-start(bf16[256,256]{1,0:T(8,128)(2,1)S(1)} %join.1.refs_0_), channel_id=1, source_target_pairs={{0,2},{2,0},{4,6},{6,4},{1,3},{3,1},{5,7},{7,5},{8,10},{10,8},{12,... | collective-permute-start | bytes 393224 | tf_op jit(solution)/shard_map/ppermute | solution.py:278
  55.3 1.5 %collective-permute-start.12 = (bf16[1024,128]{1,0:T(8,128)(2,1)S(1)}, bf16[1024,128]{1,0:T(8,128)(2,1)S(1)}, u32[]{:S(2)}, u32[]{:S(2)}) collective-permute-start(bf16[1024,128]{1,0:T(8,128)(2,1)S(1)} %take.1.refs_4_), channel_id=1, source_target_pairs={{0,8},{8,0},{1,9},{9,1},{2,10},{10,2},{3,11},{11,3},{4,12},{12,4},... | collective-permute-start | bytes 786440 | tf_op jit(solution)/shard_map/ppermute | solution.py:274
  56.8 0.9 %collective-permute-done.11.refs_3_ = bf16[256,256]{1,0:T(8,128)(2,1)S(1)} collective-permute-done((bf16[256,256]{1,0:T(8,128)(2,1)S(1)}, bf16[256,256]{1,0:T(8,128)(2,1)S(1)}, u32[]{:S(2)}, u32[]{:S(2)}) %collective-permute-start.11) | collective-permute-done | bytes 131104 | tf_op jit(solution)/shard_map/ppermute | solution.py:278
  57.7 1.6 %collective-permute-start.13 = (bf16[1024,128]{1,0:T(8,128)(2,1)S(1)}, bf16[1024,128]{1,0:T(8,128)(2,1)S(1)}, u32[]{:S(2)}, u32[]{:S(2)}) collective-permute-start(bf16[1024,128]{1,0:T(8,128)(2,1)S(1)} %collective-permute-done.6.refs_5_), channel_id=1, source_target_pairs={{0,8},{8,0},{1,9},{9,1},{2,10},{10,2},{3,11},{11,3},{4,12},{12,4},... | collective-permute-start | bytes 786440 | tf_op jit(solution)/shard_map/ppermute | solution.py:274
  59.2 2.8 %collective-permute-done.10.refs_2_ = bf16[256,256]{1,0:T(8,128)(2,1)S(1)} collective-permute-done((bf16[256,256]{1,0:T(8,128)(2,1)S(1)}, bf16[256,256]{1,0:T(8,128)(2,1)S(1)}, u32[]{:S(2)}, u32[]{:S(2)}) %collective-permute-start.10) | collective-permute-done | bytes 131104 | tf_op jit(solution)/shard_map/ppermute | solution.py:278
  62.1 1.8 %collective-permute-start.15 = (bf16[1024,128]{1,0:T(8,128)(2,1)S(1)}, bf16[1024,128]{1,0:T(8,128)(2,1)S(1)}, u32[]{:S(2)}, u32[]{:S(2)}) collective-permute-start(bf16[1024,128]{1,0:T(8,128)(2,1)S(1)} %collective-permute-done.7.refs_7_), channel_id=1, source_target_pairs={{0,8},{8,0},{1,9},{9,1},{2,10},{10,2},{3,11},{11,3},{4,12},{12,4},... | collective-permute-start | bytes 786440 | tf_op jit(solution)/shard_map/ppermute | solution.py:274
  64.2 0.8 collective-permute-done.15.refs_11_
  65.4 2.9 %project.1 = (bf16[256,1024]{1,0:T(8,128)(2,1)S(1)}, bf16[64,1024]{1,0:T(8,128)(2,1)S(1)}) custom-call(s32[3]{0:T(128)S(1)} %pad_add_fusion.place_ref, bf16[256,256]{1,0:T(8,128)(2,1)S(1)} %join.1.refs_0_, bf16[256,256]{1,0:T(8,128)(2,1)S(1)} %collective-permute-done.9.refs_1_, bf16[256,256]{1,0:T(8,128)(2,1)S(1)} %collective-permute-done.10.refs_2_, ...), custom_call_target="tpu_custom_call" | custom-call | flops 2000000000 | bytes 1048576 | tf_op jit(solution)/shard_map/project/pallas_call | solution.py:359
  69.1 0.9 %collective-permute-start.16 = (bf16[1024,1024]{1,0:T(8,128)(2,1)S(1)}, bf16[1024,1024]{1,0:T(8,128)(2,1)S(1)}, u32[]{:S(2)}, u32[]{:S(2)}) collective-permute-start(bf16[1024,1024]{1,0:T(8,128)(2,1)S(1)} %bitcast.15), channel_id=1, source_target_pairs={{0,8},{8,0},{1,9},{9,1},{2,10},{10,2},{3,11},{11,3},{4,12},{12,4},... | collective-permute-start | bytes 6291464 | tf_op jit(solution)/shard_map/ppermute | solution.py:274
  70.0 2.0 %own_feed.1 = (bf16[256,1024]{1,0:T(8,128)(2,1)S(1)}, f32[256,1024]{1,0:T(8,128)S(1)}) custom-call(bf16[256,1024]{1,0:T(8,128)(2,1)} %copy-done.5, bf16[1024,1024]{1,0:T(8,128)(2,1)S(1)} %bitcast.16), custom_call_target="tpu_custom_call" | custom-call | flops 2000000000 | bytes 1048576 | tf_op jit(solution)/shard_map/own_feed/pallas_call | solution.py:376
  72.0 1.8 %collective-permute-done.16.theirs_ref = bf16[1024,1024]{1,0:T(8,128)(2,1)S(1)} collective-permute-done((bf16[1024,1024]{1,0:T(8,128)(2,1)S(1)}, bf16[1024,1024]{1,0:T(8,128)(2,1)S(1)}, u32[]{:S(2)}, u32[]{:S(2)}) %collective-permute-start.16) | collective-permute-done | bytes 2097184 | tf_op jit(solution)/shard_map/ppermute | solution.py:274
  73.8 1.4 %feed.3 = (bf16[64,1024]{1,0:T(8,128)(2,1)S(1)}, bf16[64,1024]{1,0:T(8,128)(2,1)S(1)}) custom-call(s32[3]{0:T(128)S(1)} %pad_add_fusion.place_ref, bf16[256,1024]{1,0:T(8,128)(2,1)S(1)} %get-tuple-element.71.arrived_ref, f32[256,1024]{1,0:T(8,128)S(1)} %get-tuple-element.72.own_ref, bf16[1024,1024]{1,0:T(8,128)(2,1)S(1)} %collective-permute-done.16.theirs_ref), custom_call_target="tpu_custom_call" | custom-call | flops 1000000000 | bytes 1048576 | tf_op jit(solution)/shard_map/feed/pallas_call | solution.py:386
  75.2 2.7 %collective-permute-start.18 = (bf16[64,1024]{1,0:T(8,128)(2,1)S(1)}, bf16[64,1024]{1,0:T(8,128)(2,1)S(1)}, u32[]{:S(2)}, u32[]{:S(2)}) collective-permute-start(bf16[64,1024]{1,0:T(8,128)(2,1)S(1)} %get-tuple-element.75), channel_id=1, source_target_pairs={{0,4},{2,6},{4,0},{6,2},{1,5},{3,7},{5,1},{7,3},{8,12},{10,14},{12... | collective-permute-start | bytes 393224 | tf_op jit(solution)/shard_map/ppermute | solution.py:278
  78.5 1.4 %feed.2 = (bf16[64,1024]{1,0:T(8,128)(2,1)S(1)}, bf16[64,1024]{1,0:T(8,128)(2,1)S(1)}) custom-call(s32[3]{0:T(128)S(1)} %pad_add_fusion.place_ref, bf16[256,1024]{1,0:T(8,128)(2,1)S(1)} %get-tuple-element.71.arrived_ref, f32[256,1024]{1,0:T(8,128)S(1)} %get-tuple-element.72.own_ref, bf16[1024,1024]{1,0:T(8,128)(2,1)S(1)} %collective-permute-done.16.theirs_ref), custom_call_target="tpu_custom_call" | custom-call | flops 1000000000 | bytes 1048576 | tf_op jit(solution)/shard_map/feed/pallas_call | solution.py:386
  80.1 1.4 %cache.1 = (bf16[512,128]{1,0:T(8,128)(2,1)}, bf16[512,128]{1,0:T(8,128)(2,1)}) custom-call(s32[3]{0:T(128)S(1)} %pad_add_fusion.place_ref, bf16[512,128]{1,0:T(8,128)(2,1)S(1)} %get-tuple-element.78.own_ref, bf16[768,128]{1,0:T(8,128)(2,1)S(1)} %collective-permute-done.5.got_ref), custom_call_target="tpu_custom_call" | custom-call | flops 1000000000 | bytes 1048576 | tf_op jit(solution)/shard_map/cache/pallas_call | solution.py:356
  81.5 2.9 %collective-permute-done.19.refs_3_ = bf16[64,1024]{1,0:T(8,128)(2,1)S(1)} collective-permute-done((bf16[64,1024]{1,0:T(8,128)(2,1)S(1)}, bf16[64,1024]{1,0:T(8,128)(2,1)S(1)}, u32[]{:S(2)}, u32[]{:S(2)}) %collective-permute-start.19) | collective-permute-done | bytes 131104 | tf_op jit(solution)/shard_map/ppermute | solution.py:278
  84.5 0.9 %final.1 = bf16[64,1024]{1,0:T(8,128)(2,1)} custom-call(bf16[64,1024]{1,0:T(8,128)(2,1)S(1)} %get-tuple-element.73.refs_0_, bf16[64,1024]{1,0:T(8,128)(2,1)S(1)} %collective-permute-done.17.refs_1_, bf16[64,1024]{1,0:T(8,128)(2,1)S(1)} %collective-permute-done.18.refs_2_, bf16[64,1024]{1,0:T(8,128)(2,1)S(1)} %collective-permute-done.19.refs_3_, ...), custom_call_target="tpu_custom_call" | custom-call | bytes 1048576 | tf_op jit(solution)/shard_map/final/pallas_call | solution.py:397
  (39 shorter events, 5.5 us)
Async XLA Ops:
  0.6 19.4 %copy-start.4 = (s32[512]{0:T(512)S(1)}, s32[512]{0:T(512)}, u32[]{:S(2)}) copy-start(s32[512]{0:T(512)} %param.11) | copy-start | bytes 6148
  0.6 29.5 %collective-permute-start.3 = (bf16[512,1024]{1,0:T(8,128)(2,1)}, bf16[512,1024]{1,0:T(8,128)(2,1)S(1)}, u32[]{:S(2)}, u32[]{:S(2)}) collective-permute-start(bf16[512,1024]{1,0:T(8,128)(2,1)} %refs_12_.1), channel_id=1, source_target_pairs={{0,8},{8,0},{1,9},{9,1},{2,10},{10,2},{3,11},{11,3},{4,12},{12,4},... | collective-permute-start | bytes 3145736 | tf_op jit(solution)/shard_map/ppermute | solution.py:274
  4.3 28.5 %all-to-all-start = ((bf16[128,8,512]{2,1,0:T(8,128)(2,1)}), bf16[128,8,512]{2,1,0:T(8,128)(2,1)S(1)}, u32[]{:S(2)}, u32[]{:S(2)}) async-start(bf16[128,8,512]{2,1,0:T(8,128)(2,1)} %bitcast.3), calls=%async_computation | async-start | bytes 2097152 | tf_op jit(solution)/shard_map/all_to_all | solution.py:270
  15.5 7.1 %collective-permute-start = (bf16[8,2048]{1,0:T(8,128)(2,1)S(1)}, bf16[8,2048]{1,0:T(8,128)(2,1)S(1)}, u32[]{:S(2)}, u32[]{:S(2)}) collective-permute-start(bf16[8,2048]{1,0:T(8,128)(2,1)S(1)} %get-tuple-element.43), channel_id=1, source_target_pairs={{0,2},{2,0},{4,6},{6,4},{1,3},{3,1},{5,7},{7,5},{8,10},{10,8},{12,... | collective-permute-start | bytes 98312 | tf_op jit(solution)/shard_map/ppermute | solution.py:278
  17.1 13.0 %collective-permute-start.1 = (bf16[8,2048]{1,0:T(8,128)(2,1)S(1)}, bf16[8,2048]{1,0:T(8,128)(2,1)S(1)}, u32[]{:S(2)}, u32[]{:S(2)}) collective-permute-start(bf16[8,2048]{1,0:T(8,128)(2,1)S(1)} %get-tuple-element.44), channel_id=1, source_target_pairs={{0,4},{2,6},{4,0},{6,2},{1,5},{3,7},{5,1},{7,3},{8,12},{10,14},{12... | collective-permute-start | bytes 98312 | tf_op jit(solution)/shard_map/ppermute | solution.py:278
  20.1 10.1 %collective-permute-start.2 = (bf16[8,2048]{1,0:T(8,128)(2,1)S(1)}, bf16[8,2048]{1,0:T(8,128)(2,1)S(1)}, u32[]{:S(2)}, u32[]{:S(2)}) collective-permute-start(bf16[8,2048]{1,0:T(8,128)(2,1)S(1)} %get-tuple-element.45), channel_id=1, source_target_pairs={{0,6},{2,4},{4,2},{6,0},{1,7},{3,5},{5,3},{7,1},{8,14},{10,12},{12... | collective-permute-start | bytes 98312 | tf_op jit(solution)/shard_map/ppermute | solution.py:278
  20.1 2.1 %collective-permute-start.4 = (s32[512]{0:T(512)S(1)}, s32[512]{0:T(512)S(1)}, u32[]{:S(2)}, u32[]{:S(2)}) collective-permute-start(s32[512]{0:T(512)S(1)} %copy-done.4), channel_id=1, source_target_pairs={{0,8},{8,0},{1,9},{9,1},{2,10},{10,2},{3,11},{11,3},{4,12},{12,4},... | collective-permute-start | bytes 6152 | tf_op jit(solution)/shard_map/ppermute | solution.py:274
  30.1 2.6 %copy-start.6 = (bf16[512,1024]{1,0:T(8,128)(2,1)}, bf16[512,1024]{1,0:T(8,128)(2,1)S(1)}, u32[]{:S(2)}) copy-start(bf16[512,1024]{1,0:T(8,128)(2,1)S(1)} %collective-permute-done.3.other_hbm) | copy-start | bytes 3145732
  32.7 36.3 %all-to-all-start.1 = ((bf16[32,4,8,1024]{3,2,1,0:T(8,128)(2,1)}), bf16[32,4,8,1024]{3,2,1,0:T(8,128)(2,1)S(1)}, u32[]{:S(2)}, u32[]{:S(2)}) async-start(bf16[32,4,8,1024]{3,2,1,0:T(8,128)(2,1)} %bitcast.5), calls=%async_computation.1 | async-start | bytes 4194304 | tf_op jit(solution)/shard_map/all_to_all | solution.py:270
  40.7 9.0 %collective-permute-start.7 = (bf16[1024,128]{1,0:T(8,128)(2,1)S(1)}, bf16[1024,128]{1,0:T(8,128)(2,1)S(1)}, u32[]{:S(2)}, u32[]{:S(2)}) collective-permute-start(bf16[1024,128]{1,0:T(8,128)(2,1)S(1)} %take.1.refs_4_), channel_id=1, source_target_pairs={{0,6},{2,4},{4,2},{6,0},{1,7},{3,5},{5,3},{7,1},{8,14},{10,12},{12... | collective-permute-start | bytes 786440 | tf_op jit(solution)/shard_map/ppermute | solution.py:278
  41.4 8.3 %collective-permute-start.6 = (bf16[1024,128]{1,0:T(8,128)(2,1)S(1)}, bf16[1024,128]{1,0:T(8,128)(2,1)S(1)}, u32[]{:S(2)}, u32[]{:S(2)}) collective-permute-start(bf16[1024,128]{1,0:T(8,128)(2,1)S(1)} %take.1.refs_4_), channel_id=1, source_target_pairs={{0,2},{2,0},{4,6},{6,4},{1,3},{3,1},{5,7},{7,5},{8,10},{10,8},{12,... | collective-permute-start | bytes 786440 | tf_op jit(solution)/shard_map/ppermute | solution.py:278
  41.4 24.0 %copy-start.2 = (f32[1024]{0:T(1024)S(1)}, f32[1024]{0:T(1024)}, u32[]{:S(2)}) copy-start(f32[1024]{0:T(1024)} %param.16) | copy-start | bytes 12292
  41.4 24.0 %copy-start.3 = (f32[1024]{0:T(1024)S(1)}, f32[1024]{0:T(1024)}, u32[]{:S(2)}) copy-start(f32[1024]{0:T(1024)} %param.17) | copy-start | bytes 12292
  47.9 1.7 %collective-permute-start.5 = (bf16[768,128]{1,0:T(8,128)(2,1)S(1)}, bf16[768,128]{1,0:T(8,128)(2,1)S(1)}, u32[]{:S(2)}, u32[]{:S(2)}) collective-permute-start(bf16[768,128]{1,0:T(8,128)(2,1)S(1)} %get-tuple-element.54), channel_id=1, source_target_pairs={{0,8},{8,0},{1,9},{9,1},{2,10},{10,2},{3,11},{11,3},{4,12},{12,4},... | collective-permute-start | bytes 589832 | tf_op jit(solution)/shard_map/ppermute | solution.py:274
  49.7 14.2 %collective-permute-start.8 = (bf16[1024,128]{1,0:T(8,128)(2,1)S(1)}, bf16[1024,128]{1,0:T(8,128)(2,1)S(1)}, u32[]{:S(2)}, u32[]{:S(2)}) collective-permute-start(bf16[1024,128]{1,0:T(8,128)(2,1)S(1)} %collective-permute-done.7.refs_7_), channel_id=1, source_target_pairs={{0,2},{2,0},{4,6},{6,4},{1,3},{3,1},{5,7},{7,5},{8,10},{10,8},{12,... | collective-permute-start | bytes 786440 | tf_op jit(solution)/shard_map/ppermute | solution.py:278
  52.0 5.7 %collective-permute-start.11 = (bf16[256,256]{1,0:T(8,128)(2,1)S(1)}, bf16[256,256]{1,0:T(8,128)(2,1)S(1)}, u32[]{:S(2)}, u32[]{:S(2)}) collective-permute-start(bf16[256,256]{1,0:T(8,128)(2,1)S(1)} %join.1.refs_0_), channel_id=1, source_target_pairs={{0,6},{2,4},{4,2},{6,0},{1,7},{3,5},{5,3},{7,1},{8,14},{10,12},{12... | collective-permute-start | bytes 393224 | tf_op jit(solution)/shard_map/ppermute | solution.py:278
  54.1 8.0 %collective-permute-start.10 = (bf16[256,256]{1,0:T(8,128)(2,1)S(1)}, bf16[256,256]{1,0:T(8,128)(2,1)S(1)}, u32[]{:S(2)}, u32[]{:S(2)}) collective-permute-start(bf16[256,256]{1,0:T(8,128)(2,1)S(1)} %join.1.refs_0_), channel_id=1, source_target_pairs={{0,4},{2,6},{4,0},{6,2},{1,5},{3,7},{5,1},{7,3},{8,12},{10,14},{12... | collective-permute-start | bytes 393224 | tf_op jit(solution)/shard_map/ppermute | solution.py:278
  54.1 9.7 %collective-permute-start.9 = (bf16[256,256]{1,0:T(8,128)(2,1)S(1)}, bf16[256,256]{1,0:T(8,128)(2,1)S(1)}, u32[]{:S(2)}, u32[]{:S(2)}) collective-permute-start(bf16[256,256]{1,0:T(8,128)(2,1)S(1)} %join.1.refs_0_), channel_id=1, source_target_pairs={{0,2},{2,0},{4,6},{6,4},{1,3},{3,1},{5,7},{7,5},{8,10},{10,8},{12,... | collective-permute-start | bytes 393224 | tf_op jit(solution)/shard_map/ppermute | solution.py:278
  55.3 8.9 %collective-permute-start.12 = (bf16[1024,128]{1,0:T(8,128)(2,1)S(1)}, bf16[1024,128]{1,0:T(8,128)(2,1)S(1)}, u32[]{:S(2)}, u32[]{:S(2)}) collective-permute-start(bf16[1024,128]{1,0:T(8,128)(2,1)S(1)} %take.1.refs_4_), channel_id=1, source_target_pairs={{0,8},{8,0},{1,9},{9,1},{2,10},{10,2},{3,11},{11,3},{4,12},{12,4},... | collective-permute-start | bytes 786440 | tf_op jit(solution)/shard_map/ppermute | solution.py:274
  57.7 6.5 %collective-permute-start.13 = (bf16[1024,128]{1,0:T(8,128)(2,1)S(1)}, bf16[1024,128]{1,0:T(8,128)(2,1)S(1)}, u32[]{:S(2)}, u32[]{:S(2)}) collective-permute-start(bf16[1024,128]{1,0:T(8,128)(2,1)S(1)} %collective-permute-done.6.refs_5_), channel_id=1, source_target_pairs={{0,8},{8,0},{1,9},{9,1},{2,10},{10,2},{3,11},{11,3},{4,12},{12,4},... | collective-permute-start | bytes 786440 | tf_op jit(solution)/shard_map/ppermute | solution.py:274
  62.1 2.9 %collective-permute-start.15 = (bf16[1024,128]{1,0:T(8,128)(2,1)S(1)}, bf16[1024,128]{1,0:T(8,128)(2,1)S(1)}, u32[]{:S(2)}, u32[]{:S(2)}) collective-permute-start(bf16[1024,128]{1,0:T(8,128)(2,1)S(1)} %collective-permute-done.7.refs_7_), channel_id=1, source_target_pairs={{0,8},{8,0},{1,9},{9,1},{2,10},{10,2},{3,11},{11,3},{4,12},{12,4},... | collective-permute-start | bytes 786440 | tf_op jit(solution)/shard_map/ppermute | solution.py:274
  63.9 1.5 %collective-permute-start.14 = (bf16[1024,128]{1,0:T(8,128)(2,1)S(1)}, bf16[1024,128]{1,0:T(8,128)(2,1)S(1)}, u32[]{:S(2)}, u32[]{:S(2)}) collective-permute-start(bf16[1024,128]{1,0:T(8,128)(2,1)S(1)} %collective-permute-done.8.refs_6_), channel_id=1, source_target_pairs={{0,8},{8,0},{1,9},{9,1},{2,10},{10,2},{3,11},{11,3},{4,12},{12,4},... | collective-permute-start | bytes 786440 | tf_op jit(solution)/shard_map/ppermute | solution.py:274
  68.3 0.8 copy-start.5
  69.1 4.7 %collective-permute-start.16 = (bf16[1024,1024]{1,0:T(8,128)(2,1)S(1)}, bf16[1024,1024]{1,0:T(8,128)(2,1)S(1)}, u32[]{:S(2)}, u32[]{:S(2)}) collective-permute-start(bf16[1024,1024]{1,0:T(8,128)(2,1)S(1)} %bitcast.15), channel_id=1, source_target_pairs={{0,8},{8,0},{1,9},{9,1},{2,10},{10,2},{3,11},{11,3},{4,12},{12,4},... | collective-permute-start | bytes 6291464 | tf_op jit(solution)/shard_map/ppermute | solution.py:274
  75.2 6.3 %collective-permute-start.18 = (bf16[64,1024]{1,0:T(8,128)(2,1)S(1)}, bf16[64,1024]{1,0:T(8,128)(2,1)S(1)}, u32[]{:S(2)}, u32[]{:S(2)}) collective-permute-start(bf16[64,1024]{1,0:T(8,128)(2,1)S(1)} %get-tuple-element.75), channel_id=1, source_target_pairs={{0,4},{2,6},{4,0},{6,2},{1,5},{3,7},{5,1},{7,3},{8,12},{10,14},{12... | collective-permute-start | bytes 393224 | tf_op jit(solution)/shard_map/ppermute | solution.py:278
  77.9 6.5 %collective-permute-start.19 = (bf16[64,1024]{1,0:T(8,128)(2,1)S(1)}, bf16[64,1024]{1,0:T(8,128)(2,1)S(1)}, u32[]{:S(2)}, u32[]{:S(2)}) collective-permute-start(bf16[64,1024]{1,0:T(8,128)(2,1)S(1)} %get-tuple-element.76), channel_id=1, source_target_pairs={{0,6},{2,4},{4,2},{6,0},{1,7},{3,5},{5,3},{7,1},{8,14},{10,12},{12... | collective-permute-start | bytes 393224 | tf_op jit(solution)/shard_map/ppermute | solution.py:278
  80.0 4.5 %copy-start = (f32[1024]{0:T(1024)S(1)}, f32[1024]{0:T(1024)}, u32[]{:S(2)}) copy-start(f32[1024]{0:T(1024)} %param.18) | copy-start | bytes 12292
  80.0 4.5 %copy-start.1 = (f32[1024]{0:T(1024)S(1)}, f32[1024]{0:T(1024)}, u32[]{:S(2)}) copy-start(f32[1024]{0:T(1024)} %param.19) | copy-start | bytes 12292
  80.0 4.5 %collective-permute-start.17 = (bf16[64,1024]{1,0:T(8,128)(2,1)S(1)}, bf16[64,1024]{1,0:T(8,128)(2,1)S(1)}, u32[]{:S(2)}, u32[]{:S(2)}) collective-permute-start(bf16[64,1024]{1,0:T(8,128)(2,1)S(1)} %get-tuple-element.74), channel_id=1, source_target_pairs={{0,2},{2,0},{4,6},{6,4},{1,3},{3,1},{5,7},{7,5},{8,10},{10,8},{12,... | collective-permute-start | bytes 393224 | tf_op jit(solution)/shard_map/ppermute | solution.py:278

commit v7 on v6

--- a/solution.py
+++ b/solution.py
@@ -49,20 +49,26 @@
     return jnp.concatenate(tiles, axis=1)
 
 
-def replicate(row_scr, packed_hbm, sems, twin_at):
+def replicate(row_scr, packed_hbm, sems):
     copies = []
     for copy in range(packed_hbm.shape[0]):
-        for twin in range(packed_hbm.shape[twin_at]):
-            target = packed_hbm.at[copy, :, :, twin] if twin_at == 3 else packed_hbm.at[copy, :, twin]
+        for twin in range(packed_hbm.shape[2]):
+            target = packed_hbm.at[copy, :, twin]
             copies.append(pltpu.make_async_copy(row_scr, target, sems.at[copy, twin]))
             copies[-1].start()
     for copy in copies:
         copy.wait()
 
 
-def pack_first_kernel(qkv_ref, out_ref, packed_ref, row_scr, sems):
-    rows = qkv_ref.shape[0]
-    width = qkv_ref.shape[1] // 3
+def pack_first_kernel(qkv_hbm, out_hbm, packed_hbm, qkv_ref, out_ref, row_scr, in_sems, sems):
+    rows, width = out_ref.shape
+    pairs = [(out_hbm, out_ref)]
+    for kind in range(3):
+        span = slice(kind * width, (kind + 1) * width)
+        pairs.append((qkv_hbm.at[:, span], qkv_ref.at[:, span]))
+    loads = [pltpu.make_async_copy(source, target, in_sems.at[i]) for i, (source, target) in enumerate(pairs)]
+    for load in loads:
+        load.start()
     cores, depth = row_scr.shape[:2]
     low = low_lanes((rows, 128))
 
@@ -70,6 +76,9 @@
         start = kind * width + number * 128
         return qkv_ref[:, start : start + 128]
 
+    for load in loads:
+        load.wait()
+    copies = []
     for core in range(cores):
         for z in range(depth):
             start = core * (width // cores) + z * 128
@@ -86,7 +95,13 @@
             else:
                 parts.append(jnp.where(low, turned(one), two))
             row_scr[core, z] = jnp.concatenate(parts, axis=1).astype(BF)
-    replicate(row_scr, packed_ref, sems, 3)
+        for copy in range(packed_hbm.shape[0]):
+            for twin in range(packed_hbm.shape[3]):
+                target = packed_hbm.at[copy, core, :, twin]
+                copies.append(pltpu.make_async_copy(row_scr.at[core], target, sems.at[core, copy, twin]))
+                copies[-1].start()
+    for copy in copies:
+        copy.wait()
 
 
 def pack_depth_kernel(place_ref, up_ref, down_ref, *piece_refs):
@@ -108,7 +123,7 @@
         for core in range(cores):
             start = core * half_h
             row_scr[core, z] = jnp.concatenate([piece_ref[:, start : start + half_h], piece_ref[:, span + start : span + start + half_h]], axis=1)
-    replicate(row_scr, packed_ref, sems, 2)
+    replicate(row_scr, packed_ref, sems)
 
 
 def take_kernel(served_ref, part_ref):
@@ -302,16 +317,22 @@
     def shape(*dims):
         return jax.ShapeDtypeStruct(dims, BF)
 
-    w_qkv, w_out, w_up, w_down, hidden_in = (pltpu.with_memory_space_constraint(x, pltpu.HBM) for x in (w_qkv, w_out, w_up, w_down, hidden_in))
+    w_qkv, w_out, hidden_in = (pltpu.with_memory_space_constraint(x, pltpu.HBM) for x in (w_qkv, w_out, hidden_in))
     first_cols = 128 + 384
     sems = pltpu.SemaphoreType.DMA((copies, twins))
     packed = call(
         pack_first_kernel,
         "pack_first",
         shape(copies, cores, depth, twins, unit, first_cols),
-        [VM, VM],
+        [HB, HB],
         out_specs=HB,
-        scratch_shapes=[pltpu.VMEM((cores, depth, unit, first_cols), BF), sems],
+        scratch_shapes=[
+            pltpu.VMEM((unit, 3 * width), F32),
+            pltpu.VMEM((unit, width), F32),
+            pltpu.VMEM((cores, depth, unit, first_cols), BF),
+            pltpu.SemaphoreType.DMA((4,)),
+            pltpu.SemaphoreType.DMA((cores, copies, twins)),
+        ],
     )(w_qkv, w_out)
     served = exchange(packed.reshape(-1, unit, first_cols), GROUP + PART).reshape(width, first_cols)
     other_hidden = swapped(hidden_in)

time: 86.1 us -> 86.2 us (level)
  transfers between devices with their start and end apart: 22 -> 22, of which waited for: 13 -> 12; matrix products, arithmetic and copies ran while one was open for 0% -> 0% of each run, Pallas kernels for 23% -> 23%
where the time goes in v7:
time: 86.2 us; the launch traced here: 85.5 us
  starting transfers between devices  41.3 us (48%)
  Pallas kernels  22 us (26%)
  waiting for transfers between devices  20.6 us (24%)
    all_to_all x2, starting transfers between devices, exchange(): return lax.all_to_all(value, axes, split_axis=0, concat_axis=0, tiled=True)  18.1 us
    ppermute x12, waiting for transfers between devices, moved(): lax.ppermute(value, 'zz', [(i, i ^ bits) for i in range(lax.axis_size('zz...  15.2 us
    ppermute x12, starting transfers between devices, moved(): lax.ppermute(value, 'zz', [(i, i ^ bits) for i in range(lax.axis_size('zz...  13.6 us
    ppermute x8, starting transfers between devices, swapped(): return lax.ppermute(value, 'cc', [(0, 1), (1, 0)])  9.54 us
    pallas_call x1, Pallas kernels, body(): call(attend_kernel, 'attend', (shape(few, 128), shape(rows, 128), shape(f...  6.48 us
    ppermute x8, waiting for transfers between devices, swapped(): return lax.ppermute(value, 'cc', [(0, 1), (1, 0)])  4.89 us
    pallas_call x1, Pallas kernels, body(): call(project_kernel, 'project', (shape(few, width), shape(share, width)),...  2.86 us
    pallas_call x2, Pallas kernels, body(): call(functools.partial(feed_kernel, targets), 'feed', (shape(share, width...  2.8 us
  transfers between devices with their start and end apart: 22, of which 12 were waited for; matrix products, arithmetic and copies ran while one was open for 0% of the time, Pallas kernels for 23%

profile of v7, /device:TPU:1, one launch (start us, length us, event | category | flops | bytes accessed | tf_op | source)
XLA Modules:
  0.0 85.5 jit_solution(1256282295296418655)
XLA Ops:
  0.7 1.5 %collective-permute-start.3 = (bf16[512,1024]{1,0:T(8,128)(2,1)}, bf16[512,1024]{1,0:T(8,128)(2,1)S(1)}, u32[]{:S(2)}, u32[]{:S(2)}) collective-permute-start(bf16[512,1024]{1,0:T(8,128)(2,1)} %refs_12_.1), channel_id=1, source_target_pairs={{0,8},{8,0},{1,9},{9,1},{2,10},{10,2},{3,11},{11,3},{4,12},{12,4},... | collective-permute-start | bytes 3145736 | tf_op jit(solution)/shard_map/ppermute | solution.py:289
  2.2 2.2 %pack_first.1 = bf16[8,2,4,2,8,512]{5,4,3,2,1,0:T(8,128)(2,1)} custom-call(f32[8,3072]{1,0:T(8,128)} %qkv_hbm.1, f32[8,1024]{1,0:T(8,128)} %out_hbm.1), custom_call_target="tpu_custom_call" | custom-call | bytes 1048576 | tf_op jit(solution)/shard_map/pack_first/pallas_call | solution.py:323
  4.4 10.2 %all-to-all-start = ((bf16[128,8,512]{2,1,0:T(8,128)(2,1)}), bf16[128,8,512]{2,1,0:T(8,128)(2,1)S(1)}, u32[]{:S(2)}, u32[]{:S(2)}) async-start(bf16[128,8,512]{2,1,0:T(8,128)(2,1)} %bitcast.3), calls=%async_computation | async-start | bytes 2097152 | tf_op jit(solution)/shard_map/all_to_all | solution.py:285
  15.2 1.6 %collective-permute-start = (bf16[8,2048]{1,0:T(8,128)(2,1)S(1)}, bf16[8,2048]{1,0:T(8,128)(2,1)S(1)}, u32[]{:S(2)}, u32[]{:S(2)}) collective-permute-start(bf16[8,2048]{1,0:T(8,128)(2,1)S(1)} %get-tuple-element.43), channel_id=1, source_target_pairs={{0,2},{2,0},{4,6},{6,4},{1,3},{3,1},{5,7},{7,5},{8,10},{10,8},{12,... | collective-permute-start | bytes 98312 | tf_op jit(solution)/shard_map/ppermute | solution.py:293
  16.8 2.9 %collective-permute-start.1 = (bf16[8,2048]{1,0:T(8,128)(2,1)S(1)}, bf16[8,2048]{1,0:T(8,128)(2,1)S(1)}, u32[]{:S(2)}, u32[]{:S(2)}) collective-permute-start(bf16[8,2048]{1,0:T(8,128)(2,1)S(1)} %get-tuple-element.44), channel_id=1, source_target_pairs={{0,4},{2,6},{4,0},{6,2},{1,5},{3,7},{5,1},{7,3},{8,12},{10,14},{12... | collective-permute-start | bytes 98312 | tf_op jit(solution)/shard_map/ppermute | solution.py:293
  19.8 1.3 %collective-permute-start.4 = (s32[512]{0:T(512)S(1)}, s32[512]{0:T(512)S(1)}, u32[]{:S(2)}, u32[]{:S(2)}) collective-permute-start(s32[512]{0:T(512)S(1)} %copy-done.6), channel_id=1, source_target_pairs={{0,8},{8,0},{1,9},{9,1},{2,10},{10,2},{3,11},{11,3},{4,12},{12,4},... | collective-permute-start | bytes 6152 | tf_op jit(solution)/shard_map/ppermute | solution.py:289
  21.1 0.8 collective-permute-done.4
  21.9 1.6 %collective-permute-done.refs_1_ = bf16[8,2048]{1,0:T(8,128)(2,1)S(1)} collective-permute-done((bf16[8,2048]{1,0:T(8,128)(2,1)S(1)}, bf16[8,2048]{1,0:T(8,128)(2,1)S(1)}, u32[]{:S(2)}, u32[]{:S(2)}) %collective-permute-start) | collective-permute-done | bytes 32800 | tf_op jit(solution)/shard_map/ppermute | solution.py:293
  23.5 6.8 %collective-permute-done.1.refs_2_ = bf16[8,2048]{1,0:T(8,128)(2,1)S(1)} collective-permute-done((bf16[8,2048]{1,0:T(8,128)(2,1)S(1)}, bf16[8,2048]{1,0:T(8,128)(2,1)S(1)}, u32[]{:S(2)}, u32[]{:S(2)}) %collective-permute-start.1) | collective-permute-done | bytes 32800 | tf_op jit(solution)/shard_map/ppermute | solution.py:293
  30.3 2.1 %pack_rest.1 = bf16[8,2,2,4,8,1024]{5,4,3,2,1,0:T(8,128)(2,1)} custom-call(s32[3]{0:T(128)S(1)} %pad_add_fusion.place_ref, bf16[8,2048]{1,0:T(8,128)(2,1)S(1)} %get-tuple-element.46.refs_0_, bf16[8,2048]{1,0:T(8,128)(2,1)S(1)} %collective-permute-done.refs_1_, bf16[8,2048]{1,0:T(8,128)(2,1)S(1)} %collective-permute-done.1.refs_2_, ...), custom_call_target="tpu_custom_call" | custom-call | bytes 1048576 | tf_op jit(solution)/shard_map/pack_rest/pallas_call | solution.py:342
  32.9 7.9 %all-to-all-start.1 = ((bf16[32,4,8,1024]{3,2,1,0:T(8,128)(2,1)}), bf16[32,4,8,1024]{3,2,1,0:T(8,128)(2,1)S(1)}, u32[]{:S(2)}, u32[]{:S(2)}) async-start(bf16[32,4,8,1024]{3,2,1,0:T(8,128)(2,1)} %bitcast.5), calls=%async_computation.1 | async-start | bytes 4194304 | tf_op jit(solution)/shard_map/all_to_all | solution.py:285
  41.5 6.5 %attend.1 = (bf16[256,128]{1,0:T(8,128)(2,1)S(1)}, bf16[512,128]{1,0:T(8,128)(2,1)S(1)}, bf16[768,128]{1,0:T(8,128)(2,1)S(1)}) custom-call(s32[3]{0:T(128)S(1)} %pad_add_fusion.place_ref, bf16[512,1024]{1,0:T(8,128)(2,1)} %refs_12_.1, bf16[512,1024]{1,0:T(8,128)(2,1)} %copy-done.8, bf16[1024,512]{1,0:T(8,128)(2,1)S(1)} %bitcast.14, s32[4,128]{1,0:T(4,128)S(1)} %bitcast.21, ...), custom_call_target="tpu_custom_call" | custom-call | flops 5000000000 | bytes 1048576 | tf_op jit(solution)/shard_map/attend/pallas_call | solution.py:358
  48.6 1.1 %collective-permute-done.5.got_ref = bf16[768,128]{1,0:T(8,128)(2,1)S(1)} collective-permute-done((bf16[768,128]{1,0:T(8,128)(2,1)S(1)}, bf16[768,128]{1,0:T(8,128)(2,1)S(1)}, u32[]{:S(2)}, u32[]{:S(2)}) %collective-permute-start.5) | collective-permute-done | bytes 196640 | tf_op jit(solution)/shard_map/ppermute | solution.py:289
  49.8 1.6 %collective-permute-start.8 = (bf16[1024,128]{1,0:T(8,128)(2,1)S(1)}, bf16[1024,128]{1,0:T(8,128)(2,1)S(1)}, u32[]{:S(2)}, u32[]{:S(2)}) collective-permute-start(bf16[1024,128]{1,0:T(8,128)(2,1)S(1)} %collective-permute-done.7.refs_7_), channel_id=1, source_target_pairs={{0,2},{2,0},{4,6},{6,4},{1,3},{3,1},{5,7},{7,5},{8,10},{10,8},{12,... | collective-permute-start | bytes 786440 | tf_op jit(solution)/shard_map/ppermute | solution.py:293
  52.1 2.1 %collective-permute-start.11 = (bf16[256,256]{1,0:T(8,128)(2,1)S(1)}, bf16[256,256]{1,0:T(8,128)(2,1)S(1)}, u32[]{:S(2)}, u32[]{:S(2)}) collective-permute-start(bf16[256,256]{1,0:T(8,128)(2,1)S(1)} %join.1.refs_0_), channel_id=1, source_target_pairs={{0,6},{2,4},{4,2},{6,0},{1,7},{3,5},{5,3},{7,1},{8,14},{10,12},{12... | collective-permute-start | bytes 393224 | tf_op jit(solution)/shard_map/ppermute | solution.py:293
  54.3 1.2 %collective-permute-start.9 = (bf16[256,256]{1,0:T(8,128)(2,1)S(1)}, bf16[256,256]{1,0:T(8,128)(2,1)S(1)}, u32[]{:S(2)}, u32[]{:S(2)}) collective-permute-start(bf16[256,256]{1,0:T(8,128)(2,1)S(1)} %join.1.refs_0_), channel_id=1, source_target_pairs={{0,2},{2,0},{4,6},{6,4},{1,3},{3,1},{5,7},{7,5},{8,10},{10,8},{12,... | collective-permute-start | bytes 393224 | tf_op jit(solution)/shard_map/ppermute | solution.py:293
  55.4 1.5 %collective-permute-start.12 = (bf16[1024,128]{1,0:T(8,128)(2,1)S(1)}, bf16[1024,128]{1,0:T(8,128)(2,1)S(1)}, u32[]{:S(2)}, u32[]{:S(2)}) collective-permute-start(bf16[1024,128]{1,0:T(8,128)(2,1)S(1)} %take.1.refs_4_), channel_id=1, source_target_pairs={{0,8},{8,0},{1,9},{9,1},{2,10},{10,2},{3,11},{11,3},{4,12},{12,4},... | collective-permute-start | bytes 786440 | tf_op jit(solution)/shard_map/ppermute | solution.py:289
  56.9 0.9 %collective-permute-done.11.refs_3_ = bf16[256,256]{1,0:T(8,128)(2,1)S(1)} collective-permute-done((bf16[256,256]{1,0:T(8,128)(2,1)S(1)}, bf16[256,256]{1,0:T(8,128)(2,1)S(1)}, u32[]{:S(2)}, u32[]{:S(2)}) %collective-permute-start.11) | collective-permute-done | bytes 131104 | tf_op jit(solution)/shard_map/ppermute | solution.py:293
  57.8 1.6 %collective-permute-start.13 = (bf16[1024,128]{1,0:T(8,128)(2,1)S(1)}, bf16[1024,128]{1,0:T(8,128)(2,1)S(1)}, u32[]{:S(2)}, u32[]{:S(2)}) collective-permute-start(bf16[1024,128]{1,0:T(8,128)(2,1)S(1)} %collective-permute-done.6.refs_5_), channel_id=1, source_target_pairs={{0,8},{8,0},{1,9},{9,1},{2,10},{10,2},{3,11},{11,3},{4,12},{12,4},... | collective-permute-start | bytes 786440 | tf_op jit(solution)/shard_map/ppermute | solution.py:289
  59.4 2.8 %collective-permute-done.10.refs_2_ = bf16[256,256]{1,0:T(8,128)(2,1)S(1)} collective-permute-done((bf16[256,256]{1,0:T(8,128)(2,1)S(1)}, bf16[256,256]{1,0:T(8,128)(2,1)S(1)}, u32[]{:S(2)}, u32[]{:S(2)}) %collective-permute-start.10) | collective-permute-done | bytes 131104 | tf_op jit(solution)/shard_map/ppermute | solution.py:293
  62.2 1.8 %collective-permute-start.15 = (bf16[1024,128]{1,0:T(8,128)(2,1)S(1)}, bf16[1024,128]{1,0:T(8,128)(2,1)S(1)}, u32[]{:S(2)}, u32[]{:S(2)}) collective-permute-start(bf16[1024,128]{1,0:T(8,128)(2,1)S(1)} %collective-permute-done.7.refs_7_), channel_id=1, source_target_pairs={{0,8},{8,0},{1,9},{9,1},{2,10},{10,2},{3,11},{11,3},{4,12},{12,4},... | collective-permute-start | bytes 786440 | tf_op jit(solution)/shard_map/ppermute | solution.py:289
  64.3 0.8 collective-permute-done.15.refs_11_
  65.5 2.9 %project.1 = (bf16[256,1024]{1,0:T(8,128)(2,1)S(1)}, bf16[64,1024]{1,0:T(8,128)(2,1)S(1)}) custom-call(s32[3]{0:T(128)S(1)} %pad_add_fusion.place_ref, bf16[256,256]{1,0:T(8,128)(2,1)S(1)} %join.1.refs_0_, bf16[256,256]{1,0:T(8,128)(2,1)S(1)} %collective-permute-done.9.refs_1_, bf16[256,256]{1,0:T(8,128)(2,1)S(1)} %collective-permute-done.10.refs_2_, ...), custom_call_target="tpu_custom_call" | custom-call | flops 2000000000 | bytes 1048576 | tf_op jit(solution)/shard_map/project/pallas_call | solution.py:380
  69.2 0.9 %collective-permute-start.16 = (bf16[1024,1024]{1,0:T(8,128)(2,1)S(1)}, bf16[1024,1024]{1,0:T(8,128)(2,1)S(1)}, u32[]{:S(2)}, u32[]{:S(2)}) collective-permute-start(bf16[1024,1024]{1,0:T(8,128)(2,1)S(1)} %bitcast.15), channel_id=1, source_target_pairs={{0,8},{8,0},{1,9},{9,1},{2,10},{10,2},{3,11},{11,3},{4,12},{12,4},... | collective-permute-start | bytes 6291464 | tf_op jit(solution)/shard_map/ppermute | solution.py:289
  70.2 2.0 %own_feed.1 = (bf16[256,1024]{1,0:T(8,128)(2,1)S(1)}, f32[256,1024]{1,0:T(8,128)S(1)}) custom-call(bf16[256,1024]{1,0:T(8,128)(2,1)} %copy-done.7, bf16[1024,1024]{1,0:T(8,128)(2,1)S(1)} %bitcast.16), custom_call_target="tpu_custom_call" | custom-call | flops 2000000000 | bytes 1048576 | tf_op jit(solution)/shard_map/own_feed/pallas_call | solution.py:397
  72.1 1.8 %collective-permute-done.16.theirs_ref = bf16[1024,1024]{1,0:T(8,128)(2,1)S(1)} collective-permute-done((bf16[1024,1024]{1,0:T(8,128)(2,1)S(1)}, bf16[1024,1024]{1,0:T(8,128)(2,1)S(1)}, u32[]{:S(2)}, u32[]{:S(2)}) %collective-permute-start.16) | collective-permute-done | bytes 2097184 | tf_op jit(solution)/shard_map/ppermute | solution.py:289
  73.9 1.4 %feed.3 = (bf16[64,1024]{1,0:T(8,128)(2,1)S(1)}, bf16[64,1024]{1,0:T(8,128)(2,1)S(1)}) custom-call(s32[3]{0:T(128)S(1)} %pad_add_fusion.place_ref, bf16[256,1024]{1,0:T(8,128)(2,1)S(1)} %get-tuple-element.71.arrived_ref, f32[256,1024]{1,0:T(8,128)S(1)} %get-tuple-element.72.own_ref, bf16[1024,1024]{1,0:T(8,128)(2,1)S(1)} %collective-permute-done.16.theirs_ref), custom_call_target="tpu_custom_call" | custom-call | flops 1000000000 | bytes 1048576 | tf_op jit(solution)/shard_map/feed/pallas_call | solution.py:407
  75.3 2.7 %collective-permute-start.18 = (bf16[64,1024]{1,0:T(8,128)(2,1)S(1)}, bf16[64,1024]{1,0:T(8,128)(2,1)S(1)}, u32[]{:S(2)}, u32[]{:S(2)}) collective-permute-start(bf16[64,1024]{1,0:T(8,128)(2,1)S(1)} %get-tuple-element.75), channel_id=1, source_target_pairs={{0,4},{2,6},{4,0},{6,2},{1,5},{3,7},{5,1},{7,3},{8,12},{10,14},{12... | collective-permute-start | bytes 393224 | tf_op jit(solution)/shard_map/ppermute | solution.py:293
  78.7 1.4 %feed.2 = (bf16[64,1024]{1,0:T(8,128)(2,1)S(1)}, bf16[64,1024]{1,0:T(8,128)(2,1)S(1)}) custom-call(s32[3]{0:T(128)S(1)} %pad_add_fusion.place_ref, bf16[256,1024]{1,0:T(8,128)(2,1)S(1)} %get-tuple-element.71.arrived_ref, f32[256,1024]{1,0:T(8,128)S(1)} %get-tuple-element.72.own_ref, bf16[1024,1024]{1,0:T(8,128)(2,1)S(1)} %collective-permute-done.16.theirs_ref), custom_call_target="tpu_custom_call" | custom-call | flops 1000000000 | bytes 1048576 | tf_op jit(solution)/shard_map/feed/pallas_call | solution.py:407
  80.2 1.4 %cache.1 = (bf16[512,128]{1,0:T(8,128)(2,1)}, bf16[512,128]{1,0:T(8,128)(2,1)}) custom-call(s32[3]{0:T(128)S(1)} %pad_add_fusion.place_ref, bf16[512,128]{1,0:T(8,128)(2,1)S(1)} %get-tuple-element.78.own_ref, bf16[768,128]{1,0:T(8,128)(2,1)S(1)} %collective-permute-done.5.got_ref), custom_call_target="tpu_custom_call" | custom-call | flops 1000000000 | bytes 1048576 | tf_op jit(solution)/shard_map/cache/pallas_call | solution.py:377
  81.6 2.9 %collective-permute-done.19.refs_3_ = bf16[64,1024]{1,0:T(8,128)(2,1)S(1)} collective-permute-done((bf16[64,1024]{1,0:T(8,128)(2,1)S(1)}, bf16[64,1024]{1,0:T(8,128)(2,1)S(1)}, u32[]{:S(2)}, u32[]{:S(2)}) %collective-permute-start.19) | collective-permute-done | bytes 131104 | tf_op jit(solution)/shard_map/ppermute | solution.py:293
  84.6 0.9 %final.1 = bf16[64,1024]{1,0:T(8,128)(2,1)} custom-call(bf16[64,1024]{1,0:T(8,128)(2,1)S(1)} %get-tuple-element.73.refs_0_, bf16[64,1024]{1,0:T(8,128)(2,1)S(1)} %collective-permute-done.17.refs_1_, bf16[64,1024]{1,0:T(8,128)(2,1)S(1)} %collective-permute-done.18.refs_2_, bf16[64,1024]{1,0:T(8,128)(2,1)S(1)} %collective-permute-done.19.refs_3_, ...), custom_call_target="tpu_custom_call" | custom-call | bytes 1048576 | tf_op jit(solution)/shard_map/final/pallas_call | solution.py:418
  (43 shorter events, 5.6 us)
Async XLA Ops:
  0.6 14.0 %copy-start.1 = (f32[8,4096]{1,0:T(8,128)S(1)}, f32[8,4096]{1,0:T(8,128)}, u32[]{:S(2)}) copy-start(f32[8,4096]{1,0:T(8,128)} %down_ref.1) | copy-start | bytes 393220
  0.6 14.0 %copy-start = (f32[8,4096]{1,0:T(8,128)S(1)}, f32[8,4096]{1,0:T(8,128)}, u32[]{:S(2)}) copy-start(f32[8,4096]{1,0:T(8,128)} %up_ref.1) | copy-start | bytes 393220
  0.7 19.1 %copy-start.6 = (s32[512]{0:T(512)S(1)}, s32[512]{0:T(512)}, u32[]{:S(2)}) copy-start(s32[512]{0:T(512)} %param.11) | copy-start | bytes 6148
  0.7 29.6 %collective-permute-start.3 = (bf16[512,1024]{1,0:T(8,128)(2,1)}, bf16[512,1024]{1,0:T(8,128)(2,1)S(1)}, u32[]{:S(2)}, u32[]{:S(2)}) collective-permute-start(bf16[512,1024]{1,0:T(8,128)(2,1)} %refs_12_.1), channel_id=1, source_target_pairs={{0,8},{8,0},{1,9},{9,1},{2,10},{10,2},{3,11},{11,3},{4,12},{12,4},... | collective-permute-start | bytes 3145736 | tf_op jit(solution)/shard_map/ppermute | solution.py:289
  4.4 28.5 %all-to-all-start = ((bf16[128,8,512]{2,1,0:T(8,128)(2,1)}), bf16[128,8,512]{2,1,0:T(8,128)(2,1)S(1)}, u32[]{:S(2)}, u32[]{:S(2)}) async-start(bf16[128,8,512]{2,1,0:T(8,128)(2,1)} %bitcast.3), calls=%async_computation | async-start | bytes 2097152 | tf_op jit(solution)/shard_map/all_to_all | solution.py:285
  15.2 8.3 %collective-permute-start = (bf16[8,2048]{1,0:T(8,128)(2,1)S(1)}, bf16[8,2048]{1,0:T(8,128)(2,1)S(1)}, u32[]{:S(2)}, u32[]{:S(2)}) collective-permute-start(bf16[8,2048]{1,0:T(8,128)(2,1)S(1)} %get-tuple-element.43), channel_id=1, source_target_pairs={{0,2},{2,0},{4,6},{6,4},{1,3},{3,1},{5,7},{7,5},{8,10},{10,8},{12,... | collective-permute-start | bytes 98312 | tf_op jit(solution)/shard_map/ppermute | solution.py:293
  16.8 13.5 %collective-permute-start.1 = (bf16[8,2048]{1,0:T(8,128)(2,1)S(1)}, bf16[8,2048]{1,0:T(8,128)(2,1)S(1)}, u32[]{:S(2)}, u32[]{:S(2)}) collective-permute-start(bf16[8,2048]{1,0:T(8,128)(2,1)S(1)} %get-tuple-element.44), channel_id=1, source_target_pairs={{0,4},{2,6},{4,0},{6,2},{1,5},{3,7},{5,1},{7,3},{8,12},{10,14},{12... | collective-permute-start | bytes 98312 | tf_op jit(solution)/shard_map/ppermute | solution.py:293
  19.8 10.5 %collective-permute-start.2 = (bf16[8,2048]{1,0:T(8,128)(2,1)S(1)}, bf16[8,2048]{1,0:T(8,128)(2,1)S(1)}, u32[]{:S(2)}, u32[]{:S(2)}) collective-permute-start(bf16[8,2048]{1,0:T(8,128)(2,1)S(1)} %get-tuple-element.45), channel_id=1, source_target_pairs={{0,6},{2,4},{4,2},{6,0},{1,7},{3,5},{5,3},{7,1},{8,14},{10,12},{12... | collective-permute-start | bytes 98312 | tf_op jit(solution)/shard_map/ppermute | solution.py:293
  19.8 2.1 %collective-permute-start.4 = (s32[512]{0:T(512)S(1)}, s32[512]{0:T(512)S(1)}, u32[]{:S(2)}, u32[]{:S(2)}) collective-permute-start(s32[512]{0:T(512)S(1)} %copy-done.6), channel_id=1, source_target_pairs={{0,8},{8,0},{1,9},{9,1},{2,10},{10,2},{3,11},{11,3},{4,12},{12,4},... | collective-permute-start | bytes 6152 | tf_op jit(solution)/shard_map/ppermute | solution.py:289
  30.3 2.6 %copy-start.8 = (bf16[512,1024]{1,0:T(8,128)(2,1)}, bf16[512,1024]{1,0:T(8,128)(2,1)S(1)}, u32[]{:S(2)}) copy-start(bf16[512,1024]{1,0:T(8,128)(2,1)S(1)} %collective-permute-done.3.other_hbm) | copy-start | bytes 3145732
  32.9 36.4 %all-to-all-start.1 = ((bf16[32,4,8,1024]{3,2,1,0:T(8,128)(2,1)}), bf16[32,4,8,1024]{3,2,1,0:T(8,128)(2,1)S(1)}, u32[]{:S(2)}, u32[]{:S(2)}) async-start(bf16[32,4,8,1024]{3,2,1,0:T(8,128)(2,1)} %bitcast.5), calls=%async_computation.1 | async-start | bytes 4194304 | tf_op jit(solution)/shard_map/all_to_all | solution.py:285
  40.8 9.0 %collective-permute-start.7 = (bf16[1024,128]{1,0:T(8,128)(2,1)S(1)}, bf16[1024,128]{1,0:T(8,128)(2,1)S(1)}, u32[]{:S(2)}, u32[]{:S(2)}) collective-permute-start(bf16[1024,128]{1,0:T(8,128)(2,1)S(1)} %take.1.refs_4_), channel_id=1, source_target_pairs={{0,6},{2,4},{4,2},{6,0},{1,7},{3,5},{5,3},{7,1},{8,14},{10,12},{12... | collective-permute-start | bytes 786440 | tf_op jit(solution)/shard_map/ppermute | solution.py:293
  41.5 8.3 %collective-permute-start.6 = (bf16[1024,128]{1,0:T(8,128)(2,1)S(1)}, bf16[1024,128]{1,0:T(8,128)(2,1)S(1)}, u32[]{:S(2)}, u32[]{:S(2)}) collective-permute-start(bf16[1024,128]{1,0:T(8,128)(2,1)S(1)} %take.1.refs_4_), channel_id=1, source_target_pairs={{0,2},{2,0},{4,6},{6,4},{1,3},{3,1},{5,7},{7,5},{8,10},{10,8},{12,... | collective-permute-start | bytes 786440 | tf_op jit(solution)/shard_map/ppermute | solution.py:293
  41.5 24.0 %copy-start.4 = (f32[1024]{0:T(1024)S(1)}, f32[1024]{0:T(1024)}, u32[]{:S(2)}) copy-start(f32[1024]{0:T(1024)} %param.16) | copy-start | bytes 12292
  41.5 24.0 %copy-start.5 = (f32[1024]{0:T(1024)S(1)}, f32[1024]{0:T(1024)}, u32[]{:S(2)}) copy-start(f32[1024]{0:T(1024)} %param.17) | copy-start | bytes 12292
  48.0 1.7 %collective-permute-start.5 = (bf16[768,128]{1,0:T(8,128)(2,1)S(1)}, bf16[768,128]{1,0:T(8,128)(2,1)S(1)}, u32[]{:S(2)}, u32[]{:S(2)}) collective-permute-start(bf16[768,128]{1,0:T(8,128)(2,1)S(1)} %get-tuple-element.54), channel_id=1, source_target_pairs={{0,8},{8,0},{1,9},{9,1},{2,10},{10,2},{3,11},{11,3},{4,12},{12,4},... | collective-permute-start | bytes 589832 | tf_op jit(solution)/shard_map/ppermute | solution.py:289
  49.8 14.2 %collective-permute-start.8 = (bf16[1024,128]{1,0:T(8,128)(2,1)S(1)}, bf16[1024,128]{1,0:T(8,128)(2,1)S(1)}, u32[]{:S(2)}, u32[]{:S(2)}) collective-permute-start(bf16[1024,128]{1,0:T(8,128)(2,1)S(1)} %collective-permute-done.7.refs_7_), channel_id=1, source_target_pairs={{0,2},{2,0},{4,6},{6,4},{1,3},{3,1},{5,7},{7,5},{8,10},{10,8},{12,... | collective-permute-start | bytes 786440 | tf_op jit(solution)/shard_map/ppermute | solution.py:293
  52.1 5.7 %collective-permute-start.11 = (bf16[256,256]{1,0:T(8,128)(2,1)S(1)}, bf16[256,256]{1,0:T(8,128)(2,1)S(1)}, u32[]{:S(2)}, u32[]{:S(2)}) collective-permute-start(bf16[256,256]{1,0:T(8,128)(2,1)S(1)} %join.1.refs_0_), channel_id=1, source_target_pairs={{0,6},{2,4},{4,2},{6,0},{1,7},{3,5},{5,3},{7,1},{8,14},{10,12},{12... | collective-permute-start | bytes 393224 | tf_op jit(solution)/shard_map/ppermute | solution.py:293
  54.3 8.0 %collective-permute-start.10 = (bf16[256,256]{1,0:T(8,128)(2,1)S(1)}, bf16[256,256]{1,0:T(8,128)(2,1)S(1)}, u32[]{:S(2)}, u32[]{:S(2)}) collective-permute-start(bf16[256,256]{1,0:T(8,128)(2,1)S(1)} %join.1.refs_0_), channel_id=1, source_target_pairs={{0,4},{2,6},{4,0},{6,2},{1,5},{3,7},{5,1},{7,3},{8,12},{10,14},{12... | collective-permute-start | bytes 393224 | tf_op jit(solution)/shard_map/ppermute | solution.py:293
  54.3 9.7 %collective-permute-start.9 = (bf16[256,256]{1,0:T(8,128)(2,1)S(1)}, bf16[256,256]{1,0:T(8,128)(2,1)S(1)}, u32[]{:S(2)}, u32[]{:S(2)}) collective-permute-start(bf16[256,256]{1,0:T(8,128)(2,1)S(1)} %join.1.refs_0_), channel_id=1, source_target_pairs={{0,2},{2,0},{4,6},{6,4},{1,3},{3,1},{5,7},{7,5},{8,10},{10,8},{12,... | collective-permute-start | bytes 393224 | tf_op jit(solution)/shard_map/ppermute | solution.py:293
  55.4 8.9 %collective-permute-start.12 = (bf16[1024,128]{1,0:T(8,128)(2,1)S(1)}, bf16[1024,128]{1,0:T(8,128)(2,1)S(1)}, u32[]{:S(2)}, u32[]{:S(2)}) collective-permute-start(bf16[1024,128]{1,0:T(8,128)(2,1)S(1)} %take.1.refs_4_), channel_id=1, source_target_pairs={{0,8},{8,0},{1,9},{9,1},{2,10},{10,2},{3,11},{11,3},{4,12},{12,4},... | collective-permute-start | bytes 786440 | tf_op jit(solution)/shard_map/ppermute | solution.py:289
  57.8 6.5 %collective-permute-start.13 = (bf16[1024,128]{1,0:T(8,128)(2,1)S(1)}, bf16[1024,128]{1,0:T(8,128)(2,1)S(1)}, u32[]{:S(2)}, u32[]{:S(2)}) collective-permute-start(bf16[1024,128]{1,0:T(8,128)(2,1)S(1)} %collective-permute-done.6.refs_5_), channel_id=1, source_target_pairs={{0,8},{8,0},{1,9},{9,1},{2,10},{10,2},{3,11},{11,3},{4,12},{12,4},... | collective-permute-start | bytes 786440 | tf_op jit(solution)/shard_map/ppermute | solution.py:289
  62.2 2.9 %collective-permute-start.15 = (bf16[1024,128]{1,0:T(8,128)(2,1)S(1)}, bf16[1024,128]{1,0:T(8,128)(2,1)S(1)}, u32[]{:S(2)}, u32[]{:S(2)}) collective-permute-start(bf16[1024,128]{1,0:T(8,128)(2,1)S(1)} %collective-permute-done.7.refs_7_), channel_id=1, source_target_pairs={{0,8},{8,0},{1,9},{9,1},{2,10},{10,2},{3,11},{11,3},{4,12},{12,4},... | collective-permute-start | bytes 786440 | tf_op jit(solution)/shard_map/ppermute | solution.py:289
  64.0 1.5 %collective-permute-start.14 = (bf16[1024,128]{1,0:T(8,128)(2,1)S(1)}, bf16[1024,128]{1,0:T(8,128)(2,1)S(1)}, u32[]{:S(2)}, u32[]{:S(2)}) collective-permute-start(bf16[1024,128]{1,0:T(8,128)(2,1)S(1)} %collective-permute-done.8.refs_6_), channel_id=1, source_target_pairs={{0,8},{8,0},{1,9},{9,1},{2,10},{10,2},{3,11},{11,3},{4,12},{12,4},... | collective-permute-start | bytes 786440 | tf_op jit(solution)/shard_map/ppermute | solution.py:289
  68.4 0.8 copy-start.7
  69.2 4.7 %collective-permute-start.16 = (bf16[1024,1024]{1,0:T(8,128)(2,1)S(1)}, bf16[1024,1024]{1,0:T(8,128)(2,1)S(1)}, u32[]{:S(2)}, u32[]{:S(2)}) collective-permute-start(bf16[1024,1024]{1,0:T(8,128)(2,1)S(1)} %bitcast.15), channel_id=1, source_target_pairs={{0,8},{8,0},{1,9},{9,1},{2,10},{10,2},{3,11},{11,3},{4,12},{12,4},... | collective-permute-start | bytes 6291464 | tf_op jit(solution)/shard_map/ppermute | solution.py:289
  75.3 6.3 %collective-permute-start.18 = (bf16[64,1024]{1,0:T(8,128)(2,1)S(1)}, bf16[64,1024]{1,0:T(8,128)(2,1)S(1)}, u32[]{:S(2)}, u32[]{:S(2)}) collective-permute-start(bf16[64,1024]{1,0:T(8,128)(2,1)S(1)} %get-tuple-element.75), channel_id=1, source_target_pairs={{0,4},{2,6},{4,0},{6,2},{1,5},{3,7},{5,1},{7,3},{8,12},{10,14},{12... | collective-permute-start | bytes 393224 | tf_op jit(solution)/shard_map/ppermute | solution.py:293
  78.1 6.5 %collective-permute-start.19 = (bf16[64,1024]{1,0:T(8,128)(2,1)S(1)}, bf16[64,1024]{1,0:T(8,128)(2,1)S(1)}, u32[]{:S(2)}, u32[]{:S(2)}) collective-permute-start(bf16[64,1024]{1,0:T(8,128)(2,1)S(1)} %get-tuple-element.76), channel_id=1, source_target_pairs={{0,6},{2,4},{4,2},{6,0},{1,7},{3,5},{5,3},{7,1},{8,14},{10,12},{12... | collective-permute-start | bytes 393224 | tf_op jit(solution)/shard_map/ppermute | solution.py:293
  80.1 4.5 %copy-start.2 = (f32[1024]{0:T(1024)S(1)}, f32[1024]{0:T(1024)}, u32[]{:S(2)}) copy-start(f32[1024]{0:T(1024)} %param.18) | copy-start | bytes 12292
  80.1 4.5 %copy-start.3 = (f32[1024]{0:T(1024)S(1)}, f32[1024]{0:T(1024)}, u32[]{:S(2)}) copy-start(f32[1024]{0:T(1024)} %param.19) | copy-start | bytes 12292
  80.1 4.4 %collective-permute-start.17 = (bf16[64,1024]{1,0:T(8,128)(2,1)S(1)}, bf16[64,1024]{1,0:T(8,128)(2,1)S(1)}, u32[]{:S(2)}, u32[]{:S(2)}) collective-permute-start(bf16[64,1024]{1,0:T(8,128)(2,1)S(1)} %get-tuple-element.74), channel_id=1, source_target_pairs={{0,2},{2,0},{4,6},{6,4},{1,3},{3,1},{5,7},{7,5},{8,10},{10,8},{12,... | collective-permute-start | bytes 393224 | tf_op jit(solution)/shard_map/ppermute | solution.py:293

commit v8 on v7

--- a/solution.py
+++ b/solution.py
@@ -317,6 +317,7 @@
     def shape(*dims):
         return jax.ShapeDtypeStruct(dims, BF)
 
+    plain_hidden = hidden_in
     w_qkv, w_out, hidden_in = (pltpu.with_memory_space_constraint(x, pltpu.HBM) for x in (w_qkv, w_out, hidden_in))
     first_cols = 128 + 384
     sems = pltpu.SemaphoreType.DMA((copies, twins))
@@ -390,7 +391,7 @@
             pltpu.VMEM((few, width), BF),
             pltpu.SemaphoreType.DMA((depth,)),
         ],
-    )(place, *pieces, *out_parts, *their_parts, hidden_in, ln1_gain[None, :], ln1_shift[None, :])
+    )(place, *pieces, *out_parts, *their_parts, plain_hidden, ln1_gain[None, :], ln1_shift[None, :])
     rest, norm = lax.optimization_barrier((rest, norm))
     norm = pltpu.with_memory_space_constraint(norm, pltpu.HBM)
     theirs = swapped(rest)

time: 86.2 us -> 86.2 us (level)
  transfers between devices with their start and end apart: 22 -> 22, of which waited for: 12 -> 11; matrix products, arithmetic and copies ran while one was open for 0% -> 0% of each run, Pallas kernels for 23% -> 23%
where the time goes in v8:
time: 86.2 us; the launch traced here: 85.5 us
  starting transfers between devices  41.2 us (48%)
  Pallas kernels  22 us (26%)
  waiting for transfers between devices  20.6 us (24%)
    all_to_all x2, starting transfers between devices, exchange(): return lax.all_to_all(value, axes, split_axis=0, concat_axis=0, tiled=True)  18.1 us
    ppermute x12, waiting for transfers between devices, moved(): lax.ppermute(value, 'zz', [(i, i ^ bits) for i in range(lax.axis_size('zz...  15.2 us
    ppermute x12, starting transfers between devices, moved(): lax.ppermute(value, 'zz', [(i, i ^ bits) for i in range(lax.axis_size('zz...  13.7 us
    ppermute x8, starting transfers between devices, swapped(): return lax.ppermute(value, 'cc', [(0, 1), (1, 0)])  9.39 us
    pallas_call x1, Pallas kernels, body(): call(attend_kernel, 'attend', (shape(few, 128), shape(rows, 128), shape(f...  6.65 us
    ppermute x8, waiting for transfers between devices, swapped(): return lax.ppermute(value, 'cc', [(0, 1), (1, 0)])  4.86 us
    pallas_call x2, Pallas kernels, body(): call(functools.partial(feed_kernel, targets), 'feed', (shape(share, width...  2.8 us
    pallas_call x1, Pallas kernels, body(): call(project_kernel, 'project', (shape(few, width), shape(share, width)),...  2.71 us
  transfers between devices with their start and end apart: 22, of which 11 were waited for; matrix products, arithmetic and copies ran while one was open for 0% of the time, Pallas kernels for 23%

profile of v8, /device:TPU:1, one launch (start us, length us, event | category | flops | bytes accessed | tf_op | source)
XLA Modules:
  0.0 85.5 jit_solution(3500618878383273842)
XLA Ops:
  0.7 1.5 %collective-permute-start.3 = (bf16[512,1024]{1,0:T(8,128)(2,1)}, bf16[512,1024]{1,0:T(8,128)(2,1)S(1)}, u32[]{:S(2)}, u32[]{:S(2)}) collective-permute-start(bf16[512,1024]{1,0:T(8,128)(2,1)} %refs_12_.1), channel_id=1, source_target_pairs={{0,8},{8,0},{1,9},{9,1},{2,10},{10,2},{3,11},{11,3},{4,12},{12,4},... | collective-permute-start | bytes 3145736 | tf_op jit(solution)/shard_map/ppermute | solution.py:289
  2.2 2.2 %pack_first.1 = bf16[8,2,4,2,8,512]{5,4,3,2,1,0:T(8,128)(2,1)} custom-call(f32[8,3072]{1,0:T(8,128)} %qkv_hbm.1, f32[8,1024]{1,0:T(8,128)} %out_hbm.1), custom_call_target="tpu_custom_call" | custom-call | bytes 1048576 | tf_op jit(solution)/shard_map/pack_first/pallas_call | solution.py:324
  4.4 10.2 %all-to-all-start = ((bf16[128,8,512]{2,1,0:T(8,128)(2,1)}), bf16[128,8,512]{2,1,0:T(8,128)(2,1)S(1)}, u32[]{:S(2)}, u32[]{:S(2)}) async-start(bf16[128,8,512]{2,1,0:T(8,128)(2,1)} %bitcast.3), calls=%async_computation | async-start | bytes 2097152 | tf_op jit(solution)/shard_map/all_to_all | solution.py:285
  15.2 1.6 %collective-permute-start = (bf16[8,2048]{1,0:T(8,128)(2,1)S(1)}, bf16[8,2048]{1,0:T(8,128)(2,1)S(1)}, u32[]{:S(2)}, u32[]{:S(2)}) collective-permute-start(bf16[8,2048]{1,0:T(8,128)(2,1)S(1)} %get-tuple-element.43), channel_id=1, source_target_pairs={{0,2},{2,0},{4,6},{6,4},{1,3},{3,1},{5,7},{7,5},{8,10},{10,8},{12,... | collective-permute-start | bytes 98312 | tf_op jit(solution)/shard_map/ppermute | solution.py:293
  16.8 2.9 %collective-permute-start.1 = (bf16[8,2048]{1,0:T(8,128)(2,1)S(1)}, bf16[8,2048]{1,0:T(8,128)(2,1)S(1)}, u32[]{:S(2)}, u32[]{:S(2)}) collective-permute-start(bf16[8,2048]{1,0:T(8,128)(2,1)S(1)} %get-tuple-element.44), channel_id=1, source_target_pairs={{0,4},{2,6},{4,0},{6,2},{1,5},{3,7},{5,1},{7,3},{8,12},{10,14},{12... | collective-permute-start | bytes 98312 | tf_op jit(solution)/shard_map/ppermute | solution.py:293
  19.8 1.3 %collective-permute-start.4 = (s32[512]{0:T(512)S(1)}, s32[512]{0:T(512)S(1)}, u32[]{:S(2)}, u32[]{:S(2)}) collective-permute-start(s32[512]{0:T(512)S(1)} %copy-done.7), channel_id=1, source_target_pairs={{0,8},{8,0},{1,9},{9,1},{2,10},{10,2},{3,11},{11,3},{4,12},{12,4},... | collective-permute-start | bytes 6152 | tf_op jit(solution)/shard_map/ppermute | solution.py:289
  21.1 0.8 collective-permute-done.4
  21.9 1.6 %collective-permute-done.refs_1_ = bf16[8,2048]{1,0:T(8,128)(2,1)S(1)} collective-permute-done((bf16[8,2048]{1,0:T(8,128)(2,1)S(1)}, bf16[8,2048]{1,0:T(8,128)(2,1)S(1)}, u32[]{:S(2)}, u32[]{:S(2)}) %collective-permute-start) | collective-permute-done | bytes 32800 | tf_op jit(solution)/shard_map/ppermute | solution.py:293
  23.5 6.8 %collective-permute-done.1.refs_2_ = bf16[8,2048]{1,0:T(8,128)(2,1)S(1)} collective-permute-done((bf16[8,2048]{1,0:T(8,128)(2,1)S(1)}, bf16[8,2048]{1,0:T(8,128)(2,1)S(1)}, u32[]{:S(2)}, u32[]{:S(2)}) %collective-permute-start.1) | collective-permute-done | bytes 32800 | tf_op jit(solution)/shard_map/ppermute | solution.py:293
  30.3 2.1 %pack_rest.1 = bf16[8,2,2,4,8,1024]{5,4,3,2,1,0:T(8,128)(2,1)} custom-call(s32[3]{0:T(128)S(1)} %pad_add_fusion.place_ref, bf16[8,2048]{1,0:T(8,128)(2,1)S(1)} %get-tuple-element.46.refs_0_, bf16[8,2048]{1,0:T(8,128)(2,1)S(1)} %collective-permute-done.refs_1_, bf16[8,2048]{1,0:T(8,128)(2,1)S(1)} %collective-permute-done.1.refs_2_, ...), custom_call_target="tpu_custom_call" | custom-call | bytes 1048576 | tf_op jit(solution)/shard_map/pack_rest/pallas_call | solution.py:343
  32.9 7.9 %all-to-all-start.1 = ((bf16[32,4,8,1024]{3,2,1,0:T(8,128)(2,1)}), bf16[32,4,8,1024]{3,2,1,0:T(8,128)(2,1)S(1)}, u32[]{:S(2)}, u32[]{:S(2)}) async-start(bf16[32,4,8,1024]{3,2,1,0:T(8,128)(2,1)} %bitcast.5), calls=%async_computation.1 | async-start | bytes 4194304 | tf_op jit(solution)/shard_map/all_to_all | solution.py:285
  41.5 6.6 %attend.1 = (bf16[256,128]{1,0:T(8,128)(2,1)S(1)}, bf16[512,128]{1,0:T(8,128)(2,1)S(1)}, bf16[768,128]{1,0:T(8,128)(2,1)S(1)}) custom-call(s32[3]{0:T(128)S(1)} %pad_add_fusion.place_ref, bf16[512,1024]{1,0:T(8,128)(2,1)} %refs_12_.1, bf16[512,1024]{1,0:T(8,128)(2,1)} %copy-done.9, bf16[1024,512]{1,0:T(8,128)(2,1)S(1)} %bitcast.14, s32[4,128]{1,0:T(4,128)S(1)} %bitcast.21, ...), custom_call_target="tpu_custom_call" | custom-call | flops 5000000000 | bytes 1048576 | tf_op jit(solution)/shard_map/attend/pallas_call | solution.py:359
  48.8 1.1 %collective-permute-done.5.got_ref = bf16[768,128]{1,0:T(8,128)(2,1)S(1)} collective-permute-done((bf16[768,128]{1,0:T(8,128)(2,1)S(1)}, bf16[768,128]{1,0:T(8,128)(2,1)S(1)}, u32[]{:S(2)}, u32[]{:S(2)}) %collective-permute-start.5) | collective-permute-done | bytes 196640 | tf_op jit(solution)/shard_map/ppermute | solution.py:289
  49.9 1.7 %collective-permute-start.8 = (bf16[1024,128]{1,0:T(8,128)(2,1)S(1)}, bf16[1024,128]{1,0:T(8,128)(2,1)S(1)}, u32[]{:S(2)}, u32[]{:S(2)}) collective-permute-start(bf16[1024,128]{1,0:T(8,128)(2,1)S(1)} %collective-permute-done.7.refs_7_), channel_id=1, source_target_pairs={{0,2},{2,0},{4,6},{6,4},{1,3},{3,1},{5,7},{7,5},{8,10},{10,8},{12,... | collective-permute-start | bytes 786440 | tf_op jit(solution)/shard_map/ppermute | solution.py:293
  52.3 2.2 %collective-permute-start.11 = (bf16[256,256]{1,0:T(8,128)(2,1)S(1)}, bf16[256,256]{1,0:T(8,128)(2,1)S(1)}, u32[]{:S(2)}, u32[]{:S(2)}) collective-permute-start(bf16[256,256]{1,0:T(8,128)(2,1)S(1)} %join.1.refs_0_), channel_id=1, source_target_pairs={{0,6},{2,4},{4,2},{6,0},{1,7},{3,5},{5,3},{7,1},{8,14},{10,12},{12... | collective-permute-start | bytes 393224 | tf_op jit(solution)/shard_map/ppermute | solution.py:293
  54.4 1.2 %collective-permute-start.9 = (bf16[256,256]{1,0:T(8,128)(2,1)S(1)}, bf16[256,256]{1,0:T(8,128)(2,1)S(1)}, u32[]{:S(2)}, u32[]{:S(2)}) collective-permute-start(bf16[256,256]{1,0:T(8,128)(2,1)S(1)} %join.1.refs_0_), channel_id=1, source_target_pairs={{0,2},{2,0},{4,6},{6,4},{1,3},{3,1},{5,7},{7,5},{8,10},{10,8},{12,... | collective-permute-start | bytes 393224 | tf_op jit(solution)/shard_map/ppermute | solution.py:293
  55.6 1.5 %collective-permute-start.12 = (bf16[1024,128]{1,0:T(8,128)(2,1)S(1)}, bf16[1024,128]{1,0:T(8,128)(2,1)S(1)}, u32[]{:S(2)}, u32[]{:S(2)}) collective-permute-start(bf16[1024,128]{1,0:T(8,128)(2,1)S(1)} %take.1.refs_4_), channel_id=1, source_target_pairs={{0,8},{8,0},{1,9},{9,1},{2,10},{10,2},{3,11},{11,3},{4,12},{12,4},... | collective-permute-start | bytes 786440 | tf_op jit(solution)/shard_map/ppermute | solution.py:289
  57.1 0.9 %collective-permute-done.11.refs_3_ = bf16[256,256]{1,0:T(8,128)(2,1)S(1)} collective-permute-done((bf16[256,256]{1,0:T(8,128)(2,1)S(1)}, bf16[256,256]{1,0:T(8,128)(2,1)S(1)}, u32[]{:S(2)}, u32[]{:S(2)}) %collective-permute-start.11) | collective-permute-done | bytes 131104 | tf_op jit(solution)/shard_map/ppermute | solution.py:293
  57.9 1.5 %collective-permute-start.13 = (bf16[1024,128]{1,0:T(8,128)(2,1)S(1)}, bf16[1024,128]{1,0:T(8,128)(2,1)S(1)}, u32[]{:S(2)}, u32[]{:S(2)}) collective-permute-start(bf16[1024,128]{1,0:T(8,128)(2,1)S(1)} %collective-permute-done.6.refs_5_), channel_id=1, source_target_pairs={{0,8},{8,0},{1,9},{9,1},{2,10},{10,2},{3,11},{11,3},{4,12},{12,4},... | collective-permute-start | bytes 786440 | tf_op jit(solution)/shard_map/ppermute | solution.py:289
  59.5 3.0 %collective-permute-done.10.refs_2_ = bf16[256,256]{1,0:T(8,128)(2,1)S(1)} collective-permute-done((bf16[256,256]{1,0:T(8,128)(2,1)S(1)}, bf16[256,256]{1,0:T(8,128)(2,1)S(1)}, u32[]{:S(2)}, u32[]{:S(2)}) %collective-permute-start.10) | collective-permute-done | bytes 131104 | tf_op jit(solution)/shard_map/ppermute | solution.py:293
  62.5 1.6 %collective-permute-start.15 = (bf16[1024,128]{1,0:T(8,128)(2,1)S(1)}, bf16[1024,128]{1,0:T(8,128)(2,1)S(1)}, u32[]{:S(2)}, u32[]{:S(2)}) collective-permute-start(bf16[1024,128]{1,0:T(8,128)(2,1)S(1)} %collective-permute-done.7.refs_7_), channel_id=1, source_target_pairs={{0,8},{8,0},{1,9},{9,1},{2,10},{10,2},{3,11},{11,3},{4,12},{12,4},... | collective-permute-start | bytes 786440 | tf_op jit(solution)/shard_map/ppermute | solution.py:289
  65.7 2.7 %project.1 = (bf16[256,1024]{1,0:T(8,128)(2,1)S(1)}, bf16[64,1024]{1,0:T(8,128)(2,1)S(1)}) custom-call(s32[3]{0:T(128)S(1)} %pad_add_fusion.place_ref, bf16[256,256]{1,0:T(8,128)(2,1)S(1)} %join.1.refs_0_, bf16[256,256]{1,0:T(8,128)(2,1)S(1)} %collective-permute-done.9.refs_1_, bf16[256,256]{1,0:T(8,128)(2,1)S(1)} %collective-permute-done.10.refs_2_, ...), custom_call_target="tpu_custom_call" | custom-call | flops 2000000000 | bytes 1048576 | tf_op jit(solution)/shard_map/project/pallas_call | solution.py:381
  68.4 0.8 copy-done.8
  69.2 1.0 %collective-permute-start.16 = (bf16[1024,1024]{1,0:T(8,128)(2,1)S(1)}, bf16[1024,1024]{1,0:T(8,128)(2,1)S(1)}, u32[]{:S(2)}, u32[]{:S(2)}) collective-permute-start(bf16[1024,1024]{1,0:T(8,128)(2,1)S(1)} %bitcast.15), channel_id=1, source_target_pairs={{0,8},{8,0},{1,9},{9,1},{2,10},{10,2},{3,11},{11,3},{4,12},{12,4},... | collective-permute-start | bytes 6291464 | tf_op jit(solution)/shard_map/ppermute | solution.py:289
  70.1 2.0 %own_feed.1 = (bf16[256,1024]{1,0:T(8,128)(2,1)S(1)}, f32[256,1024]{1,0:T(8,128)S(1)}) custom-call(bf16[256,1024]{1,0:T(8,128)(2,1)} %copy-done.8, bf16[1024,1024]{1,0:T(8,128)(2,1)S(1)} %bitcast.16), custom_call_target="tpu_custom_call" | custom-call | flops 2000000000 | bytes 1048576 | tf_op jit(solution)/shard_map/own_feed/pallas_call | solution.py:398
  72.1 1.8 %collective-permute-done.16.theirs_ref = bf16[1024,1024]{1,0:T(8,128)(2,1)S(1)} collective-permute-done((bf16[1024,1024]{1,0:T(8,128)(2,1)S(1)}, bf16[1024,1024]{1,0:T(8,128)(2,1)S(1)}, u32[]{:S(2)}, u32[]{:S(2)}) %collective-permute-start.16) | collective-permute-done | bytes 2097184 | tf_op jit(solution)/shard_map/ppermute | solution.py:289
  73.9 1.4 %feed.3 = (bf16[64,1024]{1,0:T(8,128)(2,1)S(1)}, bf16[64,1024]{1,0:T(8,128)(2,1)S(1)}) custom-call(s32[3]{0:T(128)S(1)} %pad_add_fusion.place_ref, bf16[256,1024]{1,0:T(8,128)(2,1)S(1)} %get-tuple-element.71.arrived_ref, f32[256,1024]{1,0:T(8,128)S(1)} %get-tuple-element.72.own_ref, bf16[1024,1024]{1,0:T(8,128)(2,1)S(1)} %collective-permute-done.16.theirs_ref), custom_call_target="tpu_custom_call" | custom-call | flops 1000000000 | bytes 1048576 | tf_op jit(solution)/shard_map/feed/pallas_call | solution.py:408
  75.3 2.8 %collective-permute-start.18 = (bf16[64,1024]{1,0:T(8,128)(2,1)S(1)}, bf16[64,1024]{1,0:T(8,128)(2,1)S(1)}, u32[]{:S(2)}, u32[]{:S(2)}) collective-permute-start(bf16[64,1024]{1,0:T(8,128)(2,1)S(1)} %get-tuple-element.75), channel_id=1, source_target_pairs={{0,4},{2,6},{4,0},{6,2},{1,5},{3,7},{5,1},{7,3},{8,12},{10,14},{12... | collective-permute-start | bytes 393224 | tf_op jit(solution)/shard_map/ppermute | solution.py:293
  78.7 1.4 %feed.2 = (bf16[64,1024]{1,0:T(8,128)(2,1)S(1)}, bf16[64,1024]{1,0:T(8,128)(2,1)S(1)}) custom-call(s32[3]{0:T(128)S(1)} %pad_add_fusion.place_ref, bf16[256,1024]{1,0:T(8,128)(2,1)S(1)} %get-tuple-element.71.arrived_ref, f32[256,1024]{1,0:T(8,128)S(1)} %get-tuple-element.72.own_ref, bf16[1024,1024]{1,0:T(8,128)(2,1)S(1)} %collective-permute-done.16.theirs_ref), custom_call_target="tpu_custom_call" | custom-call | flops 1000000000 | bytes 1048576 | tf_op jit(solution)/shard_map/feed/pallas_call | solution.py:408
  80.2 1.4 %cache.1 = (bf16[512,128]{1,0:T(8,128)(2,1)}, bf16[512,128]{1,0:T(8,128)(2,1)}) custom-call(s32[3]{0:T(128)S(1)} %pad_add_fusion.place_ref, bf16[512,128]{1,0:T(8,128)(2,1)S(1)} %get-tuple-element.78.own_ref, bf16[768,128]{1,0:T(8,128)(2,1)S(1)} %collective-permute-done.5.got_ref), custom_call_target="tpu_custom_call" | custom-call | flops 1000000000 | bytes 1048576 | tf_op jit(solution)/shard_map/cache/pallas_call | solution.py:378
  81.6 2.9 %collective-permute-done.19.refs_3_ = bf16[64,1024]{1,0:T(8,128)(2,1)S(1)} collective-permute-done((bf16[64,1024]{1,0:T(8,128)(2,1)S(1)}, bf16[64,1024]{1,0:T(8,128)(2,1)S(1)}, u32[]{:S(2)}, u32[]{:S(2)}) %collective-permute-start.19) | collective-permute-done | bytes 131104 | tf_op jit(solution)/shard_map/ppermute | solution.py:293
  84.6 0.9 %final.1 = bf16[64,1024]{1,0:T(8,128)(2,1)} custom-call(bf16[64,1024]{1,0:T(8,128)(2,1)S(1)} %get-tuple-element.73.refs_0_, bf16[64,1024]{1,0:T(8,128)(2,1)S(1)} %collective-permute-done.17.refs_1_, bf16[64,1024]{1,0:T(8,128)(2,1)S(1)} %collective-permute-done.18.refs_2_, bf16[64,1024]{1,0:T(8,128)(2,1)S(1)} %collective-permute-done.19.refs_3_, ...), custom_call_target="tpu_custom_call" | custom-call | bytes 1048576 | tf_op jit(solution)/shard_map/final/pallas_call | solution.py:419
  (45 shorter events, 5.5 us)
Async XLA Ops:
  0.6 14.0 %copy-start.1 = (f32[8,4096]{1,0:T(8,128)S(1)}, f32[8,4096]{1,0:T(8,128)}, u32[]{:S(2)}) copy-start(f32[8,4096]{1,0:T(8,128)} %down_ref.1) | copy-start | bytes 393220
  0.6 14.0 %copy-start = (f32[8,4096]{1,0:T(8,128)S(1)}, f32[8,4096]{1,0:T(8,128)}, u32[]{:S(2)}) copy-start(f32[8,4096]{1,0:T(8,128)} %up_ref.1) | copy-start | bytes 393220
  0.7 19.1 %copy-start.7 = (s32[512]{0:T(512)S(1)}, s32[512]{0:T(512)}, u32[]{:S(2)}) copy-start(s32[512]{0:T(512)} %param.11) | copy-start | bytes 6148
  0.7 29.6 %collective-permute-start.3 = (bf16[512,1024]{1,0:T(8,128)(2,1)}, bf16[512,1024]{1,0:T(8,128)(2,1)S(1)}, u32[]{:S(2)}, u32[]{:S(2)}) collective-permute-start(bf16[512,1024]{1,0:T(8,128)(2,1)} %refs_12_.1), channel_id=1, source_target_pairs={{0,8},{8,0},{1,9},{9,1},{2,10},{10,2},{3,11},{11,3},{4,12},{12,4},... | collective-permute-start | bytes 3145736 | tf_op jit(solution)/shard_map/ppermute | solution.py:289
  4.4 28.5 %all-to-all-start = ((bf16[128,8,512]{2,1,0:T(8,128)(2,1)}), bf16[128,8,512]{2,1,0:T(8,128)(2,1)S(1)}, u32[]{:S(2)}, u32[]{:S(2)}) async-start(bf16[128,8,512]{2,1,0:T(8,128)(2,1)} %bitcast.3), calls=%async_computation | async-start | bytes 2097152 | tf_op jit(solution)/shard_map/all_to_all | solution.py:285
  15.2 8.3 %collective-permute-start = (bf16[8,2048]{1,0:T(8,128)(2,1)S(1)}, bf16[8,2048]{1,0:T(8,128)(2,1)S(1)}, u32[]{:S(2)}, u32[]{:S(2)}) collective-permute-start(bf16[8,2048]{1,0:T(8,128)(2,1)S(1)} %get-tuple-element.43), channel_id=1, source_target_pairs={{0,2},{2,0},{4,6},{6,4},{1,3},{3,1},{5,7},{7,5},{8,10},{10,8},{12,... | collective-permute-start | bytes 98312 | tf_op jit(solution)/shard_map/ppermute | solution.py:293
  16.8 13.5 %collective-permute-start.1 = (bf16[8,2048]{1,0:T(8,128)(2,1)S(1)}, bf16[8,2048]{1,0:T(8,128)(2,1)S(1)}, u32[]{:S(2)}, u32[]{:S(2)}) collective-permute-start(bf16[8,2048]{1,0:T(8,128)(2,1)S(1)} %get-tuple-element.44), channel_id=1, source_target_pairs={{0,4},{2,6},{4,0},{6,2},{1,5},{3,7},{5,1},{7,3},{8,12},{10,14},{12... | collective-permute-start | bytes 98312 | tf_op jit(solution)/shard_map/ppermute | solution.py:293
  19.8 10.5 %collective-permute-start.2 = (bf16[8,2048]{1,0:T(8,128)(2,1)S(1)}, bf16[8,2048]{1,0:T(8,128)(2,1)S(1)}, u32[]{:S(2)}, u32[]{:S(2)}) collective-permute-start(bf16[8,2048]{1,0:T(8,128)(2,1)S(1)} %get-tuple-element.45), channel_id=1, source_target_pairs={{0,6},{2,4},{4,2},{6,0},{1,7},{3,5},{5,3},{7,1},{8,14},{10,12},{12... | collective-permute-start | bytes 98312 | tf_op jit(solution)/shard_map/ppermute | solution.py:293
  19.8 2.1 %collective-permute-start.4 = (s32[512]{0:T(512)S(1)}, s32[512]{0:T(512)S(1)}, u32[]{:S(2)}, u32[]{:S(2)}) collective-permute-start(s32[512]{0:T(512)S(1)} %copy-done.7), channel_id=1, source_target_pairs={{0,8},{8,0},{1,9},{9,1},{2,10},{10,2},{3,11},{11,3},{4,12},{12,4},... | collective-permute-start | bytes 6152 | tf_op jit(solution)/shard_map/ppermute | solution.py:289
  30.3 2.6 %copy-start.9 = (bf16[512,1024]{1,0:T(8,128)(2,1)}, bf16[512,1024]{1,0:T(8,128)(2,1)S(1)}, u32[]{:S(2)}) copy-start(bf16[512,1024]{1,0:T(8,128)(2,1)S(1)} %collective-permute-done.3.other_hbm) | copy-start | bytes 3145732
  32.9 36.3 %all-to-all-start.1 = ((bf16[32,4,8,1024]{3,2,1,0:T(8,128)(2,1)}), bf16[32,4,8,1024]{3,2,1,0:T(8,128)(2,1)S(1)}, u32[]{:S(2)}, u32[]{:S(2)}) async-start(bf16[32,4,8,1024]{3,2,1,0:T(8,128)(2,1)} %bitcast.5), calls=%async_computation.1 | async-start | bytes 4194304 | tf_op jit(solution)/shard_map/all_to_all | solution.py:285
  40.8 9.0 %collective-permute-start.7 = (bf16[1024,128]{1,0:T(8,128)(2,1)S(1)}, bf16[1024,128]{1,0:T(8,128)(2,1)S(1)}, u32[]{:S(2)}, u32[]{:S(2)}) collective-permute-start(bf16[1024,128]{1,0:T(8,128)(2,1)S(1)} %take.1.refs_4_), channel_id=1, source_target_pairs={{0,6},{2,4},{4,2},{6,0},{1,7},{3,5},{5,3},{7,1},{8,14},{10,12},{12... | collective-permute-start | bytes 786440 | tf_op jit(solution)/shard_map/ppermute | solution.py:293
  41.5 8.3 %collective-permute-start.6 = (bf16[1024,128]{1,0:T(8,128)(2,1)S(1)}, bf16[1024,128]{1,0:T(8,128)(2,1)S(1)}, u32[]{:S(2)}, u32[]{:S(2)}) collective-permute-start(bf16[1024,128]{1,0:T(8,128)(2,1)S(1)} %take.1.refs_4_), channel_id=1, source_target_pairs={{0,2},{2,0},{4,6},{6,4},{1,3},{3,1},{5,7},{7,5},{8,10},{10,8},{12,... | collective-permute-start | bytes 786440 | tf_op jit(solution)/shard_map/ppermute | solution.py:293
  41.5 24.1 %copy-start.4 = (bf16[512,1024]{1,0:T(8,128)(2,1)S(1)}, bf16[512,1024]{1,0:T(8,128)(2,1)}, u32[]{:S(2)}) copy-start(bf16[512,1024]{1,0:T(8,128)(2,1)} %refs_12_.1) | copy-start | bytes 3145732
  41.5 24.1 %copy-start.5 = (f32[1024]{0:T(1024)S(1)}, f32[1024]{0:T(1024)}, u32[]{:S(2)}) copy-start(f32[1024]{0:T(1024)} %param.16) | copy-start | bytes 12292
  41.5 24.1 %copy-start.6 = (f32[1024]{0:T(1024)S(1)}, f32[1024]{0:T(1024)}, u32[]{:S(2)}) copy-start(f32[1024]{0:T(1024)} %param.17) | copy-start | bytes 12292
  48.2 1.7 %collective-permute-start.5 = (bf16[768,128]{1,0:T(8,128)(2,1)S(1)}, bf16[768,128]{1,0:T(8,128)(2,1)S(1)}, u32[]{:S(2)}, u32[]{:S(2)}) collective-permute-start(bf16[768,128]{1,0:T(8,128)(2,1)S(1)} %get-tuple-element.54), channel_id=1, source_target_pairs={{0,8},{8,0},{1,9},{9,1},{2,10},{10,2},{3,11},{11,3},{4,12},{12,4},... | collective-permute-start | bytes 589832 | tf_op jit(solution)/shard_map/ppermute | solution.py:289
  49.9 14.2 %collective-permute-start.8 = (bf16[1024,128]{1,0:T(8,128)(2,1)S(1)}, bf16[1024,128]{1,0:T(8,128)(2,1)S(1)}, u32[]{:S(2)}, u32[]{:S(2)}) collective-permute-start(bf16[1024,128]{1,0:T(8,128)(2,1)S(1)} %collective-permute-done.7.refs_7_), channel_id=1, source_target_pairs={{0,2},{2,0},{4,6},{6,4},{1,3},{3,1},{5,7},{7,5},{8,10},{10,8},{12,... | collective-permute-start | bytes 786440 | tf_op jit(solution)/shard_map/ppermute | solution.py:293
  52.3 5.7 %collective-permute-start.11 = (bf16[256,256]{1,0:T(8,128)(2,1)S(1)}, bf16[256,256]{1,0:T(8,128)(2,1)S(1)}, u32[]{:S(2)}, u32[]{:S(2)}) collective-permute-start(bf16[256,256]{1,0:T(8,128)(2,1)S(1)} %join.1.refs_0_), channel_id=1, source_target_pairs={{0,6},{2,4},{4,2},{6,0},{1,7},{3,5},{5,3},{7,1},{8,14},{10,12},{12... | collective-permute-start | bytes 393224 | tf_op jit(solution)/shard_map/ppermute | solution.py:293
  54.4 8.1 %collective-permute-start.10 = (bf16[256,256]{1,0:T(8,128)(2,1)S(1)}, bf16[256,256]{1,0:T(8,128)(2,1)S(1)}, u32[]{:S(2)}, u32[]{:S(2)}) collective-permute-start(bf16[256,256]{1,0:T(8,128)(2,1)S(1)} %join.1.refs_0_), channel_id=1, source_target_pairs={{0,4},{2,6},{4,0},{6,2},{1,5},{3,7},{5,1},{7,3},{8,12},{10,14},{12... | collective-permute-start | bytes 393224 | tf_op jit(solution)/shard_map/ppermute | solution.py:293
  54.4 9.6 %collective-permute-start.9 = (bf16[256,256]{1,0:T(8,128)(2,1)S(1)}, bf16[256,256]{1,0:T(8,128)(2,1)S(1)}, u32[]{:S(2)}, u32[]{:S(2)}) collective-permute-start(bf16[256,256]{1,0:T(8,128)(2,1)S(1)} %join.1.refs_0_), channel_id=1, source_target_pairs={{0,2},{2,0},{4,6},{6,4},{1,3},{3,1},{5,7},{7,5},{8,10},{10,8},{12,... | collective-permute-start | bytes 393224 | tf_op jit(solution)/shard_map/ppermute | solution.py:293
  55.6 8.9 %collective-permute-start.12 = (bf16[1024,128]{1,0:T(8,128)(2,1)S(1)}, bf16[1024,128]{1,0:T(8,128)(2,1)S(1)}, u32[]{:S(2)}, u32[]{:S(2)}) collective-permute-start(bf16[1024,128]{1,0:T(8,128)(2,1)S(1)} %take.1.refs_4_), channel_id=1, source_target_pairs={{0,8},{8,0},{1,9},{9,1},{2,10},{10,2},{3,11},{11,3},{4,12},{12,4},... | collective-permute-start | bytes 786440 | tf_op jit(solution)/shard_map/ppermute | solution.py:289
  57.9 6.5 %collective-permute-start.13 = (bf16[1024,128]{1,0:T(8,128)(2,1)S(1)}, bf16[1024,128]{1,0:T(8,128)(2,1)S(1)}, u32[]{:S(2)}, u32[]{:S(2)}) collective-permute-start(bf16[1024,128]{1,0:T(8,128)(2,1)S(1)} %collective-permute-done.6.refs_5_), channel_id=1, source_target_pairs={{0,8},{8,0},{1,9},{9,1},{2,10},{10,2},{3,11},{11,3},{4,12},{12,4},... | collective-permute-start | bytes 786440 | tf_op jit(solution)/shard_map/ppermute | solution.py:289
  62.5 2.7 %collective-permute-start.15 = (bf16[1024,128]{1,0:T(8,128)(2,1)S(1)}, bf16[1024,128]{1,0:T(8,128)(2,1)S(1)}, u32[]{:S(2)}, u32[]{:S(2)}) collective-permute-start(bf16[1024,128]{1,0:T(8,128)(2,1)S(1)} %collective-permute-done.7.refs_7_), channel_id=1, source_target_pairs={{0,8},{8,0},{1,9},{9,1},{2,10},{10,2},{3,11},{11,3},{4,12},{12,4},... | collective-permute-start | bytes 786440 | tf_op jit(solution)/shard_map/ppermute | solution.py:289
  64.0 1.6 %collective-permute-start.14 = (bf16[1024,128]{1,0:T(8,128)(2,1)S(1)}, bf16[1024,128]{1,0:T(8,128)(2,1)S(1)}, u32[]{:S(2)}, u32[]{:S(2)}) collective-permute-start(bf16[1024,128]{1,0:T(8,128)(2,1)S(1)} %collective-permute-done.8.refs_6_), channel_id=1, source_target_pairs={{0,8},{8,0},{1,9},{9,1},{2,10},{10,2},{3,11},{11,3},{4,12},{12,4},... | collective-permute-start | bytes 786440 | tf_op jit(solution)/shard_map/ppermute | solution.py:289
  68.4 0.8 copy-start.8
  69.2 4.8 %collective-permute-start.16 = (bf16[1024,1024]{1,0:T(8,128)(2,1)S(1)}, bf16[1024,1024]{1,0:T(8,128)(2,1)S(1)}, u32[]{:S(2)}, u32[]{:S(2)}) collective-permute-start(bf16[1024,1024]{1,0:T(8,128)(2,1)S(1)} %bitcast.15), channel_id=1, source_target_pairs={{0,8},{8,0},{1,9},{9,1},{2,10},{10,2},{3,11},{11,3},{4,12},{12,4},... | collective-permute-start | bytes 6291464 | tf_op jit(solution)/shard_map/ppermute | solution.py:289
  75.3 6.3 %collective-permute-start.18 = (bf16[64,1024]{1,0:T(8,128)(2,1)S(1)}, bf16[64,1024]{1,0:T(8,128)(2,1)S(1)}, u32[]{:S(2)}, u32[]{:S(2)}) collective-permute-start(bf16[64,1024]{1,0:T(8,128)(2,1)S(1)} %get-tuple-element.75), channel_id=1, source_target_pairs={{0,4},{2,6},{4,0},{6,2},{1,5},{3,7},{5,1},{7,3},{8,12},{10,14},{12... | collective-permute-start | bytes 393224 | tf_op jit(solution)/shard_map/ppermute | solution.py:293
  78.1 6.5 %collective-permute-start.19 = (bf16[64,1024]{1,0:T(8,128)(2,1)S(1)}, bf16[64,1024]{1,0:T(8,128)(2,1)S(1)}, u32[]{:S(2)}, u32[]{:S(2)}) collective-permute-start(bf16[64,1024]{1,0:T(8,128)(2,1)S(1)} %get-tuple-element.76), channel_id=1, source_target_pairs={{0,6},{2,4},{4,2},{6,0},{1,7},{3,5},{5,3},{7,1},{8,14},{10,12},{12... | collective-permute-start | bytes 393224 | tf_op jit(solution)/shard_map/ppermute | solution.py:293
  80.1 4.4 %copy-start.2 = (f32[1024]{0:T(1024)S(1)}, f32[1024]{0:T(1024)}, u32[]{:S(2)}) copy-start(f32[1024]{0:T(1024)} %param.18) | copy-start | bytes 12292
  80.1 4.4 %copy-start.3 = (f32[1024]{0:T(1024)S(1)}, f32[1024]{0:T(1024)}, u32[]{:S(2)}) copy-start(f32[1024]{0:T(1024)} %param.19) | copy-start | bytes 12292
  80.1 4.4 %collective-permute-start.17 = (bf16[64,1024]{1,0:T(8,128)(2,1)S(1)}, bf16[64,1024]{1,0:T(8,128)(2,1)S(1)}, u32[]{:S(2)}, u32[]{:S(2)}) collective-permute-start(bf16[64,1024]{1,0:T(8,128)(2,1)S(1)} %get-tuple-element.74), channel_id=1, source_target_pairs={{0,2},{2,0},{4,6},{6,4},{1,3},{3,1},{5,7},{7,5},{8,10},{10,8},{12,... | collective-permute-start | bytes 393224 | tf_op jit(solution)/shard_map/ppermute | solution.py:293
